TPU v7x, 32 devices: a whole 2x2x4 slice. The times are simulated.
32 devices in a mesh: row: 8 (over y, x, core), col: 4 (over z).
Axes of the slice: x: 2, y: 2, z: 4, core: 2. Of those that a mesh axis runs over, the one named last changes fastest.
Arguments:
- trailing: float32 [512, 512], P('row', 'col'), may hold values from -6 to 6
- panel_block: bfloat16 [512, 1024], P('row'), may hold values from -24 to 24
- diag_inverse: bfloat16 [1024, 1024], P('col'), as said below
- panel_points: float32 [20, 1024], replicated, may hold values from 0 to 1
- lengthscales: float32 [20], replicated, may hold values from 0.15 to 5
- targets: bfloat16 [1024], replicated, may hold values from -96 to 96
- base_a: float32 [20, 24576], P(None, 'row'), may hold values from 0 to 1
- base_b: float32 [20, 24576], P(None, 'row'), may hold values from 0 to 1
- pick_sets: int32 [96, 20], P('row'), may hold values 0 or 1
- cross_rhs: bfloat16 [512, 24576], P('col', 'row'), may hold values from -0.59765625 to 0.59765625
- mean_in: float32 [24576], P('row'), may hold values from -3 to 3
- var_in: float32 [24576], P('row'), may hold values from 1 to 2
Outputs:
- trailing_next: float32 [512, 512], P('row', 'col')
- cross_next: bfloat16 [512, 24576], P('col', 'row')
- post_mean: float32 [24576], P('row')
- post_variance: float32 [24576], P('row')
Inputs may be any that keep to these rules, and one draw needn't show every extreme that they name: diag_inverse is lower triangular.
All inputs are finite; a program needn't handle non-finite values. No bound on the sum of `pick_sets` on one device may be relied on, other than what follows from the above.
Results may differ from a plain program's by a relative error of at most 0.0034.
Values may be sent and summed in bfloat16 or wider, within the bound.
No kernel may reach another device: no remote copies, remote signals or barrier semaphores. Data moves between devices by JAX's collectives and lax.ppermute only.
A program may use at most 64 MiB of HBM per device.

v0:
```python
import jax
import jax.numpy as jnp
from jax import lax
from jax.sharding import PartitionSpec as P

QB = 256


def kernel_block(scaled_points, candidates):
    inner = lax.dot_general(
        scaled_points,
        candidates,
        (((0,), (0,)), ((), ())),
        precision=lax.Precision.HIGHEST,
        preferred_element_type=jnp.float32,
    )
    distance = (
        jnp.sum(scaled_points * scaled_points, axis=0)[:, None]
        + jnp.sum(candidates * candidates, axis=0)[None, :]
        - 2.0 * inner
    )
    return jnp.exp(-0.5 * distance).astype(jnp.bfloat16)


def local(
    trailing,
    panel_block,
    diag_inverse,
    panel_points,
    lengthscales,
    targets,
    base_a,
    base_b,
    pick_sets,
    cross_rhs,
    mean_in,
    var_in,
):
    slab_cols = lax.dot_general(
        panel_block, diag_inverse, (((1,), (1,)), ((), ())), preferred_element_type=jnp.float32
    ).astype(jnp.bfloat16)
    own_rows = lax.all_gather(slab_cols, "col", axis=1, tiled=True)
    slice_height = own_rows.shape[0] // lax.axis_size("col")
    own_slice = lax.dynamic_slice_in_dim(
        own_rows, lax.axis_index("col") * slice_height, slice_height, 0
    )
    cyc_rows = lax.all_gather(own_slice, "row", axis=0, tiled=True)
    trailing_next = trailing - lax.dot_general(
        own_rows, cyc_rows, (((1,), (1,)), ((), ())), preferred_element_type=jnp.float32
    )
    chosen = jnp.repeat(pick_sets, QB, axis=0).T
    scaled_points = panel_points / lengthscales[:, None]
    candidates = jnp.where(chosen == 1, base_b, base_a) / lengthscales[:, None]
    kernel_cols = kernel_block(scaled_points, candidates)
    solve_slab = jnp.dot(diag_inverse, kernel_cols, preferred_element_type=jnp.float32).astype(
        jnp.bfloat16
    )
    weight_slab = jnp.dot(diag_inverse, targets, preferred_element_type=jnp.float32).astype(
        jnp.bfloat16
    )
    solve_piece = lax.all_gather(solve_slab, "col", axis=0, tiled=True)
    weight_piece = lax.all_gather(weight_slab, "col", axis=0, tiled=True)
    update_sum = jnp.dot(cyc_rows, solve_piece, preferred_element_type=jnp.float32)
    mean_sum = jnp.dot(weight_piece, solve_piece, preferred_element_type=jnp.float32)
    widened = solve_piece.astype(jnp.float32)
    square_sum = jnp.sum(widened * widened, axis=0)
    update_sum, mean_sum, square_sum = (update_sum, mean_sum, square_sum)
    cross_next = (cross_rhs.astype(jnp.float32) - update_sum).astype(jnp.bfloat16)
    post_mean = mean_in + mean_sum
    post_variance = var_in - square_sum
    return (trailing_next, cross_next, post_mean, post_variance)


def solution(mesh):
    placed = (
        P("row", "col"),
        P("row", None),
        P("col", None),
        P(),
        P(),
        P(),
        P(None, "row"),
        P(None, "row"),
        P("row", None),
        P("col", "row"),
        P("row"),
        P("row"),
    )
    return jax.shard_map(
        local,
        mesh=mesh,
        in_specs=placed,
        out_specs=(P("row", "col"), P("col", "row"), P("row"), P("row")),
        check_vma=False,
    )
```

profile of v0, /device:TPU:0, one launch (start us, length us, event | category | flops | bytes accessed | tf_op | source)
XLA Modules:
  0.0 166.4 jit_solution(10842736419029884639)
XLA Ops:
  7.2 0.0 copy-start
  7.2 0.0 all-gather.3.cloned.1.call-start
  7.2 0.8 broadcast_compare_fusion
  8.0 0.1 copy.18
  8.1 0.1 broadcast_bitcast_fusion
  8.3 1.0 multiply_reduce_fusion.2
  9.3 1.2 multiply_reduce_fusion.1
  10.5 14.2 %exponential_convert_fusion = bf16[1024,3072]{1,0:T(8,128)(2,1)S(1)} fusion(f32[3072]{0:T(1024)S(1)} %multiply_reduce_fusion.1, f32[1024]{0:T(1024)S(1)} %multiply_reduce_fusion.2, f32[20,1024]{1,0:T(8,128)} %param.15, f32[20]{0:T(128)} %param.16, f32[20,3072]{1,0:T(8,128)} %param.19, f32[20,3072]{1,0:T(8,128)} %param.18, pred[3072,20]{0,1:T(8,128)(4,1)S(1)} %bitcast.30), kind=kOutput, calls=%fused_computation.1 | convolution fusion | flops 770846720 | bytes 6942800 | tf_op jit(solution)/shard_map/dot_general | solution.py:10
  24.7 0.0 copy-start.7
  24.7 0.0 copy-start.3
  24.7 3.2 %fusion = bf16[256,3072]{0,1:T(8,128)(2,1)} fusion(bf16[1024,3072]{1,0:T(8,128)(2,1)S(1)} %exponential_convert_fusion, bf16[256,1024]{1,0:T(8,128)(2,1)S(1)} %copy-done), kind=kOutput, calls=%fused_computation.4 | convolution fusion | flops 1611399168 | bytes 8388608 | tf_op jit(solution)/shard_map/dot_general | solution.py:55
  27.9 0.0 all-gather.3.cloned.1.call-update
  28.0 0.2 fusion.2
  28.2 12.6 %all-gather = bf16[4,1,256]{2,1,0:T(2,128)(2,1)S(1)} all-gather(bf16[1,1,256]{2,1,0:T(2,128)(2,1)S(1)} %reshape.14), channel_id=1, replica_groups=mesh['row'=8,'col'=4] {'col'}, dimensions={0}, use_global_device_ids=true | all-gather | bytes 2560 | tf_op jit(solution)/shard_map/all_gather | solution.py:62
  40.8 0.3 convolution_convert_fusion.1
  41.1 38.7 %all_gather.12 = bf16[64,1024]{1,0:T(8,128)(2,1)S(1)} all-gather(bf16[64,256]{1,0:T(8,128)(2,1)S(1)} %convolution_convert_fusion.1), channel_id=1, replica_groups=mesh['row'=8,'col'=4] {'col'}, dimensions={1}, use_global_device_ids=true | all-gather | bytes 163840 | tf_op jit(solution)/shard_map/all_gather | solution.py:42
  79.8 9.5 %all_gather.13 = bf16[128,1024]{1,0:T(8,128)(2,1)S(1)} all-gather(bf16[16,1024]{1,0:T(8,128)(2,1)S(1)} %constant_dynamic-slice_fusion), channel_id=1, replica_groups=mesh['row'=8,'col'=4] {'row'}, dimensions={0}, use_global_device_ids=true | all-gather | bytes 294912 | tf_op jit(solution)/shard_map/all_gather | solution.py:47
  89.3 0.8 convolution_subtract_fusion.1
  90.1 59.2 %all-gather.3.cloned.1.call-done = bf16[1024,3072]{0,1:T(8,128)(2,1)} async-done(((bf16[256,3072]{0,1:T(8,128)(2,1)}), bf16[1024,3072]{0,1:T(8,128)(2,1)}) %all-gather.3.cloned.1.call-update) | async-done | bytes 6291472 | tf_op jit(solution)/shard_map/all_gather | solution.py:61
  149.3 4.7 %fusion.3 = f32[1,3072]{1,0:T(1,128)S(1)} fusion(bf16[1024,1]{0,1:T(2,128)(2,1)S(1)} %bitcast.32, bf16[1024,3072]{0,1:T(8,128)(2,1)} %all-gather.3.cloned.1.call-done), kind=kOutput, calls=%fused_computation.16 | convolution fusion | flops 6291456 | bytes 6305792 | tf_op jit(solution)/shard_map/dot_general | solution.py:64
  153.9 0.6 add.23
  154.6 1.3 multiply_reduce_fusion
  155.9 0.6 sub.15
  156.5 3.1 %fusion.1 = bf16[128,3072]{1,0:T(8,128)(2,1)} fusion(bf16[128,1024]{1,0:T(8,128)(2,1)S(1)} %all_gather.13, bf16[1024,3072]{0,1:T(8,128)(2,1)S(1)} %copy-done.1, bf16[128,3072]{1,0:T(8,128)(2,1)S(1)} %copy-done.2), kind=kOutput, calls=%fused_computation.5 | convolution fusion | flops 806486016 | bytes 8126464 | tf_op jit(solution)/shard_map/dot_general | solution.py:63
  (19 shorter events, 0.1 us)
Async XLA Ops:
  7.2 17.5 %copy-start = (bf16[256,1024]{1,0:T(8,128)(2,1)S(1)}, bf16[256,1024]{1,0:T(8,128)(2,1)}, u32[]{:S(2)}) copy-start(bf16[256,1024]{1,0:T(8,128)(2,1)} %param.14) | copy-start | bytes 1572868
  7.2 142.1 %all-gather.3.cloned.1.call-start = ((), (), s32[]{:S(2)}) async-start(), calls=%async_computation | async-start | bytes 7864320 | tf_op jit(solution)/shard_map/all_gather | solution.py:61
  24.7 3.2 %copy-start.7 = (bf16[1024]{0:T(1024)(128)(2,1)S(1)}, bf16[1024]{0:T(1024)(128)(2,1)}, u32[]{:S(2)}) copy-start(bf16[1024]{0:T(1024)(128)(2,1)} %param.17) | copy-start | bytes 6148
  24.7 16.1 %copy-start.3 = (bf16[64,1024]{1,0:T(8,128)(2,1)S(1)}, bf16[64,1024]{1,0:T(8,128)(2,1)}, u32[]{:S(2)}) copy-start(bf16[64,1024]{1,0:T(8,128)(2,1)} %param.13) | copy-start | bytes 393220
  24.7 64.5 %copy-start.4 = (f32[64,128]{1,0:T(8,128)S(1)}, f32[64,128]{1,0:T(8,128)}, u32[]{:S(2)}) copy-start(f32[64,128]{1,0:T(8,128)} %param.12) | copy-start | bytes 98308
  27.9 126.0 %copy-start.5 = (f32[3072]{0:T(1024)S(1)}, f32[3072]{0:T(1024)}, u32[]{:S(2)}) copy-start(f32[3072]{0:T(1024)} %param.22) | copy-start | bytes 36868
  149.3 5.3 %copy-start.1 = (bf16[1024,3072]{0,1:T(8,128)(2,1)S(1)}, bf16[1024,3072]{0,1:T(8,128)(2,1)}, u32[]{:S(2)}) copy-start(bf16[1024,3072]{0,1:T(8,128)(2,1)} %all-gather.3.cloned.1.call-done) | copy-start | bytes 18874372
  149.3 6.6 %copy-start.6 = (f32[3072]{0:T(1024)S(1)}, f32[3072]{0:T(1024)}, u32[]{:S(2)}) copy-start(f32[3072]{0:T(1024)} %param.23) | copy-start | bytes 36868
  149.3 7.2 %copy-start.2 = (bf16[128,3072]{1,0:T(8,128)(2,1)S(1)}, bf16[128,3072]{1,0:T(8,128)(2,1)}, u32[]{:S(2)}) copy-start(bf16[128,3072]{1,0:T(8,128)(2,1)} %param.21) | copy-start | bytes 2359300
Sparse Core Ops, SparseCore 0:
  28.0 121.1 all-gather.2
where the time goes:
time: 167 us; the launch traced here: 166 us
  blocking collectives  60.8 us (36%)
  waiting for transfers between devices  59.2 us (35%)
  matrix products  26.4 us (16%)
  between operations  14.2 us (9%)
  other arithmetic  5.48 us (3%)
    all_gather x1, waiting for transfers between devices, local(): solve_piece = lax.all_gather(solve_slab, 'col', axis=0, tiled=True)  59.2 us
    all_gather x1, blocking collectives, local(): own_rows = lax.all_gather(slab_cols, 'col', axis=1, tiled=True)  38.7 us
    dot_general x1, matrix products, kernel_block(): lax.dot_general(scaled_points, candidates, (((0,), (0,)), ((), ())), prec...  14.2 us
    all_gather x1, blocking collectives, local(): weight_piece = lax.all_gather(weight_slab, 'col', axis=0, tiled=True)  12.6 us
    all_gather x1, blocking collectives, local(): cyc_rows = lax.all_gather(own_slice, 'row', axis=0, tiled=True)  9.47 us
    dot_general x1, matrix products, local(): jnp.dot(weight_piece, solve_piece, preferred_element_type=jnp.float32)  4.65 us
  transfers between devices with their start and end apart: 1, of which 1 were waited for; matrix products, arithmetic and copies ran while one was open for 1% of the time, Pallas kernels for 0%

commit v1 on v0

v1 whole, which is shorter than its diff:
```python
import functools
import math

import jax
import jax.numpy as jnp
from jax import lax
from jax.experimental import pallas as pl
from jax.experimental.pallas import tpu as pltpu
from jax.sharding import PartitionSpec as P

LOG2E = math.log2(math.e)
GROUP = 32
DEPTH = 8 * GROUP
LINK = jnp.float32
VMEM = pl.BlockSpec(memory_space=pltpu.VMEM)


def tile_of(n, most):
    while n % most:
        most //= 2
    return most


def column(row):
    n = row.shape[1]
    eye = lax.broadcasted_iota(jnp.int32, (n, n), 0) == lax.broadcasted_iota(jnp.int32, (n, n), 1)
    return jnp.sum(jnp.where(eye, row, jnp.zeros_like(row)), axis=1, keepdims=True)


def split3(x):
    first = x.astype(jnp.bfloat16).astype(jnp.float32)
    rest = x - first
    second = rest.astype(jnp.bfloat16).astype(jnp.float32)
    third = (rest - second).astype(jnp.bfloat16).astype(jnp.float32)
    return first, second, third


def pick_row(shape, rows):
    index = lax.broadcasted_iota(jnp.int32, shape, 0)
    out = jnp.zeros(shape, jnp.float32)
    for i, row in enumerate(rows):
        out = jnp.where(index == i, row, out)
    return out


def partial_kernel(n_col, swapped, panel_ref, inv_ref, *out_refs):
    rows = panel_ref.shape[0] // n_col
    me = lax.axis_index("col")
    inv = inv_ref[...]
    for d in range(n_col):
        block = me ^ d if swapped else d
        mine = panel_ref[pl.ds(block * rows, rows), :]
        slab = lax.dot_general(
            mine, inv, (((1,), (1,)), ((), ())), preferred_element_type=jnp.float32
        ).astype(jnp.bfloat16)
        part = jnp.dot(slab, inv, preferred_element_type=jnp.float32)
        if swapped:
            out_refs[d][...] = part.astype(out_refs[d].dtype)
        else:
            out_refs[0][d] = part.astype(out_refs[0].dtype)


def partial(panel, inv, n_col, swapped):
    rows, width = panel.shape[0] // n_col, panel.shape[1]
    if swapped:
        shapes = [jax.ShapeDtypeStruct((rows, width), jnp.float32 if d == 0 else LINK) for d in range(n_col)]
    else:
        shapes = [jax.ShapeDtypeStruct((n_col, rows, width), LINK)]
    return pl.pallas_call(
        functools.partial(partial_kernel, n_col, swapped),
        out_shape=shapes,
        in_specs=[VMEM] * 2,
        out_specs=[VMEM] * len(shapes),
        name="partial",
    )(panel, inv)


def columns_kernel(
    per_tile, points_ref, scale_ref, target_ref, pick_ref, a_ref, b_ref, inv_ref,
    k_ref, sums_ref, p32, pwide, pt, s32, st, inverse_scale, weight,
):
    din = points_ref.shape[0]
    depth = points_ref.shape[1]
    step = pl.program_id(0)

    @pl.when(step == 0)
    def _():
        inverse = 1.0 / column(scale_ref[...])
        inverse_scale[...] = inverse
        p32[...] = jnp.zeros_like(p32)
        s32[...] = jnp.zeros_like(s32)
        st[...] = jnp.zeros_like(st)
        p32[:din, :] = (points_ref[...] - 0.5) * inverse * LOG2E
        p = p32[...]
        first, second, third = split3(p)
        for g, part in enumerate((first, first, second, second, first, third)):
            pwide[g * GROUP : (g + 1) * GROUP, :] = part
        norm = (-0.5 / LOG2E) * jnp.sum(p * p, axis=0, keepdims=True)
        minus = jnp.full_like(norm, -1.0)
        pwide[6 * GROUP : 7 * GROUP, :] = pick_row((GROUP, depth), (minus, minus, minus) + split3(norm))
        pwide[7 * GROUP :, :] = jnp.zeros((GROUP, depth), jnp.float32)
        pt[...] = jnp.transpose(pwide[...]).astype(jnp.bfloat16)
        weight[...] = (
            jnp.sum(inv_ref[...].astype(jnp.float32) * target_ref[...].astype(jnp.float32), axis=1, keepdims=True)
            .astype(jnp.bfloat16)
            .astype(jnp.float32)
        )

    tile = a_ref.shape[1]
    wide = tile // per_tile
    for i in range(per_tile):
        chosen = column(pick_ref[pl.ds(step * per_tile + i, 1), :])
        here = pl.ds(i * wide, wide)
        s32[:din, here] = (jnp.where(chosen == 1, b_ref[:, here], a_ref[:, here]) - 0.5) * inverse_scale[...]
    s = s32[...]
    first, second, third = split3(s)
    for g, part in enumerate((first, second, first, second, third, first)):
        st[g * GROUP : (g + 1) * GROUP, :] = part.astype(jnp.bfloat16)
    norm = (0.5 * LOG2E) * jnp.sum(s * s, axis=0, keepdims=True)
    one = jnp.ones_like(norm)
    st[6 * GROUP : 7 * GROUP, :] = pick_row((GROUP, tile), split3(norm) + (one, one, one)).astype(jnp.bfloat16)

    chunk = min(256, depth)
    solve = None
    for m in range(depth // chunk):
        here = slice(m * chunk, (m + 1) * chunk)
        power = jnp.dot(pt[here, :], st[...], preferred_element_type=jnp.float32)
        k = jnp.exp2(power).astype(jnp.bfloat16)
        k_ref[here, :] = k
        term = jnp.dot(inv_ref[:, here], k, preferred_element_type=jnp.float32)
        solve = term if solve is None else solve + term
    solve = solve.astype(jnp.bfloat16).astype(jnp.float32)
    sums_ref[0:1, :] = jnp.sum(solve * weight[...], axis=0, keepdims=True)
    sums_ref[1:2, :] = jnp.sum(solve * solve, axis=0, keepdims=True)


def columns(points, scales, targets, base_a, base_b, picks, inv):
    din, depth = points.shape
    wide = base_a.shape[1]
    blocks = picks.shape[0]
    per_tile = 2 if blocks % 2 == 0 else 1
    tile = wide // blocks * per_tile
    slab = inv.shape[0]
    whole = lambda shape: pl.BlockSpec(shape, lambda i: (0, 0), pipeline_mode=pl.Buffered(1))
    moving = lambda rows: pl.BlockSpec((rows, tile), lambda i: (0, i))
    return pl.pallas_call(
        functools.partial(columns_kernel, per_tile),
        grid=(wide // tile,),
        out_shape=[
            jax.ShapeDtypeStruct((depth, wide), jnp.bfloat16),
            jax.ShapeDtypeStruct((2, wide), jnp.float32),
        ],
        in_specs=[
            whole((din, depth)), whole((1, din)), whole((1, depth)), whole((blocks, din)),
            moving(din), moving(din), whole((slab, depth)),
        ],
        out_specs=[moving(depth), moving(2)],
        scratch_shapes=[
            pltpu.VMEM((GROUP, depth), jnp.float32),
            pltpu.VMEM((DEPTH, depth), jnp.float32),
            pltpu.VMEM((depth, DEPTH), jnp.bfloat16),
            pltpu.VMEM((GROUP, tile), jnp.float32),
            pltpu.VMEM((DEPTH, tile), jnp.bfloat16),
            pltpu.VMEM((din, 1), jnp.float32),
            pltpu.VMEM((slab, 1), jnp.float32),
        ],
        compiler_params=pltpu.CompilerParams(vmem_limit_bytes=32 * 2**20),
        cost_estimate=pl.CostEstimate(
            flops=2 * depth * wide * (DEPTH + slab), bytes_accessed=2 * depth * wide, transcendentals=depth * wide
        ),
        name="columns",
    )(points, scales.reshape(1, din), targets.reshape(1, depth), picks, base_a, base_b, inv)


def update_kernel(places, n_in, *refs):
    blocks, (k_ref, rhs_ref, panel_ref, trailing_ref) = refs[:n_in], refs[n_in : n_in + 4]
    cross_ref, next_ref, left = refs[n_in + 4 :]
    rows = cross_ref.shape[0]

    @pl.when(pl.program_id(0) == 0)
    def _():
        me = lax.axis_index("row")
        for ref, place in zip(blocks, places):
            height = ref.shape[0]
            start = 0 if place is None else (me ^ place) * height
            full = ref[...].astype(jnp.float32)
            high = full.astype(jnp.bfloat16)
            left[0, pl.ds(start, height), :] = high
            left[1, pl.ds(start, height), :] = (full - high.astype(jnp.float32)).astype(jnp.bfloat16)
        panel = panel_ref[...]
        product = sum(
            lax.dot_general(panel, left[i], (((1,), (1,)), ((), ())), preferred_element_type=jnp.float32)
            for i in range(2)
        )
        next_ref[...] = trailing_ref[...] - product

    k = k_ref[...]
    product = jnp.dot(left[...].reshape(2 * rows, left.shape[2]), k, preferred_element_type=jnp.float32)
    cross_ref[...] = (
        rhs_ref[...].astype(jnp.float32) - (product[:rows] + product[rows:])
    ).astype(cross_ref.dtype)


def update(blocks, places, k, rhs, panel, trailing):
    depth, wide = k.shape
    rows = rhs.shape[0]
    tile = tile_of(wide, 512)
    whole = lambda x: pl.BlockSpec(x.shape, lambda i: (0, 0), pipeline_mode=pl.Buffered(1))
    moving = lambda rows: pl.BlockSpec((rows, tile), lambda i: (0, i))
    return pl.pallas_call(
        functools.partial(update_kernel, places, len(blocks)),
        grid=(wide // tile,),
        out_shape=[
            jax.ShapeDtypeStruct(rhs.shape, rhs.dtype),
            jax.ShapeDtypeStruct(trailing.shape, trailing.dtype),
        ],
        in_specs=[whole(b) for b in blocks] + [moving(depth), moving(rows), whole(panel), whole(trailing)],
        out_specs=[moving(rows), pl.BlockSpec(trailing.shape, lambda i: (0, 0))],
        scratch_shapes=[pltpu.VMEM((2, rows, depth), jnp.bfloat16)],
        compiler_params=pltpu.CompilerParams(vmem_limit_bytes=32 * 2**20),
        cost_estimate=pl.CostEstimate(
            flops=4 * rows * depth * wide, bytes_accessed=2 * depth * wide, transcendentals=0
        ),
        name="update",
    )(*blocks, k, rhs, panel, trailing)


def swap(x, axis, d):
    return lax.ppermute(x, axis, [(i, i ^ d) for i in range(lax.axis_size(axis))])


def local(
    trailing,
    panel_block,
    diag_inverse,
    panel_points,
    lengthscales,
    targets,
    base_a,
    base_b,
    pick_sets,
    cross_rhs,
    mean_in,
    var_in,
):
    n_row, n_col = lax.axis_size("row"), lax.axis_size("col")
    near = n_col in (2, 4)
    parts = partial(panel_block, diag_inverse, n_col, near)
    if near:
        got = [swap(parts[d], "col", d) for d in range(1, n_col)]
    k, sums = columns(panel_points, lengthscales, targets, base_a, base_b, pick_sets, diag_inverse)
    if near:
        reduced = parts[0]
        for x in got:
            reduced = reduced + x.astype(jnp.float32)
        totals = [sums] + [swap(sums, "col", d) for d in range(1, n_col)]
        total = sum(totals[1:], totals[0])
    else:
        reduced = lax.all_to_all(parts[0], "col", 0, 0).astype(jnp.float32).sum(0)
        total = lax.psum(sums, "col")
    reduced = reduced.astype(LINK)
    if n_row == 8:
        even = {0: reduced, **{d: swap(reduced, "row", d) for d in (2, 4, 6)}}
        odd = {d + 1: swap(x, "row", 1) for d, x in even.items()}
        both = {**even, **odd}
        places, blocks = tuple(both), list(both.values())
    else:
        places, blocks = (None,), [lax.all_gather(reduced, "row", axis=0, tiled=True)]
    cross_next, trailing_next = update(blocks, places, k, cross_rhs, panel_block, trailing)
    return trailing_next, cross_next, mean_in + total[0], var_in - total[1]


def solution(mesh):
    placed = (
        P("row", "col"),
        P("row", None),
        P("col", None),
        P(),
        P(),
        P(),
        P(None, "row"),
        P(None, "row"),
        P("row", None),
        P("col", "row"),
        P("row"),
        P("row"),
    )
    return jax.shard_map(
        local,
        mesh=mesh,
        in_specs=placed,
        out_specs=(P("row", "col"), P("col", "row"), P("row"), P("row")),
        check_vma=False,
    )
```

time: 167 us -> 43 us (0.26)
  blocking collectives: 60.8 us -> 0 us
  waiting for transfers between devices: 59.2 us -> 3.77 us
  matrix products: 26.4 us -> 0 us
  Pallas kernels: 0 us -> 17.1 us
  starting transfers between devices: 0.04 us -> 13.8 us
  between operations: 14.2 us -> 0.76 us
  local copies, waits for them, and re-layouts: 0.37 us -> 5.94 us
  other arithmetic: 5.48 us -> 1.25 us
    all_gather x3 -> x0, blocking collectives: 60.8 us -> none  [the longest x1 38.7 us: local(): own_rows = lax.all_gather(slab_cols, 'col', axis=1, tiled=True)]
    all_gather x1 -> x0, waiting for transfers between devices: 59.2 us -> none  [local(): solve_piece = lax.all_gather(solve_slab, 'col', axis=0, tiled=True)]
    dot_general x7 -> x0, matrix products: 26.4 us -> none  [the longest x1 14.2 us: kernel_block(): lax.dot_general(scaled_points, candidates, (((0,), (0,)), ((), ())), prec...]
    pallas_call x0 -> x3, Pallas kernels: none -> 17.1 us  [the longest x1 8.79 us: columns(): pl.pallas_call(functools.partial(columns_kernel, per_tile), grid=(wide //...]
    ppermute x0 -> x13, starting transfers between devices: none -> 13.8 us  [swap(): lax.ppermute(x, axis, [(i, i ^ d) for i in range(lax.axis_size(axis))])]
    unnamed x21 -> x24, local copies, waits for them, and re-layouts: 0.25 us -> 5.23 us
    ppermute x0 -> x13, waiting for transfers between devices: none -> 3.77 us  [swap(): lax.ppermute(x, axis, [(i, i ^ d) for i in range(lax.axis_size(axis))])]
    reduce_sum x3 -> x0, other arithmetic: 3.5 us -> none  [the longest x1 1.3 us: local(): square_sum = jnp.sum(widened * widened, axis=0)]
  transfers between devices with their start and end apart: 1 -> 13, of which waited for: 1 -> 4; matrix products, arithmetic and copies ran while one was open for 1% -> 5% of each run, Pallas kernels for 0% -> 21%
where the time goes in v1:
time: 43 us; the launch traced here: 42.6 us
  Pallas kernels  17.1 us (40%)
  starting transfers between devices  13.8 us (32%)
  local copies, waits for them, and re-layouts  5.94 us (14%)
  waiting for transfers between devices  3.77 us (9%)
  other arithmetic  1.25 us (3%)
  between operations  0.76 us (2%)
    ppermute x13, starting transfers between devices, swap(): lax.ppermute(x, axis, [(i, i ^ d) for i in range(lax.axis_size(axis))])  13.8 us
    pallas_call x1, Pallas kernels, columns(): pl.pallas_call(functools.partial(columns_kernel, per_tile), grid=(wide //...  8.79 us
    unnamed x24, local copies, waits for them, and re-layouts  5.23 us
    pallas_call x1, Pallas kernels, update(): pl.pallas_call(functools.partial(update_kernel, places, len(blocks)), gri...  4.5 us
    pallas_call x1, Pallas kernels, partial(): pl.pallas_call(functools.partial(partial_kernel, n_col, swapped), out_sha...  3.84 us
    ppermute x13, waiting for transfers between devices, swap(): lax.ppermute(x, axis, [(i, i ^ d) for i in range(lax.axis_size(axis))])  3.77 us
  transfers between devices with their start and end apart: 13, of which 4 were waited for; matrix products, arithmetic and copies ran while one was open for 5% of the time, Pallas kernels for 21%

profile of v1, /device:TPU:0, one launch (start us, length us, event | category | flops | bytes accessed | tf_op | source)
XLA Modules:
  0.0 42.6 jit_solution(9471312679236073911)
XLA Ops:
  0.7 3.8 %partial.1 = (f32[16,1024]{1,0:T(8,128)}, f32[16,1024]{1,0:T(8,128)}, f32[16,1024]{1,0:T(8,128)}, f32[16,1024]{1,0:T(8,128)}) custom-call(bf16[64,1024]{1,0:T(8,128)(2,1)} %refs_10_.1, bf16[256,1024]{1,0:T(8,128)(2,1)} %inv_ref.3), custom_call_target="tpu_custom_call" | custom-call | tf_op jit(solution)/shard_map/partial/pallas_call | solution.py:69
  4.5 3.0 %collective-permute-start = (f32[16,1024]{1,0:T(8,128)}, f32[16,1024]{1,0:T(8,128)S(1)}, u32[]{:S(2)}, u32[]{:S(2)}) collective-permute-start(f32[16,1024]{1,0:T(8,128)} %get-tuple-element.13), channel_id=1, source_target_pairs={{0,1},{1,0},{2,3},{3,2},{4,5},{5,4},{6,7},{7,6},{8,9},{9,8},{10,11... | collective-permute-start | bytes 196616 | tf_op jit(solution)/shard_map/ppermute | solution.py:229
  7.5 2.6 %collective-permute-start.1 = (f32[16,1024]{1,0:T(8,128)}, f32[16,1024]{1,0:T(8,128)S(1)}, u32[]{:S(2)}, u32[]{:S(2)}) collective-permute-start(f32[16,1024]{1,0:T(8,128)} %get-tuple-element.14), channel_id=1, source_target_pairs={{0,2},{1,3},{2,0},{3,1},{4,6},{5,7},{6,4},{7,5},{8,10},{9,11},{10,... | collective-permute-start | bytes 196616 | tf_op jit(solution)/shard_map/ppermute | solution.py:229
  10.1 0.7 %reshape.15.target_ref = bf16[1,1024]{1,0:T(2,128)(2,1)S(1)} reshape(bf16[1024]{0:T(1024)(128)(2,1)} %param.17) | data formatting | bytes 4096 | tf_op jit(solution)/shard_map/reshape | solution.py:172
  10.8 1.0 %copy-done.2 = bf16[256,1024]{1,0:T(8,128)(2,1)S(1)} copy-done((bf16[256,1024]{1,0:T(8,128)(2,1)S(1)}, bf16[256,1024]{1,0:T(8,128)(2,1)}, u32[]{:S(2)}) %copy-start.2) | copy-done | bytes 524312
  11.8 1.0 %copy-done.4 = f32[20,3072]{1,0:T(8,128)S(1)} copy-done((f32[20,3072]{1,0:T(8,128)S(1)}, f32[20,3072]{1,0:T(8,128)}, u32[]{:S(2)}) %copy-start.4) | copy-done | bytes 245784
  12.8 1.0 %copy-done.5 = f32[20,3072]{1,0:T(8,128)S(1)} copy-done((f32[20,3072]{1,0:T(8,128)S(1)}, f32[20,3072]{1,0:T(8,128)}, u32[]{:S(2)}) %copy-start.5) | copy-done | bytes 245784
  13.8 0.9 %copy-done.6 = f32[20,1024]{1,0:T(8,128)S(1)} copy-done((f32[20,1024]{1,0:T(8,128)S(1)}, f32[20,1024]{1,0:T(8,128)}, u32[]{:S(2)}) %copy-start.6) | copy-done | bytes 81944
  14.7 0.7 %copy-done.7 = s32[12,20]{1,0:T(8,128)S(1)} copy-done((s32[12,20]{1,0:T(8,128)S(1)}, s32[12,20]{1,0:T(8,128)}, u32[]{:S(2)}) %copy-start.7) | copy-done | bytes 984
  15.4 0.7 %copy-done.8 = f32[20]{0:T(128)S(1)} copy-done((f32[20]{0:T(128)S(1)}, f32[20]{0:T(128)}, u32[]{:S(2)}) %copy-start.8) | copy-done | bytes 104
  16.0 8.8 %columns.1 = (bf16[1024,3072]{1,0:T(8,128)(2,1)S(1)}, f32[2,3072]{1,0:T(2,128)S(1)}) custom-call(f32[20,1024]{1,0:T(8,128)S(1)} %copy-done.6, f32[1,20]{1,0:T(1,128)S(1)} %bitcast.3, bf16[1,1024]{1,0:T(2,128)(2,1)S(1)} %reshape.15.target_ref, s32[12,20]{1,0:T(8,128)S(1)} %copy-done.7, f32[20,3072]{1,0:T(8,128)S(1)} %copy-done.4, f32[20,3072]{1,0:T(8,128)S(1)} %copy-done.5, ...), custom_call_target="tpu_custom_call" | custom-call | flops 3221225472 | bytes 6291456 | tf_op jit(solution)/shard_map/columns/pallas_call | solution.py:146
  24.8 3.9 %collective-permute-start.12 = (f32[2,3072]{1,0:T(2,128)S(1)}, f32[2,3072]{1,0:T(2,128)S(1)}, u32[]{:S(2)}, u32[]{:S(2)}) collective-permute-start(f32[2,3072]{1,0:T(2,128)S(1)} %get-tuple-element.19), channel_id=1, source_target_pairs={{0,3},{1,2},{2,1},{3,0},{4,7},{5,6},{6,5},{7,4},{8,11},{9,10},{10,... | collective-permute-start | bytes 73736 | tf_op jit(solution)/shard_map/ppermute | solution.py:229
  28.7 0.6 %collective-permute-start.10 = (f32[2,3072]{1,0:T(2,128)S(1)}, f32[2,3072]{1,0:T(2,128)S(1)}, u32[]{:S(2)}, u32[]{:S(2)}) collective-permute-start(f32[2,3072]{1,0:T(2,128)S(1)} %get-tuple-element.19), channel_id=1, source_target_pairs={{0,1},{1,0},{2,3},{3,2},{4,5},{5,4},{6,7},{7,6},{8,9},{9,8},{10,11... | collective-permute-start | bytes 73736 | tf_op jit(solution)/shard_map/ppermute | solution.py:229
  29.4 2.6 %collective-permute-start.5 = (f32[16,1024]{1,0:T(8,128)S(1)}, f32[16,1024]{1,0:T(8,128)S(1)}, u32[]{:S(2)}, u32[]{:S(2)}) collective-permute-start(f32[16,1024]{1,0:T(8,128)S(1)} %add_add_fusion.refs_0_), channel_id=1, source_target_pairs={{0,24},{4,28},{8,16},{12,20},{16,8},{20,12},{24,0},{28,4},{1,25},{... | collective-permute-start | bytes 196616 | tf_op jit(solution)/shard_map/ppermute | solution.py:229
  32.0 0.5 %collective-permute-start.4 = (f32[16,1024]{1,0:T(8,128)S(1)}, f32[16,1024]{1,0:T(8,128)S(1)}, u32[]{:S(2)}, u32[]{:S(2)}) collective-permute-start(f32[16,1024]{1,0:T(8,128)S(1)} %add_add_fusion.refs_0_), channel_id=1, source_target_pairs={{0,16},{4,20},{8,24},{12,28},{16,0},{20,4},{24,8},{28,12},{1,17},{... | collective-permute-start | bytes 196616 | tf_op jit(solution)/shard_map/ppermute | solution.py:229
  32.6 0.4 collective-permute-start.3
  33.0 0.5 %collective-permute-done.11 = f32[2,3072]{1,0:T(2,128)S(1)} collective-permute-done((f32[2,3072]{1,0:T(2,128)S(1)}, f32[2,3072]{1,0:T(2,128)S(1)}, u32[]{:S(2)}, u32[]{:S(2)}) %collective-permute-start.11) | collective-permute-done | bytes 24608 | tf_op jit(solution)/shard_map/ppermute | solution.py:229
  33.5 0.1 collective-permute-start.6
  33.5 1.7 %collective-permute-done.5.refs_3_ = f32[16,1024]{1,0:T(8,128)S(1)} collective-permute-done((f32[16,1024]{1,0:T(8,128)S(1)}, f32[16,1024]{1,0:T(8,128)S(1)}, u32[]{:S(2)}, u32[]{:S(2)}) %collective-permute-start.5) | collective-permute-done | bytes 65568 | tf_op jit(solution)/shard_map/ppermute | solution.py:229
  35.2 1.1 %collective-permute-done.4.refs_2_ = f32[16,1024]{1,0:T(8,128)S(1)} collective-permute-done((f32[16,1024]{1,0:T(8,128)S(1)}, f32[16,1024]{1,0:T(8,128)S(1)}, u32[]{:S(2)}, u32[]{:S(2)}) %collective-permute-start.4) | collective-permute-done | bytes 65568 | tf_op jit(solution)/shard_map/ppermute | solution.py:229
  36.3 0.5 %collective-permute-done.3.refs_1_ = f32[16,1024]{1,0:T(8,128)S(1)} collective-permute-done((f32[16,1024]{1,0:T(8,128)S(1)}, f32[16,1024]{1,0:T(8,128)S(1)}, u32[]{:S(2)}, u32[]{:S(2)}) %collective-permute-start.3) | collective-permute-done | bytes 65568 | tf_op jit(solution)/shard_map/ppermute | solution.py:229
  36.9 0.6 %sub.3 = f32[3072]{0:T(1024)} subtract(f32[3072]{0:T(1024)S(1)} %copy-done.10, f32[3072]{0:T(1024)S(1)} %bitcast.5) | non-fusion elementwise | flops 3072 | bytes 36864 | tf_op jit(solution)/shard_map/sub | solution.py:270
  37.5 0.6 %add.27 = f32[3072]{0:T(1024)} add(f32[3072]{0:T(1024)S(1)} %copy-done.11, f32[3072]{0:T(1024)S(1)} %bitcast.4) | non-fusion elementwise | flops 3072 | bytes 36864 | tf_op jit(solution)/shard_map/add | solution.py:270
  38.1 4.5 %update.1 = (bf16[128,3072]{1,0:T(8,128)(2,1)}, f32[64,128]{1,0:T(8,128)}) custom-call(f32[16,1024]{1,0:T(8,128)S(1)} %add_add_fusion.refs_0_, f32[16,1024]{1,0:T(8,128)S(1)} %collective-permute-done.3.refs_1_, f32[16,1024]{1,0:T(8,128)S(1)} %collective-permute-done.4.refs_2_, f32[16,1024]{1,0:T(8,128)S(1)} %collective-permute-done.5.refs_3_, ...), custom_call_target="tpu_custom_call" | custom-call | flops 1610612736 | bytes 6291456 | tf_op jit(solution)/shard_map/update/pallas_call | solution.py:210
  (35 shorter events, 0.1 us)
Async XLA Ops:
  0.6 36.2 %copy-start.10 = (f32[3072]{0:T(1024)S(1)}, f32[3072]{0:T(1024)}, u32[]{:S(2)}) copy-start(f32[3072]{0:T(1024)} %param.23) | copy-start | bytes 36868
  0.6 36.8 %copy-start.11 = (f32[3072]{0:T(1024)S(1)}, f32[3072]{0:T(1024)}, u32[]{:S(2)}) copy-start(f32[3072]{0:T(1024)} %param.22) | copy-start | bytes 36868
  0.7 37.4 %copy-start.3 = (f32[64,128]{1,0:T(8,128)S(1)}, f32[64,128]{1,0:T(8,128)}, u32[]{:S(2)}) copy-start(f32[64,128]{1,0:T(8,128)} %refs_11_.1) | copy-start | bytes 98308
  4.5 33.6 %copy-start = (bf16[128,3072]{1,0:T(8,128)(2,1)S(1)}, bf16[128,3072]{1,0:T(8,128)(2,1)}, u32[]{:S(2)}) copy-start(bf16[128,3072]{1,0:T(8,128)(2,1)} %refs_9_.1) | copy-start | bytes 2359300
  4.5 33.6 %copy-start.1 = (bf16[64,1024]{1,0:T(8,128)(2,1)S(1)}, bf16[64,1024]{1,0:T(8,128)(2,1)}, u32[]{:S(2)}) copy-start(bf16[64,1024]{1,0:T(8,128)(2,1)} %refs_10_.1) | copy-start | bytes 393220
  4.5 24.2 %collective-permute-start = (f32[16,1024]{1,0:T(8,128)}, f32[16,1024]{1,0:T(8,128)S(1)}, u32[]{:S(2)}, u32[]{:S(2)}) collective-permute-start(f32[16,1024]{1,0:T(8,128)} %get-tuple-element.13), channel_id=1, source_target_pairs={{0,1},{1,0},{2,3},{3,2},{4,5},{5,4},{6,7},{7,6},{8,9},{9,8},{10,11... | collective-permute-start | bytes 196616 | tf_op jit(solution)/shard_map/ppermute | solution.py:229
  7.5 21.8 %collective-permute-start.1 = (f32[16,1024]{1,0:T(8,128)}, f32[16,1024]{1,0:T(8,128)S(1)}, u32[]{:S(2)}, u32[]{:S(2)}) collective-permute-start(f32[16,1024]{1,0:T(8,128)} %get-tuple-element.14), channel_id=1, source_target_pairs={{0,2},{1,3},{2,0},{3,1},{4,6},{5,7},{6,4},{7,5},{8,10},{9,11},{10,... | collective-permute-start | bytes 196616 | tf_op jit(solution)/shard_map/ppermute | solution.py:229
  10.1 19.2 %collective-permute-start.2 = (f32[16,1024]{1,0:T(8,128)}, f32[16,1024]{1,0:T(8,128)S(1)}, u32[]{:S(2)}, u32[]{:S(2)}) collective-permute-start(f32[16,1024]{1,0:T(8,128)} %get-tuple-element.15), channel_id=1, source_target_pairs={{0,3},{1,2},{2,1},{3,0},{4,7},{5,6},{6,5},{7,4},{8,11},{9,10},{10,... | collective-permute-start | bytes 196616 | tf_op jit(solution)/shard_map/ppermute | solution.py:229
  10.8 1.0 %copy-start.2 = (bf16[256,1024]{1,0:T(8,128)(2,1)S(1)}, bf16[256,1024]{1,0:T(8,128)(2,1)}, u32[]{:S(2)}) copy-start(bf16[256,1024]{1,0:T(8,128)(2,1)} %inv_ref.3) | copy-start | bytes 1572868
  11.8 1.0 %copy-start.4 = (f32[20,3072]{1,0:T(8,128)S(1)}, f32[20,3072]{1,0:T(8,128)}, u32[]{:S(2)}) copy-start(f32[20,3072]{1,0:T(8,128)} %a_ref.1) | copy-start | bytes 737284
  12.8 1.0 %copy-start.5 = (f32[20,3072]{1,0:T(8,128)S(1)}, f32[20,3072]{1,0:T(8,128)}, u32[]{:S(2)}) copy-start(f32[20,3072]{1,0:T(8,128)} %b_ref.1) | copy-start | bytes 737284
  13.8 0.9 %copy-start.6 = (f32[20,1024]{1,0:T(8,128)S(1)}, f32[20,1024]{1,0:T(8,128)}, u32[]{:S(2)}) copy-start(f32[20,1024]{1,0:T(8,128)} %points_ref.1) | copy-start | bytes 245764
  14.7 0.7 %copy-start.7 = (s32[12,20]{1,0:T(8,128)S(1)}, s32[12,20]{1,0:T(8,128)}, u32[]{:S(2)}) copy-start(s32[12,20]{1,0:T(8,128)} %pick_ref.1) | copy-start | bytes 2884
  16.0 13.3 %copy-start.9 = (f32[16,1024]{1,0:T(8,128)S(1)}, f32[16,1024]{1,0:T(8,128)}, u32[]{:S(2)}) copy-start(f32[16,1024]{1,0:T(8,128)} %get-tuple-element.12) | copy-start | bytes 196612
  24.8 7.7 %collective-permute-start.12 = (f32[2,3072]{1,0:T(2,128)S(1)}, f32[2,3072]{1,0:T(2,128)S(1)}, u32[]{:S(2)}, u32[]{:S(2)}) collective-permute-start(f32[2,3072]{1,0:T(2,128)S(1)} %get-tuple-element.19), channel_id=1, source_target_pairs={{0,3},{1,2},{2,1},{3,0},{4,7},{5,6},{6,5},{7,4},{8,11},{9,10},{10,... | collective-permute-start | bytes 73736 | tf_op jit(solution)/shard_map/ppermute | solution.py:229
  28.7 4.7 %collective-permute-start.11 = (f32[2,3072]{1,0:T(2,128)S(1)}, f32[2,3072]{1,0:T(2,128)S(1)}, u32[]{:S(2)}, u32[]{:S(2)}) collective-permute-start(f32[2,3072]{1,0:T(2,128)S(1)} %get-tuple-element.19), channel_id=1, source_target_pairs={{0,2},{1,3},{2,0},{3,1},{4,6},{5,7},{6,4},{7,5},{8,10},{9,11},{10,... | collective-permute-start | bytes 73736 | tf_op jit(solution)/shard_map/ppermute | solution.py:229
  28.7 4.7 %collective-permute-start.10 = (f32[2,3072]{1,0:T(2,128)S(1)}, f32[2,3072]{1,0:T(2,128)S(1)}, u32[]{:S(2)}, u32[]{:S(2)}) collective-permute-start(f32[2,3072]{1,0:T(2,128)S(1)} %get-tuple-element.19), channel_id=1, source_target_pairs={{0,1},{1,0},{2,3},{3,2},{4,5},{5,4},{6,7},{7,6},{8,9},{9,8},{10,11... | collective-permute-start | bytes 73736 | tf_op jit(solution)/shard_map/ppermute | solution.py:229
  29.4 5.8 %collective-permute-start.5 = (f32[16,1024]{1,0:T(8,128)S(1)}, f32[16,1024]{1,0:T(8,128)S(1)}, u32[]{:S(2)}, u32[]{:S(2)}) collective-permute-start(f32[16,1024]{1,0:T(8,128)S(1)} %add_add_fusion.refs_0_), channel_id=1, source_target_pairs={{0,24},{4,28},{8,16},{12,20},{16,8},{20,12},{24,0},{28,4},{1,25},{... | collective-permute-start | bytes 196616 | tf_op jit(solution)/shard_map/ppermute | solution.py:229
  32.0 4.3 %collective-permute-start.4 = (f32[16,1024]{1,0:T(8,128)S(1)}, f32[16,1024]{1,0:T(8,128)S(1)}, u32[]{:S(2)}, u32[]{:S(2)}) collective-permute-start(f32[16,1024]{1,0:T(8,128)S(1)} %add_add_fusion.refs_0_), channel_id=1, source_target_pairs={{0,16},{4,20},{8,24},{12,28},{16,0},{20,4},{24,8},{28,12},{1,17},{... | collective-permute-start | bytes 196616 | tf_op jit(solution)/shard_map/ppermute | solution.py:229
  32.6 4.3 %collective-permute-start.3 = (f32[16,1024]{1,0:T(8,128)S(1)}, f32[16,1024]{1,0:T(8,128)S(1)}, u32[]{:S(2)}, u32[]{:S(2)}) collective-permute-start(f32[16,1024]{1,0:T(8,128)S(1)} %add_add_fusion.refs_0_), channel_id=1, source_target_pairs={{0,8},{4,12},{8,0},{12,4},{16,24},{20,28},{24,16},{28,20},{1,9},{5... | collective-permute-start | bytes 196616 | tf_op jit(solution)/shard_map/ppermute | solution.py:229
  33.5 4.6 %collective-permute-start.6 = (f32[16,1024]{1,0:T(8,128)S(1)}, f32[16,1024]{1,0:T(8,128)S(1)}, u32[]{:S(2)}, u32[]{:S(2)}) collective-permute-start(f32[16,1024]{1,0:T(8,128)S(1)} %add_add_fusion.refs_0_), channel_id=1, source_target_pairs={{0,4},{4,0},{8,12},{12,8},{16,20},{20,16},{24,28},{28,24},{1,5},{5... | collective-permute-start | bytes 196616 | tf_op jit(solution)/shard_map/ppermute | solution.py:229
  35.2 2.8 %collective-permute-start.9 = (f32[16,1024]{1,0:T(8,128)S(1)}, f32[16,1024]{1,0:T(8,128)S(1)}, u32[]{:S(2)}, u32[]{:S(2)}) collective-permute-start(f32[16,1024]{1,0:T(8,128)S(1)} %collective-permute-done.5.refs_3_), channel_id=1, source_target_pairs={{0,4},{4,0},{8,12},{12,8},{16,20},{20,16},{24,28},{28,24},{1,5},{5... | collective-permute-start | bytes 196616 | tf_op jit(solution)/shard_map/ppermute | solution.py:229
  36.3 1.8 %collective-permute-start.8 = (f32[16,1024]{1,0:T(8,128)S(1)}, f32[16,1024]{1,0:T(8,128)S(1)}, u32[]{:S(2)}, u32[]{:S(2)}) collective-permute-start(f32[16,1024]{1,0:T(8,128)S(1)} %collective-permute-done.4.refs_2_), channel_id=1, source_target_pairs={{0,4},{4,0},{8,12},{12,8},{16,20},{20,16},{24,28},{28,24},{1,5},{5... | collective-permute-start | bytes 196616 | tf_op jit(solution)/shard_map/ppermute | solution.py:229
  36.8 1.3 %collective-permute-start.7 = (f32[16,1024]{1,0:T(8,128)S(1)}, f32[16,1024]{1,0:T(8,128)S(1)}, u32[]{:S(2)}, u32[]{:S(2)}) collective-permute-start(f32[16,1024]{1,0:T(8,128)S(1)} %collective-permute-done.3.refs_1_), channel_id=1, source_target_pairs={{0,4},{4,0},{8,12},{12,8},{16,20},{20,16},{24,28},{28,24},{1,5},{5... | collective-permute-start | bytes 196616 | tf_op jit(solution)/shard_map/ppermute | solution.py:229
  (1 other events, 0.7 us)

commit v2 on v1

v2 whole, which is shorter than its diff:
```python
import functools

import jax
import jax.numpy as jnp
from jax import lax
from jax.experimental import pallas as pl
from jax.experimental.pallas import tpu as pltpu
from jax.sharding import PartitionSpec as P

GROUP = 32
DEPTH = 8 * GROUP
LINK = jnp.float32
VMEM = pl.BlockSpec(memory_space=pltpu.VMEM)
HBM = pl.BlockSpec(memory_space=pltpu.HBM)


def in_hbm(*arrays):
    return [pltpu.with_memory_space_constraint(x, pltpu.HBM) for x in arrays]


def fetch(sources, targets, sems):
    copies = [pltpu.make_async_copy(s, t, sems.at[i]) for i, (s, t) in enumerate(zip(sources, targets))]
    for c in copies:
        c.start()
    return copies


def tile_of(n, most):
    while n % most:
        most //= 2
    return most


def column(row):
    n = row.shape[1]
    eye = lax.broadcasted_iota(jnp.int32, (n, n), 0) == lax.broadcasted_iota(jnp.int32, (n, n), 1)
    return jnp.sum(jnp.where(eye, row, jnp.zeros_like(row)), axis=1, keepdims=True)


def split3(x):
    first = x.astype(jnp.bfloat16).astype(jnp.float32)
    rest = x - first
    second = rest.astype(jnp.bfloat16).astype(jnp.float32)
    third = (rest - second).astype(jnp.bfloat16).astype(jnp.float32)
    return first, second, third


def pick_row(shape, rows):
    index = lax.broadcasted_iota(jnp.int32, shape, 0)
    out = jnp.zeros(shape, jnp.float32)
    for i, row in enumerate(rows):
        out = jnp.where(index == i, row, out)
    return out


def partial_kernel(n_col, swapped, panel_hbm, inv_hbm, *refs):
    out_refs, (panel_ref, inv_ref, sems) = refs[:-3], refs[-3:]
    copies = fetch((panel_hbm, inv_hbm), (panel_ref, inv_ref), sems)
    rows = panel_ref.shape[0] // n_col
    me = lax.axis_index("col")
    for c in copies:
        c.wait()
    inv = inv_ref[...]
    panel = panel_ref[...]
    if swapped:
        panel = jnp.concatenate([panel_ref[pl.ds((me ^ d) * rows, rows), :] for d in range(n_col)], axis=0)
    slab = lax.dot_general(
        panel, inv, (((1,), (1,)), ((), ())), preferred_element_type=jnp.float32
    ).astype(jnp.bfloat16)
    part = jnp.dot(slab, inv, preferred_element_type=jnp.float32)
    if swapped:
        for d in range(n_col):
            out_refs[d][...] = part[d * rows : (d + 1) * rows].astype(out_refs[d].dtype)
    else:
        out_refs[0][...] = part.reshape(out_refs[0].shape).astype(out_refs[0].dtype)


def partial(panel, inv, n_col, swapped):
    rows, width = panel.shape[0] // n_col, panel.shape[1]
    if swapped:
        shapes = [jax.ShapeDtypeStruct((rows, width), jnp.float32 if d == 0 else LINK) for d in range(n_col)]
    else:
        shapes = [jax.ShapeDtypeStruct((n_col, rows, width), LINK)]
    return pl.pallas_call(
        functools.partial(partial_kernel, n_col, swapped),
        out_shape=shapes,
        in_specs=[HBM] * 2,
        out_specs=[VMEM] * len(shapes),
        scratch_shapes=[pltpu.VMEM(x.shape, x.dtype) for x in (panel, inv)] + [pltpu.SemaphoreType.DMA((2,))],
        compiler_params=pltpu.CompilerParams(vmem_limit_bytes=16 * 2**20),
        name="partial",
    )(*in_hbm(panel, inv))


def columns_kernel(
    tile, points_hbm, scale_hbm, target_hbm, pick_hbm, a_hbm, b_hbm, inv_hbm,
    k_ref, sums_ref,
    points_ref, scale_ref, target_ref, pick_ref, a_ref, b_ref, inv_ref,
    p32, pwide, pt, s32, st, sems,
):
    copies = fetch(
        (points_hbm, scale_hbm, pick_hbm, a_hbm, b_hbm, inv_hbm, target_hbm),
        (points_ref, scale_ref, pick_ref, a_ref, b_ref, inv_ref, target_ref),
        sems,
    )
    din, depth = points_ref.shape
    wide = a_ref.shape[1]
    block = wide // pick_ref.shape[0]
    p32[...] = jnp.zeros_like(p32)
    s32[...] = jnp.zeros_like(s32)
    st[...] = jnp.zeros_like(st)
    for c in copies[:2]:
        c.wait()
    inverse = 1.0 / column(scale_ref[...])
    p32[:din, :] = (points_ref[...] - 0.5) * inverse
    p = p32[...]
    first, second, third = split3(p)
    for g, part in enumerate((first, first, second, second, first, third)):
        pwide[g * GROUP : (g + 1) * GROUP, :] = part
    norm = -0.5 * jnp.sum(p * p, axis=0, keepdims=True)
    minus = jnp.full_like(norm, -1.0)
    pwide[6 * GROUP : 7 * GROUP, :] = pick_row((GROUP, depth), (minus, minus, minus) + split3(norm))
    pwide[7 * GROUP :, :] = jnp.zeros((GROUP, depth), jnp.float32)
    pt[...] = jnp.transpose(pwide[...]).astype(jnp.bfloat16)
    for c in copies[2:]:
        c.wait()
    weight = (
        jnp.sum(inv_ref[...].astype(jnp.float32) * target_ref[...].astype(jnp.float32).reshape(1, depth), axis=1, keepdims=True)
        .astype(jnp.bfloat16)
        .astype(jnp.float32)
    )

    def step(t, carry):
        cols = pl.ds(t * tile, tile)
        for i in range(tile // block):
            chosen = column(pick_ref[pl.ds(t * (tile // block) + i, 1), :])
            here = pl.ds(t * tile + i * block, block)
            s32[:din, i * block : (i + 1) * block] = (
                jnp.where(chosen == 1, b_ref[:, here], a_ref[:, here]) - 0.5
            ) * inverse
        s = s32[...]
        first, second, third = split3(s)
        for g, part in enumerate((first, second, first, second, third, first)):
            st[g * GROUP : (g + 1) * GROUP, :] = part.astype(jnp.bfloat16)
        norm = 0.5 * jnp.sum(s * s, axis=0, keepdims=True)
        one = jnp.ones_like(norm)
        st[6 * GROUP : 7 * GROUP, :] = pick_row((GROUP, tile), split3(norm) + (one, one, one)).astype(jnp.bfloat16)
        power = jnp.dot(pt[...], st[...], preferred_element_type=jnp.float32)
        k = jnp.exp(power).astype(jnp.bfloat16)
        k_ref[:, cols] = k
        solve = jnp.dot(inv_ref[...], k, preferred_element_type=jnp.float32)
        solve = solve.astype(jnp.bfloat16).astype(jnp.float32)
        sums_ref[0:1, cols] = jnp.sum(solve * weight, axis=0, keepdims=True)
        sums_ref[1:2, cols] = jnp.sum(solve * solve, axis=0, keepdims=True)
        return carry

    lax.fori_loop(0, wide // tile, step, 0, unroll=True)


def columns(points, scales, targets, base_a, base_b, picks, inv):
    din, depth = points.shape
    wide = base_a.shape[1]
    blocks = picks.shape[0]
    tile = wide // blocks * (2 if blocks % 2 == 0 else 1)
    ins = (points, scales.reshape(1, din), targets, picks, base_a, base_b, inv)
    return pl.pallas_call(
        functools.partial(columns_kernel, tile),
        out_shape=[
            jax.ShapeDtypeStruct((depth, wide), jnp.bfloat16),
            jax.ShapeDtypeStruct((2, wide), jnp.float32),
        ],
        in_specs=[HBM] * len(ins),
        out_specs=[VMEM] * 2,
        scratch_shapes=[pltpu.VMEM(x.shape, x.dtype) for x in ins]
        + [
            pltpu.VMEM((GROUP, depth), jnp.float32),
            pltpu.VMEM((DEPTH, depth), jnp.float32),
            pltpu.VMEM((depth, DEPTH), jnp.bfloat16),
            pltpu.VMEM((GROUP, tile), jnp.float32),
            pltpu.VMEM((DEPTH, tile), jnp.bfloat16),
            pltpu.SemaphoreType.DMA((len(ins),)),
        ],
        compiler_params=pltpu.CompilerParams(vmem_limit_bytes=32 * 2**20),
        cost_estimate=pl.CostEstimate(
            flops=2 * depth * wide * (DEPTH + inv.shape[0]), bytes_accessed=2 * depth * wide, transcendentals=depth * wide
        ),
        name="columns",
    )(*in_hbm(*ins))


def update_kernel(places, tile, n_in, *refs):
    blocks, (k_ref, rhs_ref, panel_ref, trailing_ref) = refs[:n_in], refs[n_in : n_in + 4]
    cross_hbm, next_ref, left, cross, sems = refs[n_in + 4 :]
    rows, wide = rhs_ref.shape
    me = lax.axis_index("row")
    for ref, place in zip(blocks, places):
        height = ref.shape[0]
        start = 0 if place is None else (me ^ place) * height
        full = ref[...].astype(jnp.float32)
        high = full.astype(jnp.bfloat16)
        left[pl.ds(start, height), :] = high
        left[pl.ds(start + rows, height), :] = (full - high.astype(jnp.float32)).astype(jnp.bfloat16)
    copies = []
    for t in range(wide // tile):
        here = slice(t * tile, (t + 1) * tile)
        product = jnp.dot(left[...], k_ref[:, here], preferred_element_type=jnp.float32)
        cross[:, here] = (
            rhs_ref[:, here].astype(jnp.float32) - (product[:rows] + product[rows:])
        ).astype(cross.dtype)
        copies.append(pltpu.make_async_copy(cross.at[:, here], cross_hbm.at[:, here], sems.at[t]))
        copies[-1].start()
    product = lax.dot_general(
        panel_ref[...], left[...], (((1,), (1,)), ((), ())), preferred_element_type=jnp.float32
    )
    next_ref[...] = trailing_ref[...] - (product[:, :rows] + product[:, rows:])
    for c in copies:
        c.wait()


def update(blocks, places, k, rhs, panel, trailing):
    depth, wide = k.shape
    rows = rhs.shape[0]
    tile = tile_of(wide, 512)
    return pl.pallas_call(
        functools.partial(update_kernel, places, tile, len(blocks)),
        out_shape=[
            jax.ShapeDtypeStruct(rhs.shape, rhs.dtype),
            jax.ShapeDtypeStruct(trailing.shape, trailing.dtype),
        ],
        in_specs=[VMEM] * (len(blocks) + 4),
        out_specs=[HBM, VMEM],
        scratch_shapes=[
            pltpu.VMEM((2 * rows, depth), jnp.bfloat16),
            pltpu.VMEM(rhs.shape, rhs.dtype),
            pltpu.SemaphoreType.DMA((wide // tile,)),
        ],
        compiler_params=pltpu.CompilerParams(vmem_limit_bytes=32 * 2**20),
        cost_estimate=pl.CostEstimate(
            flops=4 * rows * depth * wide, bytes_accessed=2 * depth * wide, transcendentals=0
        ),
        name="update",
    )(*blocks, k, rhs, panel, trailing)


def finish_kernel(*refs):
    parts, (mean_ref, var_ref, out_mean, out_var) = refs[:-4], refs[-4:]
    total = parts[0][...]
    for x in parts[1:]:
        total = total + x[...]
    out_mean[...] = mean_ref[...] + total[0:1]
    out_var[...] = var_ref[...] - total[1:2]


def finish(parts, mean, var):
    wide = mean.shape[0]
    flat = jax.ShapeDtypeStruct((1, wide), jnp.float32)
    out_mean, out_var = pl.pallas_call(
        finish_kernel,
        out_shape=[flat, flat],
        in_specs=[VMEM] * (len(parts) + 2),
        out_specs=[VMEM] * 2,
        compiler_params=pltpu.CompilerParams(vmem_limit_bytes=8 * 2**20),
        name="finish",
    )(*parts, mean.reshape(1, wide), var.reshape(1, wide))
    return out_mean.reshape(wide), out_var.reshape(wide)


def swap(x, axis, d):
    return lax.ppermute(x, axis, [(i, i ^ d) for i in range(lax.axis_size(axis))])


def local(
    trailing,
    panel_block,
    diag_inverse,
    panel_points,
    lengthscales,
    targets,
    base_a,
    base_b,
    pick_sets,
    cross_rhs,
    mean_in,
    var_in,
):
    n_row, n_col = lax.axis_size("row"), lax.axis_size("col")
    near = n_col in (2, 4)
    parts = partial(panel_block, diag_inverse, n_col, near)
    if near:
        got = [swap(parts[d], "col", d) for d in range(1, n_col)]
    k, sums = columns(panel_points, lengthscales, targets, base_a, base_b, pick_sets, diag_inverse)
    if near:
        got, k, sums = lax.optimization_barrier((got, k, sums))
        reduced = parts[0]
        for x in got:
            reduced = reduced + x.astype(jnp.float32)
        totals = [sums] + [swap(sums, "col", d) for d in range(1, n_col)]
    else:
        reduced = lax.all_to_all(parts[0], "col", 0, 0).astype(jnp.float32).sum(0)
        totals = [lax.psum(sums, "col")]
    reduced = reduced.astype(LINK)
    if n_row == 8:
        even = {0: reduced, **{d: swap(reduced, "row", d) for d in (2, 4, 6)}}
        odd = {d + 1: swap(x, "row", 1) for d, x in even.items()}
        both = {**even, **odd}
        places, blocks = tuple(both), list(both.values())
    else:
        places, blocks = (None,), [lax.all_gather(reduced, "row", axis=0, tiled=True)]
    cross_next, trailing_next = update(blocks, places, k, cross_rhs, panel_block, trailing)
    cross_next, totals = lax.optimization_barrier((cross_next, totals))
    return trailing_next, cross_next, *finish(totals, mean_in, var_in)


def solution(mesh):
    placed = (
        P("row", "col"),
        P("row", None),
        P("col", None),
        P(),
        P(),
        P(),
        P(None, "row"),
        P(None, "row"),
        P("row", None),
        P("col", "row"),
        P("row"),
        P("row"),
    )
    return jax.shard_map(
        local,
        mesh=mesh,
        in_specs=placed,
        out_specs=(P("row", "col"), P("col", "row"), P("row"), P("row")),
        check_vma=False,
    )
```

time: 43 us -> 32.3 us (0.75)
  Pallas kernels: 17.1 us -> 10.7 us
  local copies, waits for them, and re-layouts: 5.94 us -> 0.03 us
  waiting for transfers between devices: 3.77 us -> 6.99 us
  other arithmetic: 1.25 us -> 0.02 us
    unnamed x24 -> x10, local copies, waits for them, and re-layouts: 5.23 us -> 0.03 us
    pallas_call x2 -> x3, Pallas kernels: 13.3 us -> 8.98 us  [the longest x1 5.08 us: columns(): pl.pallas_call(functools.partial(columns_kernel, tile), out_shape=[jax.Sh...]
    ppermute x13, waiting for transfers between devices: 3.77 us -> 6.99 us  [swap(): lax.ppermute(x, axis, [(i, i ^ d) for i in range(lax.axis_size(axis))])]
    pallas_call x1, Pallas kernels: 3.84 us -> 1.71 us  [partial(): pl.pallas_call(functools.partial(partial_kernel, n_col, swapped), out_sha...]
    reshape x1 -> x0, local copies, waits for them, and re-layouts: 0.69 us -> none  [columns(): targets.reshape(1, depth)]
    add x2 -> x0, other arithmetic: 0.63 us -> none  [the longest x1 0.6 us: local(): return (trailing_next, cross_next, mean_in + total[0], var_in - total[1])]
    sub x1 -> x0, other arithmetic: 0.6 us -> none  [local(): return (trailing_next, cross_next, mean_in + total[0], var_in - total[1])]
  transfers between devices with their start and end apart: 13 -> 13, of which waited for: 4 -> 5; matrix products, arithmetic and copies ran while one was open for 5% -> 0% of each run, Pallas kernels for 21% -> 26%
where the time goes in v2:
time: 32.3 us; the launch traced here: 32.1 us
  starting transfers between devices  13.6 us (42%)
  Pallas kernels  10.7 us (33%)
  waiting for transfers between devices  6.99 us (22%)
  between operations  0.76 us (2%)
    ppermute x13, starting transfers between devices, swap(): lax.ppermute(x, axis, [(i, i ^ d) for i in range(lax.axis_size(axis))])  13.6 us
    ppermute x13, waiting for transfers between devices, swap(): lax.ppermute(x, axis, [(i, i ^ d) for i in range(lax.axis_size(axis))])  6.99 us
    pallas_call x1, Pallas kernels, columns(): pl.pallas_call(functools.partial(columns_kernel, tile), out_shape=[jax.Sh...  5.08 us
    pallas_call x1, Pallas kernels, update(): pl.pallas_call(functools.partial(update_kernel, places, tile, len(blocks)...  3.28 us
    pallas_call x1, Pallas kernels, partial(): pl.pallas_call(functools.partial(partial_kernel, n_col, swapped), out_sha...  1.71 us
  transfers between devices with their start and end apart: 13, of which 5 were waited for; matrix products, arithmetic and copies ran while one was open for 0% of the time, Pallas kernels for 26%

profile of v2, /device:TPU:0, one launch (start us, length us, event | category | flops | bytes accessed | tf_op | source)
XLA Modules:
  0.0 32.1 jit_solution(3394639046933280366)
XLA Ops:
  0.6 1.7 %partial.1 = (f32[16,1024]{1,0:T(8,128)S(1)}, f32[16,1024]{1,0:T(8,128)S(1)}, f32[16,1024]{1,0:T(8,128)S(1)}, f32[16,1024]{1,0:T(8,128)S(1)}) custom-call(bf16[64,1024]{1,0:T(8,128)(2,1)} %refs_10_.1, bf16[256,1024]{1,0:T(8,128)(2,1)} %inv_hbm.3), custom_call_target="tpu_custom_call" | custom-call | tf_op jit(solution)/shard_map/partial/pallas_call | solution.py:84
  2.3 0.0 copy-start
  2.4 0.0 copy-start.1
  2.4 0.0 copy-start.2
  2.4 3.1 %collective-permute-start = (f32[16,1024]{1,0:T(8,128)S(1)}, f32[16,1024]{1,0:T(8,128)S(1)}, u32[]{:S(2)}, u32[]{:S(2)}) collective-permute-start(f32[16,1024]{1,0:T(8,128)S(1)} %get-tuple-element.25), channel_id=1, source_target_pairs={{0,1},{1,0},{2,3},{3,2},{4,5},{5,4},{6,7},{7,6},{8,9},{9,8},{10,11... | collective-permute-start | bytes 196616 | tf_op jit(solution)/shard_map/ppermute | solution.py:269
  5.5 2.6 %collective-permute-start.1 = (f32[16,1024]{1,0:T(8,128)S(1)}, f32[16,1024]{1,0:T(8,128)S(1)}, u32[]{:S(2)}, u32[]{:S(2)}) collective-permute-start(f32[16,1024]{1,0:T(8,128)S(1)} %get-tuple-element.26), channel_id=1, source_target_pairs={{0,2},{1,3},{2,0},{3,1},{4,6},{5,7},{6,4},{7,5},{8,10},{9,11},{10,... | collective-permute-start | bytes 196616 | tf_op jit(solution)/shard_map/ppermute | solution.py:269
  8.1 0.0 collective-permute-start.2
  8.1 5.1 %columns.1 = (bf16[1024,3072]{1,0:T(8,128)(2,1)S(1)}, f32[2,3072]{1,0:T(2,128)S(1)}) custom-call(f32[20,1024]{1,0:T(8,128)} %points_hbm.1, f32[1,20]{1,0:T(1,128)} %bitcast.9, bf16[1024]{0:T(1024)(128)(2,1)} %target_hbm.1, s32[12,20]{1,0:T(8,128)} %pick_hbm.1, f32[20,3072]{1,0:T(8,128)} %a_hbm.1, f32[20,3072]{1,0:T(8,128)} %b_hbm.1, bf16[256,1024]{1,0:T(8,128)(2,1)} %inv_hbm.3), custom_call_target="tpu_custom_call" | custom-call | flops 3221225472 | bytes 6291456 | tf_op jit(solution)/shard_map/columns/pallas_call | solution.py:166
  13.2 0.0 copy-start.3
  13.2 0.0 copy-start.4
  13.2 0.0 collective-permute-done
  13.2 0.0 collective-permute-done.1
  13.2 0.9 %collective-permute-done.2 = f32[16,1024]{1,0:T(8,128)S(1)} collective-permute-done((f32[16,1024]{1,0:T(8,128)S(1)}, f32[16,1024]{1,0:T(8,128)S(1)}, u32[]{:S(2)}, u32[]{:S(2)}) %collective-permute-start.2) | collective-permute-done | bytes 65568 | tf_op jit(solution)/shard_map/ppermute | solution.py:269
  14.2 1.6 %collective-permute-start.3 = (f32[16,1024]{1,0:T(8,128)S(1)}, f32[16,1024]{1,0:T(8,128)S(1)}, u32[]{:S(2)}, u32[]{:S(2)}) collective-permute-start(f32[16,1024]{1,0:T(8,128)S(1)} %add_add_fusion.refs_0_), channel_id=1, source_target_pairs={{0,8},{4,12},{8,0},{12,4},{16,24},{20,28},{24,16},{28,20},{1,9},{5... | collective-permute-start | bytes 196616 | tf_op jit(solution)/shard_map/ppermute | solution.py:269
  15.7 1.5 %collective-permute-start.4 = (f32[16,1024]{1,0:T(8,128)S(1)}, f32[16,1024]{1,0:T(8,128)S(1)}, u32[]{:S(2)}, u32[]{:S(2)}) collective-permute-start(f32[16,1024]{1,0:T(8,128)S(1)} %add_add_fusion.refs_0_), channel_id=1, source_target_pairs={{0,16},{4,20},{8,24},{12,28},{16,0},{20,4},{24,8},{28,12},{1,17},{... | collective-permute-start | bytes 196616 | tf_op jit(solution)/shard_map/ppermute | solution.py:269
  17.2 0.5 %collective-permute-start.5 = (f32[16,1024]{1,0:T(8,128)S(1)}, f32[16,1024]{1,0:T(8,128)S(1)}, u32[]{:S(2)}, u32[]{:S(2)}) collective-permute-start(f32[16,1024]{1,0:T(8,128)S(1)} %add_add_fusion.refs_0_), channel_id=1, source_target_pairs={{0,24},{4,28},{8,16},{12,20},{16,8},{20,12},{24,0},{28,4},{1,25},{... | collective-permute-start | bytes 196616 | tf_op jit(solution)/shard_map/ppermute | solution.py:269
  17.7 1.3 %collective-permute-done.3.refs_1_ = f32[16,1024]{1,0:T(8,128)S(1)} collective-permute-done((f32[16,1024]{1,0:T(8,128)S(1)}, f32[16,1024]{1,0:T(8,128)S(1)}, u32[]{:S(2)}, u32[]{:S(2)}) %collective-permute-start.3) | collective-permute-done | bytes 65568 | tf_op jit(solution)/shard_map/ppermute | solution.py:269
  19.0 1.2 %collective-permute-done.4.refs_2_ = f32[16,1024]{1,0:T(8,128)S(1)} collective-permute-done((f32[16,1024]{1,0:T(8,128)S(1)}, f32[16,1024]{1,0:T(8,128)S(1)}, u32[]{:S(2)}, u32[]{:S(2)}) %collective-permute-start.4) | collective-permute-done | bytes 65568 | tf_op jit(solution)/shard_map/ppermute | solution.py:269
  20.2 2.2 %collective-permute-done.5.refs_3_ = f32[16,1024]{1,0:T(8,128)S(1)} collective-permute-done((f32[16,1024]{1,0:T(8,128)S(1)}, f32[16,1024]{1,0:T(8,128)S(1)}, u32[]{:S(2)}, u32[]{:S(2)}) %collective-permute-start.5) | collective-permute-done | bytes 65568 | tf_op jit(solution)/shard_map/ppermute | solution.py:269
  22.4 3.5 %collective-permute-start.11 = (f32[2,3072]{1,0:T(2,128)S(1)}, f32[2,3072]{1,0:T(2,128)S(1)}, u32[]{:S(2)}, u32[]{:S(2)}) collective-permute-start(f32[2,3072]{1,0:T(2,128)S(1)} %get-tuple-element.38.refs_0_), channel_id=1, source_target_pairs={{0,2},{1,3},{2,0},{3,1},{4,6},{5,7},{6,4},{7,5},{8,10},{9,11},{10,... | collective-permute-start | bytes 73736 | tf_op jit(solution)/shard_map/ppermute | solution.py:269
  25.9 0.9 %collective-permute-start.12 = (f32[2,3072]{1,0:T(2,128)S(1)}, f32[2,3072]{1,0:T(2,128)S(1)}, u32[]{:S(2)}, u32[]{:S(2)}) collective-permute-start(f32[2,3072]{1,0:T(2,128)S(1)} %get-tuple-element.38.refs_0_), channel_id=1, source_target_pairs={{0,3},{1,2},{2,1},{3,0},{4,7},{5,6},{6,5},{7,4},{8,11},{9,10},{10,... | collective-permute-start | bytes 73736 | tf_op jit(solution)/shard_map/ppermute | solution.py:269
  26.8 3.3 %update.1 = (bf16[128,3072]{1,0:T(8,128)(2,1)}, f32[64,128]{1,0:T(8,128)}) custom-call(f32[16,1024]{1,0:T(8,128)S(1)} %add_add_fusion.refs_0_, f32[16,1024]{1,0:T(8,128)S(1)} %collective-permute-done.3.refs_1_, f32[16,1024]{1,0:T(8,128)S(1)} %collective-permute-done.4.refs_2_, f32[16,1024]{1,0:T(8,128)S(1)} %collective-permute-done.5.refs_3_, ...), custom_call_target="tpu_custom_call" | custom-call | flops 1610612736 | bytes 6291456 | tf_op jit(solution)/shard_map/update/pallas_call | solution.py:224
  30.1 1.4 %collective-permute-done.12.refs_3_ = f32[2,3072]{1,0:T(2,128)S(1)} collective-permute-done((f32[2,3072]{1,0:T(2,128)S(1)}, f32[2,3072]{1,0:T(2,128)S(1)}, u32[]{:S(2)}, u32[]{:S(2)}) %collective-permute-start.12) | collective-permute-done | bytes 24608 | tf_op jit(solution)/shard_map/ppermute | solution.py:269
  31.5 0.6 %finish.1 = (f32[1,3072]{1,0:T(1,128)}, f32[1,3072]{1,0:T(1,128)}) custom-call(f32[2,3072]{1,0:T(2,128)S(1)} %get-tuple-element.38.refs_0_, f32[2,3072]{1,0:T(2,128)S(1)} %collective-permute-done.10.refs_1_, f32[2,3072]{1,0:T(2,128)S(1)} %collective-permute-done.11.refs_2_, f32[2,3072]{1,0:T(2,128)S(1)} %collective-permute-done.12.refs_3_, ...), custom_call_target="tpu_custom_call" | custom-call | tf_op jit(solution)/shard_map/finish/pallas_call | solution.py:257
  (17 shorter events, 0.1 us)
Async XLA Ops:
  2.3 24.5 %copy-start = (bf16[128,3072]{1,0:T(8,128)(2,1)S(1)}, bf16[128,3072]{1,0:T(8,128)(2,1)}, u32[]{:S(2)}) copy-start(bf16[128,3072]{1,0:T(8,128)(2,1)} %refs_9_.1) | copy-start | bytes 2359300
  2.4 24.5 %copy-start.1 = (bf16[64,1024]{1,0:T(8,128)(2,1)S(1)}, bf16[64,1024]{1,0:T(8,128)(2,1)}, u32[]{:S(2)}) copy-start(bf16[64,1024]{1,0:T(8,128)(2,1)} %refs_10_.1) | copy-start | bytes 393220
  2.4 24.5 %copy-start.2 = (f32[64,128]{1,0:T(8,128)S(1)}, f32[64,128]{1,0:T(8,128)}, u32[]{:S(2)}) copy-start(f32[64,128]{1,0:T(8,128)} %refs_11_.1) | copy-start | bytes 98308
  2.4 10.8 %collective-permute-start = (f32[16,1024]{1,0:T(8,128)S(1)}, f32[16,1024]{1,0:T(8,128)S(1)}, u32[]{:S(2)}, u32[]{:S(2)}) collective-permute-start(f32[16,1024]{1,0:T(8,128)S(1)} %get-tuple-element.25), channel_id=1, source_target_pairs={{0,1},{1,0},{2,3},{3,2},{4,5},{5,4},{6,7},{7,6},{8,9},{9,8},{10,11... | collective-permute-start | bytes 196616 | tf_op jit(solution)/shard_map/ppermute | solution.py:269
  5.5 7.7 %collective-permute-start.1 = (f32[16,1024]{1,0:T(8,128)S(1)}, f32[16,1024]{1,0:T(8,128)S(1)}, u32[]{:S(2)}, u32[]{:S(2)}) collective-permute-start(f32[16,1024]{1,0:T(8,128)S(1)} %get-tuple-element.26), channel_id=1, source_target_pairs={{0,2},{1,3},{2,0},{3,1},{4,6},{5,7},{6,4},{7,5},{8,10},{9,11},{10,... | collective-permute-start | bytes 196616 | tf_op jit(solution)/shard_map/ppermute | solution.py:269
  8.1 6.1 %collective-permute-start.2 = (f32[16,1024]{1,0:T(8,128)S(1)}, f32[16,1024]{1,0:T(8,128)S(1)}, u32[]{:S(2)}, u32[]{:S(2)}) collective-permute-start(f32[16,1024]{1,0:T(8,128)S(1)} %get-tuple-element.27), channel_id=1, source_target_pairs={{0,3},{1,2},{2,1},{3,0},{4,7},{5,6},{6,5},{7,4},{8,11},{9,10},{10,... | collective-permute-start | bytes 196616 | tf_op jit(solution)/shard_map/ppermute | solution.py:269
  13.2 18.3 %copy-start.3 = (f32[3072]{0:T(1024)S(1)}, f32[3072]{0:T(1024)}, u32[]{:S(2)}) copy-start(f32[3072]{0:T(1024)} %param.22) | copy-start | bytes 36868
  13.2 18.3 %copy-start.4 = (f32[3072]{0:T(1024)S(1)}, f32[3072]{0:T(1024)}, u32[]{:S(2)}) copy-start(f32[3072]{0:T(1024)} %param.23) | copy-start | bytes 36868
  14.2 4.8 %collective-permute-start.3 = (f32[16,1024]{1,0:T(8,128)S(1)}, f32[16,1024]{1,0:T(8,128)S(1)}, u32[]{:S(2)}, u32[]{:S(2)}) collective-permute-start(f32[16,1024]{1,0:T(8,128)S(1)} %add_add_fusion.refs_0_), channel_id=1, source_target_pairs={{0,8},{4,12},{8,0},{12,4},{16,24},{20,28},{24,16},{28,20},{1,9},{5... | collective-permute-start | bytes 196616 | tf_op jit(solution)/shard_map/ppermute | solution.py:269
  15.7 4.5 %collective-permute-start.4 = (f32[16,1024]{1,0:T(8,128)S(1)}, f32[16,1024]{1,0:T(8,128)S(1)}, u32[]{:S(2)}, u32[]{:S(2)}) collective-permute-start(f32[16,1024]{1,0:T(8,128)S(1)} %add_add_fusion.refs_0_), channel_id=1, source_target_pairs={{0,16},{4,20},{8,24},{12,28},{16,0},{20,4},{24,8},{28,12},{1,17},{... | collective-permute-start | bytes 196616 | tf_op jit(solution)/shard_map/ppermute | solution.py:269
  17.2 5.2 %collective-permute-start.5 = (f32[16,1024]{1,0:T(8,128)S(1)}, f32[16,1024]{1,0:T(8,128)S(1)}, u32[]{:S(2)}, u32[]{:S(2)}) collective-permute-start(f32[16,1024]{1,0:T(8,128)S(1)} %add_add_fusion.refs_0_), channel_id=1, source_target_pairs={{0,24},{4,28},{8,16},{12,20},{16,8},{20,12},{24,0},{28,4},{1,25},{... | collective-permute-start | bytes 196616 | tf_op jit(solution)/shard_map/ppermute | solution.py:269
  17.7 4.7 %collective-permute-start.6 = (f32[16,1024]{1,0:T(8,128)S(1)}, f32[16,1024]{1,0:T(8,128)S(1)}, u32[]{:S(2)}, u32[]{:S(2)}) collective-permute-start(f32[16,1024]{1,0:T(8,128)S(1)} %add_add_fusion.refs_0_), channel_id=1, source_target_pairs={{0,4},{4,0},{8,12},{12,8},{16,20},{20,16},{24,28},{28,24},{1,5},{5... | collective-permute-start | bytes 196616 | tf_op jit(solution)/shard_map/ppermute | solution.py:269
  19.0 6.9 %collective-permute-start.7 = (f32[16,1024]{1,0:T(8,128)S(1)}, f32[16,1024]{1,0:T(8,128)S(1)}, u32[]{:S(2)}, u32[]{:S(2)}) collective-permute-start(f32[16,1024]{1,0:T(8,128)S(1)} %collective-permute-done.3.refs_1_), channel_id=1, source_target_pairs={{0,4},{4,0},{8,12},{12,8},{16,20},{20,16},{24,28},{28,24},{1,5},{5... | collective-permute-start | bytes 196616 | tf_op jit(solution)/shard_map/ppermute | solution.py:269
  20.2 6.6 %collective-permute-start.8 = (f32[16,1024]{1,0:T(8,128)S(1)}, f32[16,1024]{1,0:T(8,128)S(1)}, u32[]{:S(2)}, u32[]{:S(2)}) collective-permute-start(f32[16,1024]{1,0:T(8,128)S(1)} %collective-permute-done.4.refs_2_), channel_id=1, source_target_pairs={{0,4},{4,0},{8,12},{12,8},{16,20},{20,16},{24,28},{28,24},{1,5},{5... | collective-permute-start | bytes 196616 | tf_op jit(solution)/shard_map/ppermute | solution.py:269
  22.4 4.4 %collective-permute-start.9 = (f32[16,1024]{1,0:T(8,128)S(1)}, f32[16,1024]{1,0:T(8,128)S(1)}, u32[]{:S(2)}, u32[]{:S(2)}) collective-permute-start(f32[16,1024]{1,0:T(8,128)S(1)} %collective-permute-done.5.refs_3_), channel_id=1, source_target_pairs={{0,4},{4,0},{8,12},{12,8},{16,20},{20,16},{24,28},{28,24},{1,5},{5... | collective-permute-start | bytes 196616 | tf_op jit(solution)/shard_map/ppermute | solution.py:269
  22.4 7.7 %collective-permute-start.10 = (f32[2,3072]{1,0:T(2,128)S(1)}, f32[2,3072]{1,0:T(2,128)S(1)}, u32[]{:S(2)}, u32[]{:S(2)}) collective-permute-start(f32[2,3072]{1,0:T(2,128)S(1)} %get-tuple-element.38.refs_0_), channel_id=1, source_target_pairs={{0,1},{1,0},{2,3},{3,2},{4,5},{5,4},{6,7},{7,6},{8,9},{9,8},{10,11... | collective-permute-start | bytes 73736 | tf_op jit(solution)/shard_map/ppermute | solution.py:269
  22.4 7.7 %collective-permute-start.11 = (f32[2,3072]{1,0:T(2,128)S(1)}, f32[2,3072]{1,0:T(2,128)S(1)}, u32[]{:S(2)}, u32[]{:S(2)}) collective-permute-start(f32[2,3072]{1,0:T(2,128)S(1)} %get-tuple-element.38.refs_0_), channel_id=1, source_target_pairs={{0,2},{1,3},{2,0},{3,1},{4,6},{5,7},{6,4},{7,5},{8,10},{9,11},{10,... | collective-permute-start | bytes 73736 | tf_op jit(solution)/shard_map/ppermute | solution.py:269
  25.9 5.6 %collective-permute-start.12 = (f32[2,3072]{1,0:T(2,128)S(1)}, f32[2,3072]{1,0:T(2,128)S(1)}, u32[]{:S(2)}, u32[]{:S(2)}) collective-permute-start(f32[2,3072]{1,0:T(2,128)S(1)} %get-tuple-element.38.refs_0_), channel_id=1, source_target_pairs={{0,3},{1,2},{2,1},{3,0},{4,7},{5,6},{6,5},{7,4},{8,11},{9,10},{10,... | collective-permute-start | bytes 73736 | tf_op jit(solution)/shard_map/ppermute | solution.py:269

commit v3 on v2

--- a/solution.py
+++ b/solution.py
@@ -9,7 +9,7 @@
 
 GROUP = 32
 DEPTH = 8 * GROUP
-LINK = jnp.float32
+LINK = jnp.bfloat16
 VMEM = pl.BlockSpec(memory_space=pltpu.VMEM)
 HBM = pl.BlockSpec(memory_space=pltpu.HBM)
 
@@ -53,12 +53,14 @@
     return out
 
 
-def partial_kernel(n_col, swapped, panel_hbm, inv_hbm, *refs):
-    out_refs, (panel_ref, inv_ref, sems) = refs[:-3], refs[-3:]
-    copies = fetch((panel_hbm, inv_hbm), (panel_ref, inv_ref), sems)
+def partial_kernel(n_col, swapped, n_more, *refs):
+    sources, refs = refs[: 2 + n_more], refs[2 + n_more :]
+    more, out_refs, (panel_ref, sems) = refs[: n_more + 1], refs[n_more + 1 : -2], refs[-2:]
+    inv_ref = more[0]
+    copies = fetch(sources, (panel_ref, *more), sems)
     rows = panel_ref.shape[0] // n_col
     me = lax.axis_index("col")
-    for c in copies:
+    for c in copies[:2]:
         c.wait()
     inv = inv_ref[...]
     panel = panel_ref[...]
@@ -73,44 +75,39 @@
             out_refs[d][...] = part[d * rows : (d + 1) * rows].astype(out_refs[d].dtype)
     else:
         out_refs[0][...] = part.reshape(out_refs[0].shape).astype(out_refs[0].dtype)
-
-
-def partial(panel, inv, n_col, swapped):
+    for c in copies[2:]:
+        c.wait()
+
+
+def partial(panel, inv, more, n_col, swapped):
     rows, width = panel.shape[0] // n_col, panel.shape[1]
+    shapes = [jax.ShapeDtypeStruct(x.shape, x.dtype) for x in (inv, *more)]
     if swapped:
-        shapes = [jax.ShapeDtypeStruct((rows, width), jnp.float32 if d == 0 else LINK) for d in range(n_col)]
+        shapes += [jax.ShapeDtypeStruct((rows, width), jnp.float32 if d == 0 else LINK) for d in range(n_col)]
     else:
-        shapes = [jax.ShapeDtypeStruct((n_col, rows, width), LINK)]
-    return pl.pallas_call(
-        functools.partial(partial_kernel, n_col, swapped),
+        shapes += [jax.ShapeDtypeStruct((n_col, rows, width), LINK)]
+    out = pl.pallas_call(
+        functools.partial(partial_kernel, n_col, swapped, len(more)),
         out_shape=shapes,
-        in_specs=[HBM] * 2,
+        in_specs=[HBM] * (2 + len(more)),
         out_specs=[VMEM] * len(shapes),
-        scratch_shapes=[pltpu.VMEM(x.shape, x.dtype) for x in (panel, inv)] + [pltpu.SemaphoreType.DMA((2,))],
+        scratch_shapes=[pltpu.VMEM(panel.shape, panel.dtype), pltpu.SemaphoreType.DMA((2 + len(more),))],
         compiler_params=pltpu.CompilerParams(vmem_limit_bytes=16 * 2**20),
         name="partial",
-    )(*in_hbm(panel, inv))
+    )(*in_hbm(panel, inv, *more))
+    return out[: 1 + len(more)], out[1 + len(more) :]
 
 
 def columns_kernel(
-    tile, points_hbm, scale_hbm, target_hbm, pick_hbm, a_hbm, b_hbm, inv_hbm,
-    k_ref, sums_ref,
-    points_ref, scale_ref, target_ref, pick_ref, a_ref, b_ref, inv_ref,
-    p32, pwide, pt, s32, st, sems,
+    tile, inv_ref, points_ref, scale_ref, target_ref, pick_ref, a_ref, b_ref,
+    k_ref, sums_ref, p32, pwide, pt, s32, st,
 ):
-    copies = fetch(
-        (points_hbm, scale_hbm, pick_hbm, a_hbm, b_hbm, inv_hbm, target_hbm),
-        (points_ref, scale_ref, pick_ref, a_ref, b_ref, inv_ref, target_ref),
-        sems,
-    )
     din, depth = points_ref.shape
     wide = a_ref.shape[1]
     block = wide // pick_ref.shape[0]
     p32[...] = jnp.zeros_like(p32)
     s32[...] = jnp.zeros_like(s32)
     st[...] = jnp.zeros_like(st)
-    for c in copies[:2]:
-        c.wait()
     inverse = 1.0 / column(scale_ref[...])
     p32[:din, :] = (points_ref[...] - 0.5) * inverse
     p = p32[...]
@@ -122,8 +119,6 @@
     pwide[6 * GROUP : 7 * GROUP, :] = pick_row((GROUP, depth), (minus, minus, minus) + split3(norm))
     pwide[7 * GROUP :, :] = jnp.zeros((GROUP, depth), jnp.float32)
     pt[...] = jnp.transpose(pwide[...]).astype(jnp.bfloat16)
-    for c in copies[2:]:
-        c.wait()
     weight = (
         jnp.sum(inv_ref[...].astype(jnp.float32) * target_ref[...].astype(jnp.float32).reshape(1, depth), axis=1, keepdims=True)
         .astype(jnp.bfloat16)
@@ -157,35 +152,31 @@
     lax.fori_loop(0, wide // tile, step, 0, unroll=True)
 
 
-def columns(points, scales, targets, base_a, base_b, picks, inv):
-    din, depth = points.shape
-    wide = base_a.shape[1]
-    blocks = picks.shape[0]
+def columns(ins):
+    inv, points, _, _, picks, base, _ = ins
+    depth, wide, blocks = points.shape[1], base.shape[1], picks.shape[0]
     tile = wide // blocks * (2 if blocks % 2 == 0 else 1)
-    ins = (points, scales.reshape(1, din), targets, picks, base_a, base_b, inv)
     return pl.pallas_call(
         functools.partial(columns_kernel, tile),
         out_shape=[
             jax.ShapeDtypeStruct((depth, wide), jnp.bfloat16),
             jax.ShapeDtypeStruct((2, wide), jnp.float32),
         ],
-        in_specs=[HBM] * len(ins),
+        in_specs=[VMEM] * len(ins),
         out_specs=[VMEM] * 2,
-        scratch_shapes=[pltpu.VMEM(x.shape, x.dtype) for x in ins]
-        + [
+        scratch_shapes=[
             pltpu.VMEM((GROUP, depth), jnp.float32),
             pltpu.VMEM((DEPTH, depth), jnp.float32),
             pltpu.VMEM((depth, DEPTH), jnp.bfloat16),
             pltpu.VMEM((GROUP, tile), jnp.float32),
             pltpu.VMEM((DEPTH, tile), jnp.bfloat16),
-            pltpu.SemaphoreType.DMA((len(ins),)),
         ],
         compiler_params=pltpu.CompilerParams(vmem_limit_bytes=32 * 2**20),
         cost_estimate=pl.CostEstimate(
             flops=2 * depth * wide * (DEPTH + inv.shape[0]), bytes_accessed=2 * depth * wide, transcendentals=depth * wide
         ),
         name="columns",
-    )(*in_hbm(*ins))
+    )(*ins)
 
 
 def update_kernel(places, tile, n_in, *refs):
@@ -194,25 +185,21 @@
     rows, wide = rhs_ref.shape
     me = lax.axis_index("row")
     for ref, place in zip(blocks, places):
-        height = ref.shape[0]
-        start = 0 if place is None else (me ^ place) * height
-        full = ref[...].astype(jnp.float32)
-        high = full.astype(jnp.bfloat16)
-        left[pl.ds(start, height), :] = high
-        left[pl.ds(start + rows, height), :] = (full - high.astype(jnp.float32)).astype(jnp.bfloat16)
+        height = ref.shape[0] // len(place)
+        for i, xor in enumerate(place):
+            start = 0 if xor is None else (me ^ xor) * height
+            left[pl.ds(start, height), :] = ref[i * height : (i + 1) * height, :]
     copies = []
     for t in range(wide // tile):
         here = slice(t * tile, (t + 1) * tile)
         product = jnp.dot(left[...], k_ref[:, here], preferred_element_type=jnp.float32)
-        cross[:, here] = (
-            rhs_ref[:, here].astype(jnp.float32) - (product[:rows] + product[rows:])
-        ).astype(cross.dtype)
+        cross[:, here] = (rhs_ref[:, here].astype(jnp.float32) - product).astype(cross.dtype)
         copies.append(pltpu.make_async_copy(cross.at[:, here], cross_hbm.at[:, here], sems.at[t]))
         copies[-1].start()
     product = lax.dot_general(
         panel_ref[...], left[...], (((1,), (1,)), ((), ())), preferred_element_type=jnp.float32
     )
-    next_ref[...] = trailing_ref[...] - (product[:, :rows] + product[:, rows:])
+    next_ref[...] = trailing_ref[...] - product
     for c in copies:
         c.wait()
 
@@ -230,13 +217,13 @@
         in_specs=[VMEM] * (len(blocks) + 4),
         out_specs=[HBM, VMEM],
         scratch_shapes=[
-            pltpu.VMEM((2 * rows, depth), jnp.bfloat16),
+            pltpu.VMEM((rows, depth), jnp.bfloat16),
             pltpu.VMEM(rhs.shape, rhs.dtype),
             pltpu.SemaphoreType.DMA((wide // tile,)),
         ],
         compiler_params=pltpu.CompilerParams(vmem_limit_bytes=32 * 2**20),
         cost_estimate=pl.CostEstimate(
-            flops=4 * rows * depth * wide, bytes_accessed=2 * depth * wide, transcendentals=0
+            flops=2 * rows * depth * wide, bytes_accessed=2 * depth * wide, transcendentals=0
         ),
         name="update",
     )(*blocks, k, rhs, panel, trailing)
@@ -285,10 +272,11 @@
 ):
     n_row, n_col = lax.axis_size("row"), lax.axis_size("col")
     near = n_col in (2, 4)
-    parts = partial(panel_block, diag_inverse, n_col, near)
+    more = (panel_points, lengthscales.reshape(1, -1), targets, pick_sets, base_a, base_b)
+    ins, parts = partial(panel_block, diag_inverse, more, n_col, near)
     if near:
         got = [swap(parts[d], "col", d) for d in range(1, n_col)]
-    k, sums = columns(panel_points, lengthscales, targets, base_a, base_b, pick_sets, diag_inverse)
+    k, sums = columns(ins)
     if near:
         got, k, sums = lax.optimization_barrier((got, k, sums))
         reduced = parts[0]
@@ -300,12 +288,11 @@
         totals = [lax.psum(sums, "col")]
     reduced = reduced.astype(LINK)
     if n_row == 8:
-        even = {0: reduced, **{d: swap(reduced, "row", d) for d in (2, 4, 6)}}
-        odd = {d + 1: swap(x, "row", 1) for d, x in even.items()}
-        both = {**even, **odd}
-        places, blocks = tuple(both), list(both.values())
+        pair = jnp.concatenate([reduced, swap(reduced, "row", 1)], axis=0)
+        blocks = [pair] + [swap(pair, "row", d) for d in (2, 4, 6)]
+        places = [(d, d + 1) for d in (0, 2, 4, 6)]
     else:
-        places, blocks = (None,), [lax.all_gather(reduced, "row", axis=0, tiled=True)]
+        blocks, places = [lax.all_gather(reduced, "row", axis=0, tiled=True)], [(None,)]
     cross_next, trailing_next = update(blocks, places, k, cross_rhs, panel_block, trailing)
     cross_next, totals = lax.optimization_barrier((cross_next, totals))
     return trailing_next, cross_next, *finish(totals, mean_in, var_in)

time: 32.3 us -> 26.3 us (0.81)
  waiting for transfers between devices: 6.99 us -> 2.96 us
  Pallas kernels: 10.7 us -> 8.75 us
    ppermute x13 -> x10, waiting for transfers between devices: 6.99 us -> 2.96 us  [swap(): lax.ppermute(x, axis, [(i, i ^ d) for i in range(lax.axis_size(axis))])]
    pallas_call x1, Pallas kernels: 5.08 us -> 3.91 us  [columns(): pl.pallas_call(functools.partial(columns_kernel, tile), out_shape=[jax.Sh...]
    pallas_call x1, Pallas kernels: 3.28 us -> 2.45 us  [update(): pl.pallas_call(functools.partial(update_kernel, places, tile, len(blocks)...]
    ppermute x13 -> x10, starting transfers between devices: 13.6 us -> 13.6 us  [swap(): lax.ppermute(x, axis, [(i, i ^ d) for i in range(lax.axis_size(axis))])]
  transfers between devices with their start and end apart: 13 -> 10, of which waited for: 5 -> 2; matrix products, arithmetic and copies ran while one was open for 0% -> 0% of each run, Pallas kernels for 26% -> 24%
where the time goes in v3:
time: 26.3 us; the launch traced here: 26.2 us
  starting transfers between devices  13.6 us (52%)
  Pallas kernels  8.75 us (33%)
  waiting for transfers between devices  2.96 us (11%)
  between operations  0.79 us (3%)
    ppermute x10, starting transfers between devices, swap(): lax.ppermute(x, axis, [(i, i ^ d) for i in range(lax.axis_size(axis))])  13.6 us
    pallas_call x1, Pallas kernels, columns(): pl.pallas_call(functools.partial(columns_kernel, tile), out_shape=[jax.Sh...  3.91 us
    ppermute x10, waiting for transfers between devices, swap(): lax.ppermute(x, axis, [(i, i ^ d) for i in range(lax.axis_size(axis))])  2.96 us
    pallas_call x1, Pallas kernels, update(): pl.pallas_call(functools.partial(update_kernel, places, tile, len(blocks)...  2.45 us
    pallas_call x1, Pallas kernels, partial(): pl.pallas_call(functools.partial(partial_kernel, n_col, swapped, len(more...  1.78 us
    pallas_call x1, Pallas kernels, finish(): pl.pallas_call(finish_kernel, out_shape=[flat, flat], in_specs=[VMEM] * (...  0.62 us
  transfers between devices with their start and end apart: 10, of which 2 were waited for; matrix products, arithmetic and copies ran while one was open for 0% of the time, Pallas kernels for 24%

profile of v3, /device:TPU:0, one launch (start us, length us, event | category | flops | bytes accessed | tf_op | source)
XLA Modules:
  0.0 26.2 jit_solution(13304264070077482632)
XLA Ops:
  0.6 1.8 %partial.1 = (bf16[256,1024]{1,0:T(8,128)(2,1)S(1)}, f32[20,1024]{1,0:T(8,128)S(1)}, f32[1,20]{1,0:T(1,128)S(1)}, bf16[1024]{0:T(1024)(128)(2,1)S(1)}, s32[12,20...) custom-call(bf16[64,1024]{1,0:T(8,128)(2,1)} %refs_6_.3, ...), custom_call_target="tpu_custom_call" | custom-call | tf_op jit(solution)/shard_map/partial/pallas_call | solution.py:89
  2.4 0.0 copy-start
  2.4 0.0 copy-start.1
  2.4 0.0 copy-start.2
  2.5 3.1 %collective-permute-start = (bf16[16,1024]{1,0:T(8,128)(2,1)S(1)}, bf16[16,1024]{1,0:T(8,128)(2,1)S(1)}, u32[]{:S(2)}, u32[]{:S(2)}) collective-permute-start(bf16[16,1024]{1,0:T(8,128)(2,1)S(1)} %get-tuple-element.32), channel_id=1, source_target_pairs={{0,1},{1,0},{2,3},{3,2},{4,5},{5,4},{6,7},{7,6},{8,9},{9,8},{10,11... | collective-permute-start | bytes 98312 | tf_op jit(solution)/shard_map/ppermute | solution.py:256
  5.5 2.6 %collective-permute-start.1 = (bf16[16,1024]{1,0:T(8,128)(2,1)S(1)}, bf16[16,1024]{1,0:T(8,128)(2,1)S(1)}, u32[]{:S(2)}, u32[]{:S(2)}) collective-permute-start(bf16[16,1024]{1,0:T(8,128)(2,1)S(1)} %get-tuple-element.33), channel_id=1, source_target_pairs={{0,2},{1,3},{2,0},{3,1},{4,6},{5,7},{6,4},{7,5},{8,10},{9,11},{10,... | collective-permute-start | bytes 98312 | tf_op jit(solution)/shard_map/ppermute | solution.py:256
  8.1 3.9 %columns.1 = (bf16[1024,3072]{1,0:T(8,128)(2,1)S(1)}, f32[2,3072]{1,0:T(2,128)S(1)}) custom-call(bf16[256,1024]{1,0:T(8,128)(2,1)S(1)} %get-tuple-element.35.inv_ref, f32[20,1024]{1,0:T(8,128)S(1)} %get-tuple-element.36.points_ref, f32[1,20]{1,0:T(1,128)S(1)} %get-tuple-element.37.scale_ref, bf16[1024]{0:T(1024)(128)(2,1)S(1)} %get-tuple-element.38.target_ref, ...), custom_call_target="tpu_custom_call" | custom-call | flops 3221225472 | bytes 6291456 | tf_op jit(solution)/shard_map/columns/pallas_call | solution.py:159
  12.1 0.0 copy-start.3
  12.1 0.0 copy-start.4
  12.1 0.0 collective-permute-done
  12.1 1.7 %collective-permute-done.2 = bf16[16,1024]{1,0:T(8,128)(2,1)S(1)} collective-permute-done((bf16[16,1024]{1,0:T(8,128)(2,1)S(1)}, bf16[16,1024]{1,0:T(8,128)(2,1)S(1)}, u32[]{:S(2)}, u32[]{:S(2)}) %collective-permute-start.2) | collective-permute-done | bytes 32800 | tf_op jit(solution)/shard_map/ppermute | solution.py:256
  13.9 0.1 collective-permute-start.3
  14.0 1.2 %collective-permute-done.3 = bf16[16,1024]{1,0:T(8,128)(2,1)S(1)} collective-permute-done((bf16[16,1024]{1,0:T(8,128)(2,1)S(1)}, bf16[16,1024]{1,0:T(8,128)(2,1)S(1)}, u32[]{:S(2)}, u32[]{:S(2)}) %collective-permute-start.3) | collective-permute-done | bytes 32800 | tf_op jit(solution)/shard_map/ppermute | solution.py:256
  15.2 2.4 %collective-permute-start.6 = (bf16[32,1024]{1,0:T(8,128)(2,1)S(1)}, bf16[32,1024]{1,0:T(8,128)(2,1)S(1)}, u32[]{:S(2)}, u32[]{:S(2)}) collective-permute-start(bf16[32,1024]{1,0:T(8,128)(2,1)S(1)} %pad_maximum_fusion.refs_0_), channel_id=1, source_target_pairs={{0,24},{4,28},{8,16},{12,20},{16,8},{20,12},{24,0},{28,4},{1,25},{... | collective-permute-start | bytes 196616 | tf_op jit(solution)/shard_map/ppermute | solution.py:256
  17.6 0.5 %collective-permute-start.5 = (bf16[32,1024]{1,0:T(8,128)(2,1)S(1)}, bf16[32,1024]{1,0:T(8,128)(2,1)S(1)}, u32[]{:S(2)}, u32[]{:S(2)}) collective-permute-start(bf16[32,1024]{1,0:T(8,128)(2,1)S(1)} %pad_maximum_fusion.refs_0_), channel_id=1, source_target_pairs={{0,16},{4,20},{8,24},{12,28},{16,0},{20,4},{24,8},{28,12},{1,17},{... | collective-permute-start | bytes 196616 | tf_op jit(solution)/shard_map/ppermute | solution.py:256
  18.1 0.5 %collective-permute-start.4 = (bf16[32,1024]{1,0:T(8,128)(2,1)S(1)}, bf16[32,1024]{1,0:T(8,128)(2,1)S(1)}, u32[]{:S(2)}, u32[]{:S(2)}) collective-permute-start(bf16[32,1024]{1,0:T(8,128)(2,1)S(1)} %pad_maximum_fusion.refs_0_), channel_id=1, source_target_pairs={{0,8},{4,12},{8,0},{12,4},{16,24},{20,28},{24,16},{28,20},{1,9},{5... | collective-permute-start | bytes 196616 | tf_op jit(solution)/shard_map/ppermute | solution.py:256
  18.6 2.1 %collective-permute-start.9 = (f32[2,3072]{1,0:T(2,128)S(1)}, f32[2,3072]{1,0:T(2,128)S(1)}, u32[]{:S(2)}, u32[]{:S(2)}) collective-permute-start(f32[2,3072]{1,0:T(2,128)S(1)} %get-tuple-element.52.refs_0_), channel_id=1, source_target_pairs={{0,3},{1,2},{2,1},{3,0},{4,7},{5,6},{6,5},{7,4},{8,11},{9,10},{10,... | collective-permute-start | bytes 73736 | tf_op jit(solution)/shard_map/ppermute | solution.py:256
  20.7 0.0 collective-permute-start.8
  20.7 0.0 collective-permute-done.6.refs_3_
  20.7 2.3 %collective-permute-start.7 = (f32[2,3072]{1,0:T(2,128)S(1)}, f32[2,3072]{1,0:T(2,128)S(1)}, u32[]{:S(2)}, u32[]{:S(2)}) collective-permute-start(f32[2,3072]{1,0:T(2,128)S(1)} %get-tuple-element.52.refs_0_), channel_id=1, source_target_pairs={{0,1},{1,0},{2,3},{3,2},{4,5},{5,4},{6,7},{7,6},{8,9},{9,8},{10,11... | collective-permute-start | bytes 73736 | tf_op jit(solution)/shard_map/ppermute | solution.py:256
  23.0 0.0 collective-permute-done.5.refs_2_
  23.0 0.0 collective-permute-done.4.refs_1_
  23.1 2.4 %update.1 = (bf16[128,3072]{1,0:T(8,128)(2,1)}, f32[64,128]{1,0:T(8,128)}) custom-call(bf16[32,1024]{1,0:T(8,128)(2,1)S(1)} %pad_maximum_fusion.refs_0_, bf16[32,1024]{1,0:T(8,128)(2,1)S(1)} %collective-permute-done.4.refs_1_, bf16[32,1024]{1,0:T(8,128)(2,1)S(1)} %collective-permute-done.5.refs_2_, bf16[32,1024]{1,0:T(8,128)(2,1)S(1)} %collective-permute-done.6.refs_3_, ...), custom_call_target="tpu_custom_call" | custom-call | flops 805306368 | bytes 6291456 | tf_op jit(solution)/shard_map/update/pallas_call | solution.py:211
  25.6 0.6 %finish.1 = (f32[1,3072]{1,0:T(1,128)}, f32[1,3072]{1,0:T(1,128)}) custom-call(f32[2,3072]{1,0:T(2,128)S(1)} %get-tuple-element.52.refs_0_, f32[2,3072]{1,0:T(2,128)S(1)} %collective-permute-done.7.refs_1_, f32[2,3072]{1,0:T(2,128)S(1)} %collective-permute-done.8.refs_2_, f32[2,3072]{1,0:T(2,128)S(1)} %collective-permute-done.9.refs_3_, ...), custom_call_target="tpu_custom_call" | custom-call | tf_op jit(solution)/shard_map/finish/pallas_call | solution.py:244
  (12 shorter events, 0.0 us)
Async XLA Ops:
  2.4 20.6 %copy-start = (bf16[128,3072]{1,0:T(8,128)(2,1)S(1)}, bf16[128,3072]{1,0:T(8,128)(2,1)}, u32[]{:S(2)}) copy-start(bf16[128,3072]{1,0:T(8,128)(2,1)} %refs_5_.3) | copy-start | bytes 2359300
  2.4 20.6 %copy-start.1 = (bf16[64,1024]{1,0:T(8,128)(2,1)S(1)}, bf16[64,1024]{1,0:T(8,128)(2,1)}, u32[]{:S(2)}) copy-start(bf16[64,1024]{1,0:T(8,128)(2,1)} %refs_6_.3) | copy-start | bytes 393220
  2.4 20.6 %copy-start.2 = (f32[64,128]{1,0:T(8,128)S(1)}, f32[64,128]{1,0:T(8,128)}, u32[]{:S(2)}) copy-start(f32[64,128]{1,0:T(8,128)} %refs_7_.3) | copy-start | bytes 98308
  2.5 9.6 %collective-permute-start = (bf16[16,1024]{1,0:T(8,128)(2,1)S(1)}, bf16[16,1024]{1,0:T(8,128)(2,1)S(1)}, u32[]{:S(2)}, u32[]{:S(2)}) collective-permute-start(bf16[16,1024]{1,0:T(8,128)(2,1)S(1)} %get-tuple-element.32), channel_id=1, source_target_pairs={{0,1},{1,0},{2,3},{3,2},{4,5},{5,4},{6,7},{7,6},{8,9},{9,8},{10,11... | collective-permute-start | bytes 98312 | tf_op jit(solution)/shard_map/ppermute | solution.py:256
  5.5 6.5 %collective-permute-start.1 = (bf16[16,1024]{1,0:T(8,128)(2,1)S(1)}, bf16[16,1024]{1,0:T(8,128)(2,1)S(1)}, u32[]{:S(2)}, u32[]{:S(2)}) collective-permute-start(bf16[16,1024]{1,0:T(8,128)(2,1)S(1)} %get-tuple-element.33), channel_id=1, source_target_pairs={{0,2},{1,3},{2,0},{3,1},{4,6},{5,7},{6,4},{7,5},{8,10},{9,11},{10,... | collective-permute-start | bytes 98312 | tf_op jit(solution)/shard_map/ppermute | solution.py:256
  8.1 5.7 %collective-permute-start.2 = (bf16[16,1024]{1,0:T(8,128)(2,1)S(1)}, bf16[16,1024]{1,0:T(8,128)(2,1)S(1)}, u32[]{:S(2)}, u32[]{:S(2)}) collective-permute-start(bf16[16,1024]{1,0:T(8,128)(2,1)S(1)} %get-tuple-element.34), channel_id=1, source_target_pairs={{0,3},{1,2},{2,1},{3,0},{4,7},{5,6},{6,5},{7,4},{8,11},{9,10},{10,... | collective-permute-start | bytes 98312 | tf_op jit(solution)/shard_map/ppermute | solution.py:256
  12.1 13.5 %copy-start.3 = (f32[3072]{0:T(1024)S(1)}, f32[3072]{0:T(1024)}, u32[]{:S(2)}) copy-start(f32[3072]{0:T(1024)} %param.22) | copy-start | bytes 36868
  12.1 13.5 %copy-start.4 = (f32[3072]{0:T(1024)S(1)}, f32[3072]{0:T(1024)}, u32[]{:S(2)}) copy-start(f32[3072]{0:T(1024)} %param.23) | copy-start | bytes 36868
  13.9 1.3 %collective-permute-start.3 = (bf16[16,1024]{1,0:T(8,128)(2,1)S(1)}, bf16[16,1024]{1,0:T(8,128)(2,1)S(1)}, u32[]{:S(2)}, u32[]{:S(2)}) collective-permute-start(bf16[16,1024]{1,0:T(8,128)(2,1)S(1)} %add_convert_fusion), channel_id=1, source_target_pairs={{0,4},{4,0},{8,12},{12,8},{16,20},{20,16},{24,28},{28,24},{1,5},{5... | collective-permute-start | bytes 98312 | tf_op jit(solution)/shard_map/ppermute | solution.py:256
  15.2 5.6 %collective-permute-start.6 = (bf16[32,1024]{1,0:T(8,128)(2,1)S(1)}, bf16[32,1024]{1,0:T(8,128)(2,1)S(1)}, u32[]{:S(2)}, u32[]{:S(2)}) collective-permute-start(bf16[32,1024]{1,0:T(8,128)(2,1)S(1)} %pad_maximum_fusion.refs_0_), channel_id=1, source_target_pairs={{0,24},{4,28},{8,16},{12,20},{16,8},{20,12},{24,0},{28,4},{1,25},{... | collective-permute-start | bytes 196616 | tf_op jit(solution)/shard_map/ppermute | solution.py:256
  17.6 5.4 %collective-permute-start.5 = (bf16[32,1024]{1,0:T(8,128)(2,1)S(1)}, bf16[32,1024]{1,0:T(8,128)(2,1)S(1)}, u32[]{:S(2)}, u32[]{:S(2)}) collective-permute-start(bf16[32,1024]{1,0:T(8,128)(2,1)S(1)} %pad_maximum_fusion.refs_0_), channel_id=1, source_target_pairs={{0,16},{4,20},{8,24},{12,28},{16,0},{20,4},{24,8},{28,12},{1,17},{... | collective-permute-start | bytes 196616 | tf_op jit(solution)/shard_map/ppermute | solution.py:256
  18.1 4.9 %collective-permute-start.4 = (bf16[32,1024]{1,0:T(8,128)(2,1)S(1)}, bf16[32,1024]{1,0:T(8,128)(2,1)S(1)}, u32[]{:S(2)}, u32[]{:S(2)}) collective-permute-start(bf16[32,1024]{1,0:T(8,128)(2,1)S(1)} %pad_maximum_fusion.refs_0_), channel_id=1, source_target_pairs={{0,8},{4,12},{8,0},{12,4},{16,24},{20,28},{24,16},{28,20},{1,9},{5... | collective-permute-start | bytes 196616 | tf_op jit(solution)/shard_map/ppermute | solution.py:256
  18.6 6.9 %collective-permute-start.9 = (f32[2,3072]{1,0:T(2,128)S(1)}, f32[2,3072]{1,0:T(2,128)S(1)}, u32[]{:S(2)}, u32[]{:S(2)}) collective-permute-start(f32[2,3072]{1,0:T(2,128)S(1)} %get-tuple-element.52.refs_0_), channel_id=1, source_target_pairs={{0,3},{1,2},{2,1},{3,0},{4,7},{5,6},{6,5},{7,4},{8,11},{9,10},{10,... | collective-permute-start | bytes 73736 | tf_op jit(solution)/shard_map/ppermute | solution.py:256
  20.7 4.8 %collective-permute-start.8 = (f32[2,3072]{1,0:T(2,128)S(1)}, f32[2,3072]{1,0:T(2,128)S(1)}, u32[]{:S(2)}, u32[]{:S(2)}) collective-permute-start(f32[2,3072]{1,0:T(2,128)S(1)} %get-tuple-element.52.refs_0_), channel_id=1, source_target_pairs={{0,2},{1,3},{2,0},{3,1},{4,6},{5,7},{6,4},{7,5},{8,10},{9,11},{10,... | collective-permute-start | bytes 73736 | tf_op jit(solution)/shard_map/ppermute | solution.py:256
  20.7 4.8 %collective-permute-start.7 = (f32[2,3072]{1,0:T(2,128)S(1)}, f32[2,3072]{1,0:T(2,128)S(1)}, u32[]{:S(2)}, u32[]{:S(2)}) collective-permute-start(f32[2,3072]{1,0:T(2,128)S(1)} %get-tuple-element.52.refs_0_), channel_id=1, source_target_pairs={{0,1},{1,0},{2,3},{3,2},{4,5},{5,4},{6,7},{7,6},{8,9},{9,8},{10,11... | collective-permute-start | bytes 73736 | tf_op jit(solution)/shard_map/ppermute | solution.py:256

commit v4 on v3

--- a/solution.py
+++ b/solution.py
@@ -179,9 +179,9 @@
     )(*ins)
 
 
-def update_kernel(places, tile, n_in, *refs):
+def update_kernel(places, cuts, n_in, *refs):
     blocks, (k_ref, rhs_ref, panel_ref, trailing_ref) = refs[:n_in], refs[n_in : n_in + 4]
-    cross_hbm, next_ref, left, cross, sems = refs[n_in + 4 :]
+    cross_hbm, next_hbm, left, cross, following, sems = refs[n_in + 4 :]
     rows, wide = rhs_ref.shape
     me = lax.axis_index("row")
     for ref, place in zip(blocks, places):
@@ -189,17 +189,17 @@
         for i, xor in enumerate(place):
             start = 0 if xor is None else (me ^ xor) * height
             left[pl.ds(start, height), :] = ref[i * height : (i + 1) * height, :]
-    copies = []
-    for t in range(wide // tile):
-        here = slice(t * tile, (t + 1) * tile)
-        product = jnp.dot(left[...], k_ref[:, here], preferred_element_type=jnp.float32)
-        cross[:, here] = (rhs_ref[:, here].astype(jnp.float32) - product).astype(cross.dtype)
-        copies.append(pltpu.make_async_copy(cross.at[:, here], cross_hbm.at[:, here], sems.at[t]))
-        copies[-1].start()
     product = lax.dot_general(
         panel_ref[...], left[...], (((1,), (1,)), ((), ())), preferred_element_type=jnp.float32
     )
-    next_ref[...] = trailing_ref[...] - product
+    following[...] = trailing_ref[...] - product
+    copies = [pltpu.make_async_copy(following, next_hbm, sems.at[len(cuts)])]
+    copies[0].start()
+    for t, (start, stop) in enumerate(cuts):
+        product = jnp.dot(left[...], k_ref[:, start:stop], preferred_element_type=jnp.float32)
+        cross[:, start:stop] = (rhs_ref[:, start:stop].astype(jnp.float32) - product).astype(cross.dtype)
+        copies.append(pltpu.make_async_copy(cross.at[:, start:stop], cross_hbm.at[:, start:stop], sems.at[t]))
+        copies[-1].start()
     for c in copies:
         c.wait()
 
@@ -208,18 +208,21 @@
     depth, wide = k.shape
     rows = rhs.shape[0]
     tile = tile_of(wide, 512)
+    edges = list(range(0, wide, tile)) + [wide - tile // 2, wide]
+    cuts = list(zip(edges, edges[1:]))
     return pl.pallas_call(
-        functools.partial(update_kernel, places, tile, len(blocks)),
+        functools.partial(update_kernel, places, cuts, len(blocks)),
         out_shape=[
             jax.ShapeDtypeStruct(rhs.shape, rhs.dtype),
             jax.ShapeDtypeStruct(trailing.shape, trailing.dtype),
         ],
         in_specs=[VMEM] * (len(blocks) + 4),
-        out_specs=[HBM, VMEM],
+        out_specs=[HBM, HBM],
         scratch_shapes=[
             pltpu.VMEM((rows, depth), jnp.bfloat16),
             pltpu.VMEM(rhs.shape, rhs.dtype),
-            pltpu.SemaphoreType.DMA((wide // tile,)),
+            pltpu.VMEM(trailing.shape, trailing.dtype),
+            pltpu.SemaphoreType.DMA((len(cuts) + 1,)),
         ],
         compiler_params=pltpu.CompilerParams(vmem_limit_bytes=32 * 2**20),
         cost_estimate=pl.CostEstimate(
@@ -275,7 +278,7 @@
     more = (panel_points, lengthscales.reshape(1, -1), targets, pick_sets, base_a, base_b)
     ins, parts = partial(panel_block, diag_inverse, more, n_col, near)
     if near:
-        got = [swap(parts[d], "col", d) for d in range(1, n_col)]
+        got = [swap(parts[d], "col", d) for d in range(n_col - 1, 0, -1)]
     k, sums = columns(ins)
     if near:
         got, k, sums = lax.optimization_barrier((got, k, sums))

time: 26.3 us -> 26.2 us (level)
  Pallas kernels: 8.75 us -> 8.25 us
  waiting for transfers between devices: 2.96 us -> 3.3 us
    pallas_call x1, Pallas kernels: 2.45 us -> 1.97 us  [update(): pl.pallas_call(functools.partial(update_kernel, places, cuts, len(blocks)...]
    ppermute x10, waiting for transfers between devices: 2.96 us -> 3.3 us  [swap(): lax.ppermute(x, axis, [(i, i ^ d) for i in range(lax.axis_size(axis))])]
  transfers between devices with their start and end apart: 10 -> 10, of which waited for: 2 -> 3; matrix products, arithmetic and copies ran while one was open for 0% -> 0% of each run, Pallas kernels for 24% -> 22%
where the time goes in v4:
time: 26.2 us; the launch traced here: 26.1 us
  starting transfers between devices  13.7 us (52%)
  Pallas kernels  8.25 us (31%)
  waiting for transfers between devices  3.3 us (13%)
  between operations  0.76 us (3%)
    ppermute x10, starting transfers between devices, swap(): lax.ppermute(x, axis, [(i, i ^ d) for i in range(lax.axis_size(axis))])  13.7 us
    pallas_call x1, Pallas kernels, columns(): pl.pallas_call(functools.partial(columns_kernel, tile), out_shape=[jax.Sh...  3.89 us
    ppermute x10, waiting for transfers between devices, swap(): lax.ppermute(x, axis, [(i, i ^ d) for i in range(lax.axis_size(axis))])  3.3 us
    pallas_call x1, Pallas kernels, update(): pl.pallas_call(functools.partial(update_kernel, places, cuts, len(blocks)...  1.97 us
    pallas_call x1, Pallas kernels, partial(): pl.pallas_call(functools.partial(partial_kernel, n_col, swapped, len(more...  1.78 us
    pallas_call x1, Pallas kernels, finish(): pl.pallas_call(finish_kernel, out_shape=[flat, flat], in_specs=[VMEM] * (...  0.62 us
  transfers between devices with their start and end apart: 10, of which 3 were waited for; matrix products, arithmetic and copies ran while one was open for 0% of the time, Pallas kernels for 22%

profile of v4, /device:TPU:0, one launch (start us, length us, event | category | flops | bytes accessed | tf_op | source)
XLA Modules:
  0.0 26.1 jit_solution(10704135990042039062)
XLA Ops:
  0.6 1.8 %partial.1 = (bf16[256,1024]{1,0:T(8,128)(2,1)S(1)}, f32[20,1024]{1,0:T(8,128)S(1)}, f32[1,20]{1,0:T(1,128)S(1)}, bf16[1024]{0:T(1024)(128)(2,1)S(1)}, s32[12,20...) custom-call(bf16[64,1024]{1,0:T(8,128)(2,1)} %refs_6_.3, ...), custom_call_target="tpu_custom_call" | custom-call | tf_op jit(solution)/shard_map/partial/pallas_call | solution.py:89
  2.4 0.0 copy-start
  2.4 0.0 copy-start.1
  2.4 0.0 copy-start.2
  2.5 5.1 %collective-permute-start = (bf16[16,1024]{1,0:T(8,128)(2,1)S(1)}, bf16[16,1024]{1,0:T(8,128)(2,1)S(1)}, u32[]{:S(2)}, u32[]{:S(2)}) collective-permute-start(bf16[16,1024]{1,0:T(8,128)(2,1)S(1)} %get-tuple-element.32), channel_id=1, source_target_pairs={{0,3},{1,2},{2,1},{3,0},{4,7},{5,6},{6,5},{7,4},{8,11},{9,10},{10,... | collective-permute-start | bytes 98312 | tf_op jit(solution)/shard_map/ppermute | solution.py:259
  7.6 0.0 collective-permute-start.1
  7.6 0.6 %collective-permute-start.2 = (bf16[16,1024]{1,0:T(8,128)(2,1)S(1)}, bf16[16,1024]{1,0:T(8,128)(2,1)S(1)}, u32[]{:S(2)}, u32[]{:S(2)}) collective-permute-start(bf16[16,1024]{1,0:T(8,128)(2,1)S(1)} %get-tuple-element.34), channel_id=1, source_target_pairs={{0,1},{1,0},{2,3},{3,2},{4,5},{5,4},{6,7},{7,6},{8,9},{9,8},{10,11... | collective-permute-start | bytes 98312 | tf_op jit(solution)/shard_map/ppermute | solution.py:259
  8.2 3.9 %columns.1 = (bf16[1024,3072]{1,0:T(8,128)(2,1)S(1)}, f32[2,3072]{1,0:T(2,128)S(1)}) custom-call(bf16[256,1024]{1,0:T(8,128)(2,1)S(1)} %get-tuple-element.35.inv_ref, f32[20,1024]{1,0:T(8,128)S(1)} %get-tuple-element.36.points_ref, f32[1,20]{1,0:T(1,128)S(1)} %get-tuple-element.37.scale_ref, bf16[1024]{0:T(1024)(128)(2,1)S(1)} %get-tuple-element.38.target_ref, ...), custom_call_target="tpu_custom_call" | custom-call | flops 3221225472 | bytes 6291456 | tf_op jit(solution)/shard_map/columns/pallas_call | solution.py:159
  12.1 0.0 copy-start.3
  12.1 0.0 copy-start.4
  12.1 0.0 collective-permute-done
  12.1 0.2 collective-permute-done.1
  12.4 0.1 collective-permute-start.3
  12.5 1.2 %collective-permute-done.3 = bf16[16,1024]{1,0:T(8,128)(2,1)S(1)} collective-permute-done((bf16[16,1024]{1,0:T(8,128)(2,1)S(1)}, bf16[16,1024]{1,0:T(8,128)(2,1)S(1)}, u32[]{:S(2)}, u32[]{:S(2)}) %collective-permute-start.3) | collective-permute-done | bytes 32800 | tf_op jit(solution)/shard_map/ppermute | solution.py:259
  13.7 2.4 %collective-permute-start.6 = (bf16[32,1024]{1,0:T(8,128)(2,1)S(1)}, bf16[32,1024]{1,0:T(8,128)(2,1)S(1)}, u32[]{:S(2)}, u32[]{:S(2)}) collective-permute-start(bf16[32,1024]{1,0:T(8,128)(2,1)S(1)} %pad_maximum_fusion.refs_0_), channel_id=1, source_target_pairs={{0,24},{4,28},{8,16},{12,20},{16,8},{20,12},{24,0},{28,4},{1,25},{... | collective-permute-start | bytes 196616 | tf_op jit(solution)/shard_map/ppermute | solution.py:259
  16.1 0.5 %collective-permute-start.5 = (bf16[32,1024]{1,0:T(8,128)(2,1)S(1)}, bf16[32,1024]{1,0:T(8,128)(2,1)S(1)}, u32[]{:S(2)}, u32[]{:S(2)}) collective-permute-start(bf16[32,1024]{1,0:T(8,128)(2,1)S(1)} %pad_maximum_fusion.refs_0_), channel_id=1, source_target_pairs={{0,16},{4,20},{8,24},{12,28},{16,0},{20,4},{24,8},{28,12},{1,17},{... | collective-permute-start | bytes 196616 | tf_op jit(solution)/shard_map/ppermute | solution.py:259
  16.6 0.5 %collective-permute-start.4 = (bf16[32,1024]{1,0:T(8,128)(2,1)S(1)}, bf16[32,1024]{1,0:T(8,128)(2,1)S(1)}, u32[]{:S(2)}, u32[]{:S(2)}) collective-permute-start(bf16[32,1024]{1,0:T(8,128)(2,1)S(1)} %pad_maximum_fusion.refs_0_), channel_id=1, source_target_pairs={{0,8},{4,12},{8,0},{12,4},{16,24},{20,28},{24,16},{28,20},{1,9},{5... | collective-permute-start | bytes 196616 | tf_op jit(solution)/shard_map/ppermute | solution.py:259
  17.2 3.5 %collective-permute-start.9 = (f32[2,3072]{1,0:T(2,128)S(1)}, f32[2,3072]{1,0:T(2,128)S(1)}, u32[]{:S(2)}, u32[]{:S(2)}) collective-permute-start(f32[2,3072]{1,0:T(2,128)S(1)} %get-tuple-element.52.refs_0_), channel_id=1, source_target_pairs={{0,3},{1,2},{2,1},{3,0},{4,7},{5,6},{6,5},{7,4},{8,11},{9,10},{10,... | collective-permute-start | bytes 73736 | tf_op jit(solution)/shard_map/ppermute | solution.py:259
  20.7 0.0 collective-permute-start.8
  20.7 0.0 collective-permute-done.6.refs_3_
  20.7 0.9 %collective-permute-start.7 = (f32[2,3072]{1,0:T(2,128)S(1)}, f32[2,3072]{1,0:T(2,128)S(1)}, u32[]{:S(2)}, u32[]{:S(2)}) collective-permute-start(f32[2,3072]{1,0:T(2,128)S(1)} %get-tuple-element.52.refs_0_), channel_id=1, source_target_pairs={{0,1},{1,0},{2,3},{3,2},{4,5},{5,4},{6,7},{7,6},{8,9},{9,8},{10,11... | collective-permute-start | bytes 73736 | tf_op jit(solution)/shard_map/ppermute | solution.py:259
  21.6 2.0 %update.1 = (bf16[128,3072]{1,0:T(8,128)(2,1)}, f32[64,128]{1,0:T(8,128)}) custom-call(bf16[32,1024]{1,0:T(8,128)(2,1)S(1)} %pad_maximum_fusion.refs_0_, bf16[32,1024]{1,0:T(8,128)(2,1)S(1)} %collective-permute-done.4.refs_1_, bf16[32,1024]{1,0:T(8,128)(2,1)S(1)} %collective-permute-done.5.refs_2_, bf16[32,1024]{1,0:T(8,128)(2,1)S(1)} %collective-permute-done.6.refs_3_, ...), custom_call_target="tpu_custom_call" | custom-call | flops 805306368 | bytes 6291456 | tf_op jit(solution)/shard_map/update/pallas_call | solution.py:213
  23.6 1.8 %collective-permute-done.8.refs_2_ = f32[2,3072]{1,0:T(2,128)S(1)} collective-permute-done((f32[2,3072]{1,0:T(2,128)S(1)}, f32[2,3072]{1,0:T(2,128)S(1)}, u32[]{:S(2)}, u32[]{:S(2)}) %collective-permute-start.8) | collective-permute-done | bytes 24608 | tf_op jit(solution)/shard_map/ppermute | solution.py:259
  25.4 0.6 %finish.1 = (f32[1,3072]{1,0:T(1,128)}, f32[1,3072]{1,0:T(1,128)}) custom-call(f32[2,3072]{1,0:T(2,128)S(1)} %get-tuple-element.52.refs_0_, f32[2,3072]{1,0:T(2,128)S(1)} %collective-permute-done.7.refs_1_, f32[2,3072]{1,0:T(2,128)S(1)} %collective-permute-done.8.refs_2_, f32[2,3072]{1,0:T(2,128)S(1)} %collective-permute-done.9.refs_3_, ...), custom_call_target="tpu_custom_call" | custom-call | tf_op jit(solution)/shard_map/finish/pallas_call | solution.py:247
  (12 shorter events, 0.0 us)
Async XLA Ops:
  2.4 19.2 %copy-start = (bf16[128,3072]{1,0:T(8,128)(2,1)S(1)}, bf16[128,3072]{1,0:T(8,128)(2,1)}, u32[]{:S(2)}) copy-start(bf16[128,3072]{1,0:T(8,128)(2,1)} %refs_5_.3) | copy-start | bytes 2359300
  2.4 19.2 %copy-start.1 = (bf16[64,1024]{1,0:T(8,128)(2,1)S(1)}, bf16[64,1024]{1,0:T(8,128)(2,1)}, u32[]{:S(2)}) copy-start(bf16[64,1024]{1,0:T(8,128)(2,1)} %refs_6_.3) | copy-start | bytes 393220
  2.4 19.2 %copy-start.2 = (f32[64,128]{1,0:T(8,128)S(1)}, f32[64,128]{1,0:T(8,128)}, u32[]{:S(2)}) copy-start(f32[64,128]{1,0:T(8,128)} %refs_7_.3) | copy-start | bytes 98308
  2.5 9.7 %collective-permute-start = (bf16[16,1024]{1,0:T(8,128)(2,1)S(1)}, bf16[16,1024]{1,0:T(8,128)(2,1)S(1)}, u32[]{:S(2)}, u32[]{:S(2)}) collective-permute-start(bf16[16,1024]{1,0:T(8,128)(2,1)S(1)} %get-tuple-element.32), channel_id=1, source_target_pairs={{0,3},{1,2},{2,1},{3,0},{4,7},{5,6},{6,5},{7,4},{8,11},{9,10},{10,... | collective-permute-start | bytes 98312 | tf_op jit(solution)/shard_map/ppermute | solution.py:259
  7.6 4.8 %collective-permute-start.1 = (bf16[16,1024]{1,0:T(8,128)(2,1)S(1)}, bf16[16,1024]{1,0:T(8,128)(2,1)S(1)}, u32[]{:S(2)}, u32[]{:S(2)}) collective-permute-start(bf16[16,1024]{1,0:T(8,128)(2,1)S(1)} %get-tuple-element.33), channel_id=1, source_target_pairs={{0,2},{1,3},{2,0},{3,1},{4,6},{5,7},{6,4},{7,5},{8,10},{9,11},{10,... | collective-permute-start | bytes 98312 | tf_op jit(solution)/shard_map/ppermute | solution.py:259
  7.6 4.8 %collective-permute-start.2 = (bf16[16,1024]{1,0:T(8,128)(2,1)S(1)}, bf16[16,1024]{1,0:T(8,128)(2,1)S(1)}, u32[]{:S(2)}, u32[]{:S(2)}) collective-permute-start(bf16[16,1024]{1,0:T(8,128)(2,1)S(1)} %get-tuple-element.34), channel_id=1, source_target_pairs={{0,1},{1,0},{2,3},{3,2},{4,5},{5,4},{6,7},{7,6},{8,9},{9,8},{10,11... | collective-permute-start | bytes 98312 | tf_op jit(solution)/shard_map/ppermute | solution.py:259
  12.1 13.3 %copy-start.3 = (f32[3072]{0:T(1024)S(1)}, f32[3072]{0:T(1024)}, u32[]{:S(2)}) copy-start(f32[3072]{0:T(1024)} %param.22) | copy-start | bytes 36868
  12.1 13.3 %copy-start.4 = (f32[3072]{0:T(1024)S(1)}, f32[3072]{0:T(1024)}, u32[]{:S(2)}) copy-start(f32[3072]{0:T(1024)} %param.23) | copy-start | bytes 36868
  12.4 1.3 %collective-permute-start.3 = (bf16[16,1024]{1,0:T(8,128)(2,1)S(1)}, bf16[16,1024]{1,0:T(8,128)(2,1)S(1)}, u32[]{:S(2)}, u32[]{:S(2)}) collective-permute-start(bf16[16,1024]{1,0:T(8,128)(2,1)S(1)} %add_convert_fusion), channel_id=1, source_target_pairs={{0,4},{4,0},{8,12},{12,8},{16,20},{20,16},{24,28},{28,24},{1,5},{5... | collective-permute-start | bytes 98312 | tf_op jit(solution)/shard_map/ppermute | solution.py:259
  13.7 7.0 %collective-permute-start.6 = (bf16[32,1024]{1,0:T(8,128)(2,1)S(1)}, bf16[32,1024]{1,0:T(8,128)(2,1)S(1)}, u32[]{:S(2)}, u32[]{:S(2)}) collective-permute-start(bf16[32,1024]{1,0:T(8,128)(2,1)S(1)} %pad_maximum_fusion.refs_0_), channel_id=1, source_target_pairs={{0,24},{4,28},{8,16},{12,20},{16,8},{20,12},{24,0},{28,4},{1,25},{... | collective-permute-start | bytes 196616 | tf_op jit(solution)/shard_map/ppermute | solution.py:259
  16.1 5.4 %collective-permute-start.5 = (bf16[32,1024]{1,0:T(8,128)(2,1)S(1)}, bf16[32,1024]{1,0:T(8,128)(2,1)S(1)}, u32[]{:S(2)}, u32[]{:S(2)}) collective-permute-start(bf16[32,1024]{1,0:T(8,128)(2,1)S(1)} %pad_maximum_fusion.refs_0_), channel_id=1, source_target_pairs={{0,16},{4,20},{8,24},{12,28},{16,0},{20,4},{24,8},{28,12},{1,17},{... | collective-permute-start | bytes 196616 | tf_op jit(solution)/shard_map/ppermute | solution.py:259
  16.6 4.9 %collective-permute-start.4 = (bf16[32,1024]{1,0:T(8,128)(2,1)S(1)}, bf16[32,1024]{1,0:T(8,128)(2,1)S(1)}, u32[]{:S(2)}, u32[]{:S(2)}) collective-permute-start(bf16[32,1024]{1,0:T(8,128)(2,1)S(1)} %pad_maximum_fusion.refs_0_), channel_id=1, source_target_pairs={{0,8},{4,12},{8,0},{12,4},{16,24},{20,28},{24,16},{28,20},{1,9},{5... | collective-permute-start | bytes 196616 | tf_op jit(solution)/shard_map/ppermute | solution.py:259
  17.2 6.4 %collective-permute-start.9 = (f32[2,3072]{1,0:T(2,128)S(1)}, f32[2,3072]{1,0:T(2,128)S(1)}, u32[]{:S(2)}, u32[]{:S(2)}) collective-permute-start(f32[2,3072]{1,0:T(2,128)S(1)} %get-tuple-element.52.refs_0_), channel_id=1, source_target_pairs={{0,3},{1,2},{2,1},{3,0},{4,7},{5,6},{6,5},{7,4},{8,11},{9,10},{10,... | collective-permute-start | bytes 73736 | tf_op jit(solution)/shard_map/ppermute | solution.py:259
  20.7 4.7 %collective-permute-start.8 = (f32[2,3072]{1,0:T(2,128)S(1)}, f32[2,3072]{1,0:T(2,128)S(1)}, u32[]{:S(2)}, u32[]{:S(2)}) collective-permute-start(f32[2,3072]{1,0:T(2,128)S(1)} %get-tuple-element.52.refs_0_), channel_id=1, source_target_pairs={{0,2},{1,3},{2,0},{3,1},{4,6},{5,7},{6,4},{7,5},{8,10},{9,11},{10,... | collective-permute-start | bytes 73736 | tf_op jit(solution)/shard_map/ppermute | solution.py:259
  20.7 4.7 %collective-permute-start.7 = (f32[2,3072]{1,0:T(2,128)S(1)}, f32[2,3072]{1,0:T(2,128)S(1)}, u32[]{:S(2)}, u32[]{:S(2)}) collective-permute-start(f32[2,3072]{1,0:T(2,128)S(1)} %get-tuple-element.52.refs_0_), channel_id=1, source_target_pairs={{0,1},{1,0},{2,3},{3,2},{4,5},{5,4},{6,7},{7,6},{8,9},{9,8},{10,11... | collective-permute-start | bytes 73736 | tf_op jit(solution)/shard_map/ppermute | solution.py:259

commit v5 on v4

--- a/solution.py
+++ b/solution.py
@@ -278,7 +278,7 @@
     more = (panel_points, lengthscales.reshape(1, -1), targets, pick_sets, base_a, base_b)
     ins, parts = partial(panel_block, diag_inverse, more, n_col, near)
     if near:
-        got = [swap(parts[d], "col", d) for d in range(n_col - 1, 0, -1)]
+        got = [swap(parts[d], "col", d) for d in (2, 3, 1) if d < n_col]
     k, sums = columns(ins)
     if near:
         got, k, sums = lax.optimization_barrier((got, k, sums))

time: 26.2 us -> 25.5 us (0.973)
  waiting for transfers between devices: 3.3 us -> 2.64 us
    ppermute x10, waiting for transfers between devices: 3.3 us -> 2.64 us  [swap(): lax.ppermute(x, axis, [(i, i ^ d) for i in range(lax.axis_size(axis))])]
  transfers between devices with their start and end apart: 10 -> 10, of which waited for: 3 -> 3; matrix products, arithmetic and copies ran while one was open for 0% -> 0% of each run, Pallas kernels for 22% -> 23%
where the time goes in v5:
time: 25.5 us; the launch traced here: 25.3 us
  starting transfers between devices  13.6 us (53%)
  Pallas kernels  8.24 us (32%)
  waiting for transfers between devices  2.64 us (10%)
  between operations  0.76 us (3%)
    ppermute x10, starting transfers between devices, swap(): lax.ppermute(x, axis, [(i, i ^ d) for i in range(lax.axis_size(axis))])  13.6 us
    pallas_call x1, Pallas kernels, columns(): pl.pallas_call(functools.partial(columns_kernel, tile), out_shape=[jax.Sh...  3.89 us
    ppermute x10, waiting for transfers between devices, swap(): lax.ppermute(x, axis, [(i, i ^ d) for i in range(lax.axis_size(axis))])  2.64 us
    pallas_call x1, Pallas kernels, update(): pl.pallas_call(functools.partial(update_kernel, places, cuts, len(blocks)...  1.95 us
    pallas_call x1, Pallas kernels, partial(): pl.pallas_call(functools.partial(partial_kernel, n_col, swapped, len(more...  1.78 us
    pallas_call x1, Pallas kernels, finish(): pl.pallas_call(finish_kernel, out_shape=[flat, flat], in_specs=[VMEM] * (...  0.62 us
  transfers between devices with their start and end apart: 10, of which 3 were waited for; matrix products, arithmetic and copies ran while one was open for 0% of the time, Pallas kernels for 23%

profile of v5, /device:TPU:0, one launch (start us, length us, event | category | flops | bytes accessed | tf_op | source)
XLA Modules:
  0.0 25.3 jit_solution(8091688299769104220)
XLA Ops:
  0.6 1.8 %partial.1 = (bf16[256,1024]{1,0:T(8,128)(2,1)S(1)}, f32[20,1024]{1,0:T(8,128)S(1)}, f32[1,20]{1,0:T(1,128)S(1)}, bf16[1024]{0:T(1024)(128)(2,1)S(1)}, s32[12,20...) custom-call(bf16[64,1024]{1,0:T(8,128)(2,1)} %refs_6_.3, ...), custom_call_target="tpu_custom_call" | custom-call | tf_op jit(solution)/shard_map/partial/pallas_call | solution.py:89
  2.4 0.0 copy-start
  2.4 0.0 copy-start.1
  2.4 0.0 copy-start.2
  2.5 4.1 %collective-permute-start = (bf16[16,1024]{1,0:T(8,128)(2,1)S(1)}, bf16[16,1024]{1,0:T(8,128)(2,1)S(1)}, u32[]{:S(2)}, u32[]{:S(2)}) collective-permute-start(bf16[16,1024]{1,0:T(8,128)(2,1)S(1)} %get-tuple-element.32), channel_id=1, source_target_pairs={{0,2},{1,3},{2,0},{3,1},{4,6},{5,7},{6,4},{7,5},{8,10},{9,11},{10,... | collective-permute-start | bytes 98312 | tf_op jit(solution)/shard_map/ppermute | solution.py:259
  6.6 1.3 %collective-permute-start.1 = (bf16[16,1024]{1,0:T(8,128)(2,1)S(1)}, bf16[16,1024]{1,0:T(8,128)(2,1)S(1)}, u32[]{:S(2)}, u32[]{:S(2)}) collective-permute-start(bf16[16,1024]{1,0:T(8,128)(2,1)S(1)} %get-tuple-element.33), channel_id=1, source_target_pairs={{0,3},{1,2},{2,1},{3,0},{4,7},{5,6},{6,5},{7,4},{8,11},{9,10},{10,... | collective-permute-start | bytes 98312 | tf_op jit(solution)/shard_map/ppermute | solution.py:259
  7.9 0.2 collective-permute-start.2
  8.1 3.9 %columns.1 = (bf16[1024,3072]{1,0:T(8,128)(2,1)S(1)}, f32[2,3072]{1,0:T(2,128)S(1)}) custom-call(bf16[256,1024]{1,0:T(8,128)(2,1)S(1)} %get-tuple-element.35.inv_ref, f32[20,1024]{1,0:T(8,128)S(1)} %get-tuple-element.36.points_ref, f32[1,20]{1,0:T(1,128)S(1)} %get-tuple-element.37.scale_ref, bf16[1024]{0:T(1024)(128)(2,1)S(1)} %get-tuple-element.38.target_ref, ...), custom_call_target="tpu_custom_call" | custom-call | flops 3221225472 | bytes 6291456 | tf_op jit(solution)/shard_map/columns/pallas_call | solution.py:159
  12.0 0.0 copy-start.3
  12.0 0.0 copy-start.4
  12.1 0.0 collective-permute-done
  12.1 0.2 collective-permute-done.1
  12.3 0.1 collective-permute-start.3
  12.4 1.2 %collective-permute-done.3 = bf16[16,1024]{1,0:T(8,128)(2,1)S(1)} collective-permute-done((bf16[16,1024]{1,0:T(8,128)(2,1)S(1)}, bf16[16,1024]{1,0:T(8,128)(2,1)S(1)}, u32[]{:S(2)}, u32[]{:S(2)}) %collective-permute-start.3) | collective-permute-done | bytes 32800 | tf_op jit(solution)/shard_map/ppermute | solution.py:259
  13.6 2.4 %collective-permute-start.6 = (bf16[32,1024]{1,0:T(8,128)(2,1)S(1)}, bf16[32,1024]{1,0:T(8,128)(2,1)S(1)}, u32[]{:S(2)}, u32[]{:S(2)}) collective-permute-start(bf16[32,1024]{1,0:T(8,128)(2,1)S(1)} %pad_maximum_fusion.refs_0_), channel_id=1, source_target_pairs={{0,24},{4,28},{8,16},{12,20},{16,8},{20,12},{24,0},{28,4},{1,25},{... | collective-permute-start | bytes 196616 | tf_op jit(solution)/shard_map/ppermute | solution.py:259
  16.0 0.5 %collective-permute-start.5 = (bf16[32,1024]{1,0:T(8,128)(2,1)S(1)}, bf16[32,1024]{1,0:T(8,128)(2,1)S(1)}, u32[]{:S(2)}, u32[]{:S(2)}) collective-permute-start(bf16[32,1024]{1,0:T(8,128)(2,1)S(1)} %pad_maximum_fusion.refs_0_), channel_id=1, source_target_pairs={{0,16},{4,20},{8,24},{12,28},{16,0},{20,4},{24,8},{28,12},{1,17},{... | collective-permute-start | bytes 196616 | tf_op jit(solution)/shard_map/ppermute | solution.py:259
  16.5 0.5 %collective-permute-start.4 = (bf16[32,1024]{1,0:T(8,128)(2,1)S(1)}, bf16[32,1024]{1,0:T(8,128)(2,1)S(1)}, u32[]{:S(2)}, u32[]{:S(2)}) collective-permute-start(bf16[32,1024]{1,0:T(8,128)(2,1)S(1)} %pad_maximum_fusion.refs_0_), channel_id=1, source_target_pairs={{0,8},{4,12},{8,0},{12,4},{16,24},{20,28},{24,16},{28,20},{1,9},{5... | collective-permute-start | bytes 196616 | tf_op jit(solution)/shard_map/ppermute | solution.py:259
  17.1 2.7 %collective-permute-start.9 = (f32[2,3072]{1,0:T(2,128)S(1)}, f32[2,3072]{1,0:T(2,128)S(1)}, u32[]{:S(2)}, u32[]{:S(2)}) collective-permute-start(f32[2,3072]{1,0:T(2,128)S(1)} %get-tuple-element.52.refs_0_), channel_id=1, source_target_pairs={{0,3},{1,2},{2,1},{3,0},{4,7},{5,6},{6,5},{7,4},{8,11},{9,10},{10,... | collective-permute-start | bytes 73736 | tf_op jit(solution)/shard_map/ppermute | solution.py:259
  19.8 0.3 %collective-permute-start.8 = (f32[2,3072]{1,0:T(2,128)S(1)}, f32[2,3072]{1,0:T(2,128)S(1)}, u32[]{:S(2)}, u32[]{:S(2)}) collective-permute-start(f32[2,3072]{1,0:T(2,128)S(1)} %get-tuple-element.52.refs_0_), channel_id=1, source_target_pairs={{0,2},{1,3},{2,0},{3,1},{4,6},{5,7},{6,4},{7,5},{8,10},{9,11},{10,... | collective-permute-start | bytes 73736 | tf_op jit(solution)/shard_map/ppermute | solution.py:259
  20.1 0.0 collective-permute-done.6.refs_3_
  20.2 1.3 %collective-permute-start.7 = (f32[2,3072]{1,0:T(2,128)S(1)}, f32[2,3072]{1,0:T(2,128)S(1)}, u32[]{:S(2)}, u32[]{:S(2)}) collective-permute-start(f32[2,3072]{1,0:T(2,128)S(1)} %get-tuple-element.52.refs_0_), channel_id=1, source_target_pairs={{0,1},{1,0},{2,3},{3,2},{4,5},{5,4},{6,7},{7,6},{8,9},{9,8},{10,11... | collective-permute-start | bytes 73736 | tf_op jit(solution)/shard_map/ppermute | solution.py:259
  21.5 2.0 %update.1 = (bf16[128,3072]{1,0:T(8,128)(2,1)}, f32[64,128]{1,0:T(8,128)}) custom-call(bf16[32,1024]{1,0:T(8,128)(2,1)S(1)} %pad_maximum_fusion.refs_0_, bf16[32,1024]{1,0:T(8,128)(2,1)S(1)} %collective-permute-done.4.refs_1_, bf16[32,1024]{1,0:T(8,128)(2,1)S(1)} %collective-permute-done.5.refs_2_, bf16[32,1024]{1,0:T(8,128)(2,1)S(1)} %collective-permute-done.6.refs_3_, ...), custom_call_target="tpu_custom_call" | custom-call | flops 805306368 | bytes 6291456 | tf_op jit(solution)/shard_map/update/pallas_call | solution.py:213
  23.5 1.2 %collective-permute-done.8.refs_2_ = f32[2,3072]{1,0:T(2,128)S(1)} collective-permute-done((f32[2,3072]{1,0:T(2,128)S(1)}, f32[2,3072]{1,0:T(2,128)S(1)}, u32[]{:S(2)}, u32[]{:S(2)}) %collective-permute-start.8) | collective-permute-done | bytes 24608 | tf_op jit(solution)/shard_map/ppermute | solution.py:259
  24.7 0.6 %finish.1 = (f32[1,3072]{1,0:T(1,128)}, f32[1,3072]{1,0:T(1,128)}) custom-call(f32[2,3072]{1,0:T(2,128)S(1)} %get-tuple-element.52.refs_0_, f32[2,3072]{1,0:T(2,128)S(1)} %collective-permute-done.7.refs_1_, f32[2,3072]{1,0:T(2,128)S(1)} %collective-permute-done.8.refs_2_, f32[2,3072]{1,0:T(2,128)S(1)} %collective-permute-done.9.refs_3_, ...), custom_call_target="tpu_custom_call" | custom-call | tf_op jit(solution)/shard_map/finish/pallas_call | solution.py:247
  (12 shorter events, 0.0 us)
Async XLA Ops:
  2.4 19.1 %copy-start = (bf16[128,3072]{1,0:T(8,128)(2,1)S(1)}, bf16[128,3072]{1,0:T(8,128)(2,1)}, u32[]{:S(2)}) copy-start(bf16[128,3072]{1,0:T(8,128)(2,1)} %refs_5_.3) | copy-start | bytes 2359300
  2.4 19.0 %copy-start.1 = (bf16[64,1024]{1,0:T(8,128)(2,1)S(1)}, bf16[64,1024]{1,0:T(8,128)(2,1)}, u32[]{:S(2)}) copy-start(bf16[64,1024]{1,0:T(8,128)(2,1)} %refs_6_.3) | copy-start | bytes 393220
  2.4 19.0 %copy-start.2 = (f32[64,128]{1,0:T(8,128)S(1)}, f32[64,128]{1,0:T(8,128)}, u32[]{:S(2)}) copy-start(f32[64,128]{1,0:T(8,128)} %refs_7_.3) | copy-start | bytes 98308
  2.5 9.6 %collective-permute-start = (bf16[16,1024]{1,0:T(8,128)(2,1)S(1)}, bf16[16,1024]{1,0:T(8,128)(2,1)S(1)}, u32[]{:S(2)}, u32[]{:S(2)}) collective-permute-start(bf16[16,1024]{1,0:T(8,128)(2,1)S(1)} %get-tuple-element.32), channel_id=1, source_target_pairs={{0,2},{1,3},{2,0},{3,1},{4,6},{5,7},{6,4},{7,5},{8,10},{9,11},{10,... | collective-permute-start | bytes 98312 | tf_op jit(solution)/shard_map/ppermute | solution.py:259
  6.6 5.7 %collective-permute-start.1 = (bf16[16,1024]{1,0:T(8,128)(2,1)S(1)}, bf16[16,1024]{1,0:T(8,128)(2,1)S(1)}, u32[]{:S(2)}, u32[]{:S(2)}) collective-permute-start(bf16[16,1024]{1,0:T(8,128)(2,1)S(1)} %get-tuple-element.33), channel_id=1, source_target_pairs={{0,3},{1,2},{2,1},{3,0},{4,7},{5,6},{6,5},{7,4},{8,11},{9,10},{10,... | collective-permute-start | bytes 98312 | tf_op jit(solution)/shard_map/ppermute | solution.py:259
  7.9 4.4 %collective-permute-start.2 = (bf16[16,1024]{1,0:T(8,128)(2,1)S(1)}, bf16[16,1024]{1,0:T(8,128)(2,1)S(1)}, u32[]{:S(2)}, u32[]{:S(2)}) collective-permute-start(bf16[16,1024]{1,0:T(8,128)(2,1)S(1)} %get-tuple-element.34), channel_id=1, source_target_pairs={{0,1},{1,0},{2,3},{3,2},{4,5},{5,4},{6,7},{7,6},{8,9},{9,8},{10,11... | collective-permute-start | bytes 98312 | tf_op jit(solution)/shard_map/ppermute | solution.py:259
  12.0 12.7 %copy-start.3 = (f32[3072]{0:T(1024)S(1)}, f32[3072]{0:T(1024)}, u32[]{:S(2)}) copy-start(f32[3072]{0:T(1024)} %param.22) | copy-start | bytes 36868
  12.0 12.7 %copy-start.4 = (f32[3072]{0:T(1024)S(1)}, f32[3072]{0:T(1024)}, u32[]{:S(2)}) copy-start(f32[3072]{0:T(1024)} %param.23) | copy-start | bytes 36868
  12.3 1.3 %collective-permute-start.3 = (bf16[16,1024]{1,0:T(8,128)(2,1)S(1)}, bf16[16,1024]{1,0:T(8,128)(2,1)S(1)}, u32[]{:S(2)}, u32[]{:S(2)}) collective-permute-start(bf16[16,1024]{1,0:T(8,128)(2,1)S(1)} %add_convert_fusion), channel_id=1, source_target_pairs={{0,4},{4,0},{8,12},{12,8},{16,20},{20,16},{24,28},{28,24},{1,5},{5... | collective-permute-start | bytes 98312 | tf_op jit(solution)/shard_map/ppermute | solution.py:259
  13.6 6.6 %collective-permute-start.6 = (bf16[32,1024]{1,0:T(8,128)(2,1)S(1)}, bf16[32,1024]{1,0:T(8,128)(2,1)S(1)}, u32[]{:S(2)}, u32[]{:S(2)}) collective-permute-start(bf16[32,1024]{1,0:T(8,128)(2,1)S(1)} %pad_maximum_fusion.refs_0_), channel_id=1, source_target_pairs={{0,24},{4,28},{8,16},{12,20},{16,8},{20,12},{24,0},{28,4},{1,25},{... | collective-permute-start | bytes 196616 | tf_op jit(solution)/shard_map/ppermute | solution.py:259
  16.0 5.4 %collective-permute-start.5 = (bf16[32,1024]{1,0:T(8,128)(2,1)S(1)}, bf16[32,1024]{1,0:T(8,128)(2,1)S(1)}, u32[]{:S(2)}, u32[]{:S(2)}) collective-permute-start(bf16[32,1024]{1,0:T(8,128)(2,1)S(1)} %pad_maximum_fusion.refs_0_), channel_id=1, source_target_pairs={{0,16},{4,20},{8,24},{12,28},{16,0},{20,4},{24,8},{28,12},{1,17},{... | collective-permute-start | bytes 196616 | tf_op jit(solution)/shard_map/ppermute | solution.py:259
  16.5 4.9 %collective-permute-start.4 = (bf16[32,1024]{1,0:T(8,128)(2,1)S(1)}, bf16[32,1024]{1,0:T(8,128)(2,1)S(1)}, u32[]{:S(2)}, u32[]{:S(2)}) collective-permute-start(bf16[32,1024]{1,0:T(8,128)(2,1)S(1)} %pad_maximum_fusion.refs_0_), channel_id=1, source_target_pairs={{0,8},{4,12},{8,0},{12,4},{16,24},{20,28},{24,16},{28,20},{1,9},{5... | collective-permute-start | bytes 196616 | tf_op jit(solution)/shard_map/ppermute | solution.py:259
  17.1 6.4 %collective-permute-start.9 = (f32[2,3072]{1,0:T(2,128)S(1)}, f32[2,3072]{1,0:T(2,128)S(1)}, u32[]{:S(2)}, u32[]{:S(2)}) collective-permute-start(f32[2,3072]{1,0:T(2,128)S(1)} %get-tuple-element.52.refs_0_), channel_id=1, source_target_pairs={{0,3},{1,2},{2,1},{3,0},{4,7},{5,6},{6,5},{7,4},{8,11},{9,10},{10,... | collective-permute-start | bytes 73736 | tf_op jit(solution)/shard_map/ppermute | solution.py:259
  19.8 4.9 %collective-permute-start.8 = (f32[2,3072]{1,0:T(2,128)S(1)}, f32[2,3072]{1,0:T(2,128)S(1)}, u32[]{:S(2)}, u32[]{:S(2)}) collective-permute-start(f32[2,3072]{1,0:T(2,128)S(1)} %get-tuple-element.52.refs_0_), channel_id=1, source_target_pairs={{0,2},{1,3},{2,0},{3,1},{4,6},{5,7},{6,4},{7,5},{8,10},{9,11},{10,... | collective-permute-start | bytes 73736 | tf_op jit(solution)/shard_map/ppermute | solution.py:259
  20.2 4.5 %collective-permute-start.7 = (f32[2,3072]{1,0:T(2,128)S(1)}, f32[2,3072]{1,0:T(2,128)S(1)}, u32[]{:S(2)}, u32[]{:S(2)}) collective-permute-start(f32[2,3072]{1,0:T(2,128)S(1)} %get-tuple-element.52.refs_0_), channel_id=1, source_target_pairs={{0,1},{1,0},{2,3},{3,2},{4,5},{5,4},{6,7},{7,6},{8,9},{9,8},{10,11... | collective-permute-start | bytes 73736 | tf_op jit(solution)/shard_map/ppermute | solution.py:259

commit v6 on v5

--- a/solution.py
+++ b/solution.py
@@ -55,12 +55,30 @@
 
 def partial_kernel(n_col, swapped, n_more, *refs):
     sources, refs = refs[: 2 + n_more], refs[2 + n_more :]
-    more, out_refs, (panel_ref, sems) = refs[: n_more + 1], refs[n_more + 1 : -2], refs[-2:]
-    inv_ref = more[0]
-    copies = fetch(sources, (panel_ref, *more), sems)
+    more, pt, out_refs = refs[:n_more], refs[n_more], refs[n_more + 1 : -5]
+    panel_ref, points_ref, p32, pwide, sems = refs[-5:]
+    inv_ref, scale_ref = more[:2]
+    din, depth = points_ref.shape
+    order = (2, 3, 0, 1, 4, 5, 6, 7)
+    targets = (panel_ref, inv_ref, points_ref, *more[1:])
+    copies = fetch([sources[i] for i in order], [targets[i] for i in order], sems)
     rows = panel_ref.shape[0] // n_col
     me = lax.axis_index("col")
+    p32[...] = jnp.zeros_like(p32)
     for c in copies[:2]:
+        c.wait()
+    inverse = 1.0 / column(scale_ref[...])
+    p32[:din, :] = (points_ref[...] - 0.5) * inverse
+    p = p32[...]
+    first, second, third = split3(p)
+    for g, part in enumerate((first, first, second, second, first, third)):
+        pwide[g * GROUP : (g + 1) * GROUP, :] = part
+    norm = -0.5 * jnp.sum(p * p, axis=0, keepdims=True)
+    minus = jnp.full_like(norm, -1.0)
+    pwide[6 * GROUP : 7 * GROUP, :] = pick_row((GROUP, depth), (minus, minus, minus) + split3(norm))
+    pwide[7 * GROUP :, :] = jnp.zeros((GROUP, depth), jnp.float32)
+    pt[...] = jnp.transpose(pwide[...]).astype(jnp.bfloat16)
+    for c in copies[2:4]:
         c.wait()
     inv = inv_ref[...]
     panel = panel_ref[...]
@@ -75,13 +93,15 @@
             out_refs[d][...] = part[d * rows : (d + 1) * rows].astype(out_refs[d].dtype)
     else:
         out_refs[0][...] = part.reshape(out_refs[0].shape).astype(out_refs[0].dtype)
-    for c in copies[2:]:
+    for c in copies[4:]:
         c.wait()
 
 
 def partial(panel, inv, more, n_col, swapped):
     rows, width = panel.shape[0] // n_col, panel.shape[1]
-    shapes = [jax.ShapeDtypeStruct(x.shape, x.dtype) for x in (inv, *more)]
+    points = more[0]
+    shapes = [jax.ShapeDtypeStruct(x.shape, x.dtype) for x in (inv, *more[1:])]
+    shapes += [jax.ShapeDtypeStruct((points.shape[1], DEPTH), jnp.bfloat16)]
     if swapped:
         shapes += [jax.ShapeDtypeStruct((rows, width), jnp.float32 if d == 0 else LINK) for d in range(n_col)]
     else:
@@ -91,7 +111,13 @@
         out_shape=shapes,
         in_specs=[HBM] * (2 + len(more)),
         out_specs=[VMEM] * len(shapes),
-        scratch_shapes=[pltpu.VMEM(panel.shape, panel.dtype), pltpu.SemaphoreType.DMA((2 + len(more),))],
+        scratch_shapes=[
+            pltpu.VMEM(panel.shape, panel.dtype),
+            pltpu.VMEM(points.shape, points.dtype),
+            pltpu.VMEM((GROUP, points.shape[1]), jnp.float32),
+            pltpu.VMEM((DEPTH, points.shape[1]), jnp.float32),
+            pltpu.SemaphoreType.DMA((2 + len(more),)),
+        ],
         compiler_params=pltpu.CompilerParams(vmem_limit_bytes=16 * 2**20),
         name="partial",
     )(*in_hbm(panel, inv, *more))
@@ -99,26 +125,15 @@
 
 
 def columns_kernel(
-    tile, inv_ref, points_ref, scale_ref, target_ref, pick_ref, a_ref, b_ref,
-    k_ref, sums_ref, p32, pwide, pt, s32, st,
+    tile, inv_ref, scale_ref, target_ref, pick_ref, a_ref, b_ref, pt,
+    k_ref, sums_ref, s32, st,
 ):
-    din, depth = points_ref.shape
+    din, depth = a_ref.shape[0], pt.shape[0]
     wide = a_ref.shape[1]
     block = wide // pick_ref.shape[0]
-    p32[...] = jnp.zeros_like(p32)
     s32[...] = jnp.zeros_like(s32)
     st[...] = jnp.zeros_like(st)
     inverse = 1.0 / column(scale_ref[...])
-    p32[:din, :] = (points_ref[...] - 0.5) * inverse
-    p = p32[...]
-    first, second, third = split3(p)
-    for g, part in enumerate((first, first, second, second, first, third)):
-        pwide[g * GROUP : (g + 1) * GROUP, :] = part
-    norm = -0.5 * jnp.sum(p * p, axis=0, keepdims=True)
-    minus = jnp.full_like(norm, -1.0)
-    pwide[6 * GROUP : 7 * GROUP, :] = pick_row((GROUP, depth), (minus, minus, minus) + split3(norm))
-    pwide[7 * GROUP :, :] = jnp.zeros((GROUP, depth), jnp.float32)
-    pt[...] = jnp.transpose(pwide[...]).astype(jnp.bfloat16)
     weight = (
         jnp.sum(inv_ref[...].astype(jnp.float32) * target_ref[...].astype(jnp.float32).reshape(1, depth), axis=1, keepdims=True)
         .astype(jnp.bfloat16)
@@ -153,9 +168,9 @@
 
 
 def columns(ins):
-    inv, points, _, _, picks, base, _ = ins
-    depth, wide, blocks = points.shape[1], base.shape[1], picks.shape[0]
-    tile = wide // blocks * (2 if blocks % 2 == 0 else 1)
+    inv, _, _, picks, base, _, pt = ins
+    din, depth, wide, blocks = base.shape[0], pt.shape[0], base.shape[1], picks.shape[0]
+    tile = wide // blocks * (4 if blocks % 4 == 0 else 1)
     return pl.pallas_call(
         functools.partial(columns_kernel, tile),
         out_shape=[
@@ -165,9 +180,6 @@
         in_specs=[VMEM] * len(ins),
         out_specs=[VMEM] * 2,
         scratch_shapes=[
-            pltpu.VMEM((GROUP, depth), jnp.float32),
-            pltpu.VMEM((DEPTH, depth), jnp.float32),
-            pltpu.VMEM((depth, DEPTH), jnp.bfloat16),
             pltpu.VMEM((GROUP, tile), jnp.float32),
             pltpu.VMEM((DEPTH, tile), jnp.bfloat16),
         ],

time: 25.5 us -> 25.5 us (level)
  no operation moved by 1% of the time
where the time goes in v6:
time: 25.5 us; the launch traced here: 25.3 us
  starting transfers between devices  13.6 us (53%)
  Pallas kernels  8.23 us (32%)
  waiting for transfers between devices  2.63 us (10%)
  between operations  0.76 us (3%)
    ppermute x10, starting transfers between devices, swap(): lax.ppermute(x, axis, [(i, i ^ d) for i in range(lax.axis_size(axis))])  13.6 us
    pallas_call x1, Pallas kernels, columns(): pl.pallas_call(functools.partial(columns_kernel, tile), out_shape=[jax.Sh...  3.79 us
    ppermute x10, waiting for transfers between devices, swap(): lax.ppermute(x, axis, [(i, i ^ d) for i in range(lax.axis_size(axis))])  2.63 us
    pallas_call x1, Pallas kernels, update(): pl.pallas_call(functools.partial(update_kernel, places, cuts, len(blocks)...  1.96 us
    pallas_call x1, Pallas kernels, partial(): pl.pallas_call(functools.partial(partial_kernel, n_col, swapped, len(more...  1.87 us
    pallas_call x1, Pallas kernels, finish(): pl.pallas_call(finish_kernel, out_shape=[flat, flat], in_specs=[VMEM] * (...  0.62 us
  transfers between devices with their start and end apart: 10, of which 3 were waited for; matrix products, arithmetic and copies ran while one was open for 0% of the time, Pallas kernels for 23%

profile of v6, /device:TPU:0, one launch (start us, length us, event | category | flops | bytes accessed | tf_op | source)
XLA Modules:
  0.0 25.3 jit_solution(5889270131657658993)
XLA Ops:
  0.6 1.9 %partial.1 = (bf16[256,1024]{1,0:T(8,128)(2,1)S(1)}, f32[1,20]{1,0:T(1,128)S(1)}, bf16[1024]{0:T(1024)(128)(2,1)S(1)}, s32[12,20]{1,0:T(8,128)S(1)}, f32[20,3072...) custom-call(bf16[64,1024]{1,0:T(8,128)(2,1)} %refs_6_.3, ...), custom_call_target="tpu_custom_call" | custom-call | tf_op jit(solution)/shard_map/partial/pallas_call | solution.py:109
  2.5 0.0 copy-start
  2.5 0.0 copy-start.1
  2.5 0.0 copy-start.2
  2.5 4.1 %collective-permute-start = (bf16[16,1024]{1,0:T(8,128)(2,1)S(1)}, bf16[16,1024]{1,0:T(8,128)(2,1)S(1)}, u32[]{:S(2)}, u32[]{:S(2)}) collective-permute-start(bf16[16,1024]{1,0:T(8,128)(2,1)S(1)} %get-tuple-element.32), channel_id=1, source_target_pairs={{0,2},{1,3},{2,0},{3,1},{4,6},{5,7},{6,4},{7,5},{8,10},{9,11},{10,... | collective-permute-start | bytes 98312 | tf_op jit(solution)/shard_map/ppermute | solution.py:271
  6.6 1.3 %collective-permute-start.1 = (bf16[16,1024]{1,0:T(8,128)(2,1)S(1)}, bf16[16,1024]{1,0:T(8,128)(2,1)S(1)}, u32[]{:S(2)}, u32[]{:S(2)}) collective-permute-start(bf16[16,1024]{1,0:T(8,128)(2,1)S(1)} %get-tuple-element.33), channel_id=1, source_target_pairs={{0,3},{1,2},{2,1},{3,0},{4,7},{5,6},{6,5},{7,4},{8,11},{9,10},{10,... | collective-permute-start | bytes 98312 | tf_op jit(solution)/shard_map/ppermute | solution.py:271
  8.0 0.2 collective-permute-start.2
  8.2 3.8 %columns.1 = (bf16[1024,3072]{1,0:T(8,128)(2,1)S(1)}, f32[2,3072]{1,0:T(2,128)S(1)}) custom-call(bf16[256,1024]{1,0:T(8,128)(2,1)S(1)} %get-tuple-element.35.inv_ref, f32[1,20]{1,0:T(1,128)S(1)} %get-tuple-element.36.scale_ref, bf16[1024]{0:T(1024)(128)(2,1)S(1)} %get-tuple-element.37.target_ref, s32[12,20]{1,0:T(8,128)S(1)} %get-tuple-element.38.pick_ref, ...), custom_call_target="tpu_custom_call" | custom-call | flops 3221225472 | bytes 6291456 | tf_op jit(solution)/shard_map/columns/pallas_call | solution.py:174
  12.0 0.0 copy-start.3
  12.0 0.0 copy-start.4
  12.1 0.3 %collective-permute-done.1 = bf16[16,1024]{1,0:T(8,128)(2,1)S(1)} collective-permute-done((bf16[16,1024]{1,0:T(8,128)(2,1)S(1)}, bf16[16,1024]{1,0:T(8,128)(2,1)S(1)}, u32[]{:S(2)}, u32[]{:S(2)}) %collective-permute-start.1) | collective-permute-done | bytes 32800 | tf_op jit(solution)/shard_map/ppermute | solution.py:271
  12.4 0.1 collective-permute-start.3
  12.5 1.2 %collective-permute-done.3 = bf16[16,1024]{1,0:T(8,128)(2,1)S(1)} collective-permute-done((bf16[16,1024]{1,0:T(8,128)(2,1)S(1)}, bf16[16,1024]{1,0:T(8,128)(2,1)S(1)}, u32[]{:S(2)}, u32[]{:S(2)}) %collective-permute-start.3) | collective-permute-done | bytes 32800 | tf_op jit(solution)/shard_map/ppermute | solution.py:271
  13.7 2.4 %collective-permute-start.6 = (bf16[32,1024]{1,0:T(8,128)(2,1)S(1)}, bf16[32,1024]{1,0:T(8,128)(2,1)S(1)}, u32[]{:S(2)}, u32[]{:S(2)}) collective-permute-start(bf16[32,1024]{1,0:T(8,128)(2,1)S(1)} %pad_maximum_fusion.refs_0_), channel_id=1, source_target_pairs={{0,24},{4,28},{8,16},{12,20},{16,8},{20,12},{24,0},{28,4},{1,25},{... | collective-permute-start | bytes 196616 | tf_op jit(solution)/shard_map/ppermute | solution.py:271
  16.1 0.5 %collective-permute-start.5 = (bf16[32,1024]{1,0:T(8,128)(2,1)S(1)}, bf16[32,1024]{1,0:T(8,128)(2,1)S(1)}, u32[]{:S(2)}, u32[]{:S(2)}) collective-permute-start(bf16[32,1024]{1,0:T(8,128)(2,1)S(1)} %pad_maximum_fusion.refs_0_), channel_id=1, source_target_pairs={{0,16},{4,20},{8,24},{12,28},{16,0},{20,4},{24,8},{28,12},{1,17},{... | collective-permute-start | bytes 196616 | tf_op jit(solution)/shard_map/ppermute | solution.py:271
  16.6 0.5 %collective-permute-start.4 = (bf16[32,1024]{1,0:T(8,128)(2,1)S(1)}, bf16[32,1024]{1,0:T(8,128)(2,1)S(1)}, u32[]{:S(2)}, u32[]{:S(2)}) collective-permute-start(bf16[32,1024]{1,0:T(8,128)(2,1)S(1)} %pad_maximum_fusion.refs_0_), channel_id=1, source_target_pairs={{0,8},{4,12},{8,0},{12,4},{16,24},{20,28},{24,16},{28,20},{1,9},{5... | collective-permute-start | bytes 196616 | tf_op jit(solution)/shard_map/ppermute | solution.py:271
  17.2 2.6 %collective-permute-start.9 = (f32[2,3072]{1,0:T(2,128)S(1)}, f32[2,3072]{1,0:T(2,128)S(1)}, u32[]{:S(2)}, u32[]{:S(2)}) collective-permute-start(f32[2,3072]{1,0:T(2,128)S(1)} %get-tuple-element.52.refs_0_), channel_id=1, source_target_pairs={{0,3},{1,2},{2,1},{3,0},{4,7},{5,6},{6,5},{7,4},{8,11},{9,10},{10,... | collective-permute-start | bytes 73736 | tf_op jit(solution)/shard_map/ppermute | solution.py:271
  19.8 0.3 %collective-permute-start.8 = (f32[2,3072]{1,0:T(2,128)S(1)}, f32[2,3072]{1,0:T(2,128)S(1)}, u32[]{:S(2)}, u32[]{:S(2)}) collective-permute-start(f32[2,3072]{1,0:T(2,128)S(1)} %get-tuple-element.52.refs_0_), channel_id=1, source_target_pairs={{0,2},{1,3},{2,0},{3,1},{4,6},{5,7},{6,4},{7,5},{8,10},{9,11},{10,... | collective-permute-start | bytes 73736 | tf_op jit(solution)/shard_map/ppermute | solution.py:271
  20.1 0.0 collective-permute-done.6.refs_3_
  20.1 1.4 %collective-permute-start.7 = (f32[2,3072]{1,0:T(2,128)S(1)}, f32[2,3072]{1,0:T(2,128)S(1)}, u32[]{:S(2)}, u32[]{:S(2)}) collective-permute-start(f32[2,3072]{1,0:T(2,128)S(1)} %get-tuple-element.52.refs_0_), channel_id=1, source_target_pairs={{0,1},{1,0},{2,3},{3,2},{4,5},{5,4},{6,7},{7,6},{8,9},{9,8},{10,11... | collective-permute-start | bytes 73736 | tf_op jit(solution)/shard_map/ppermute | solution.py:271
  21.6 2.0 %update.1 = (bf16[128,3072]{1,0:T(8,128)(2,1)}, f32[64,128]{1,0:T(8,128)}) custom-call(bf16[32,1024]{1,0:T(8,128)(2,1)S(1)} %pad_maximum_fusion.refs_0_, bf16[32,1024]{1,0:T(8,128)(2,1)S(1)} %collective-permute-done.4.refs_1_, bf16[32,1024]{1,0:T(8,128)(2,1)S(1)} %collective-permute-done.5.refs_2_, bf16[32,1024]{1,0:T(8,128)(2,1)S(1)} %collective-permute-done.6.refs_3_, ...), custom_call_target="tpu_custom_call" | custom-call | flops 805306368 | bytes 6291456 | tf_op jit(solution)/shard_map/update/pallas_call | solution.py:225
  23.6 1.1 %collective-permute-done.8.refs_2_ = f32[2,3072]{1,0:T(2,128)S(1)} collective-permute-done((f32[2,3072]{1,0:T(2,128)S(1)}, f32[2,3072]{1,0:T(2,128)S(1)}, u32[]{:S(2)}, u32[]{:S(2)}) %collective-permute-start.8) | collective-permute-done | bytes 24608 | tf_op jit(solution)/shard_map/ppermute | solution.py:271
  24.7 0.0 collective-permute-done.7.refs_1_
  24.7 0.6 %finish.1 = (f32[1,3072]{1,0:T(1,128)}, f32[1,3072]{1,0:T(1,128)}) custom-call(f32[2,3072]{1,0:T(2,128)S(1)} %get-tuple-element.52.refs_0_, f32[2,3072]{1,0:T(2,128)S(1)} %collective-permute-done.7.refs_1_, f32[2,3072]{1,0:T(2,128)S(1)} %collective-permute-done.8.refs_2_, f32[2,3072]{1,0:T(2,128)S(1)} %collective-permute-done.9.refs_3_, ...), custom_call_target="tpu_custom_call" | custom-call | tf_op jit(solution)/shard_map/finish/pallas_call | solution.py:259
  (12 shorter events, 0.1 us)
Async XLA Ops:
  2.5 19.1 %copy-start = (bf16[128,3072]{1,0:T(8,128)(2,1)S(1)}, bf16[128,3072]{1,0:T(8,128)(2,1)}, u32[]{:S(2)}) copy-start(bf16[128,3072]{1,0:T(8,128)(2,1)} %refs_5_.3) | copy-start | bytes 2359300
  2.5 19.0 %copy-start.1 = (bf16[64,1024]{1,0:T(8,128)(2,1)S(1)}, bf16[64,1024]{1,0:T(8,128)(2,1)}, u32[]{:S(2)}) copy-start(bf16[64,1024]{1,0:T(8,128)(2,1)} %refs_6_.3) | copy-start | bytes 393220
  2.5 19.0 %copy-start.2 = (f32[64,128]{1,0:T(8,128)S(1)}, f32[64,128]{1,0:T(8,128)}, u32[]{:S(2)}) copy-start(f32[64,128]{1,0:T(8,128)} %refs_7_.3) | copy-start | bytes 98308
  2.5 9.5 %collective-permute-start = (bf16[16,1024]{1,0:T(8,128)(2,1)S(1)}, bf16[16,1024]{1,0:T(8,128)(2,1)S(1)}, u32[]{:S(2)}, u32[]{:S(2)}) collective-permute-start(bf16[16,1024]{1,0:T(8,128)(2,1)S(1)} %get-tuple-element.32), channel_id=1, source_target_pairs={{0,2},{1,3},{2,0},{3,1},{4,6},{5,7},{6,4},{7,5},{8,10},{9,11},{10,... | collective-permute-start | bytes 98312 | tf_op jit(solution)/shard_map/ppermute | solution.py:271
  6.6 5.7 %collective-permute-start.1 = (bf16[16,1024]{1,0:T(8,128)(2,1)S(1)}, bf16[16,1024]{1,0:T(8,128)(2,1)S(1)}, u32[]{:S(2)}, u32[]{:S(2)}) collective-permute-start(bf16[16,1024]{1,0:T(8,128)(2,1)S(1)} %get-tuple-element.33), channel_id=1, source_target_pairs={{0,3},{1,2},{2,1},{3,0},{4,7},{5,6},{6,5},{7,4},{8,11},{9,10},{10,... | collective-permute-start | bytes 98312 | tf_op jit(solution)/shard_map/ppermute | solution.py:271
  8.0 4.4 %collective-permute-start.2 = (bf16[16,1024]{1,0:T(8,128)(2,1)S(1)}, bf16[16,1024]{1,0:T(8,128)(2,1)S(1)}, u32[]{:S(2)}, u32[]{:S(2)}) collective-permute-start(bf16[16,1024]{1,0:T(8,128)(2,1)S(1)} %get-tuple-element.34), channel_id=1, source_target_pairs={{0,1},{1,0},{2,3},{3,2},{4,5},{5,4},{6,7},{7,6},{8,9},{9,8},{10,11... | collective-permute-start | bytes 98312 | tf_op jit(solution)/shard_map/ppermute | solution.py:271
  12.0 12.7 %copy-start.3 = (f32[3072]{0:T(1024)S(1)}, f32[3072]{0:T(1024)}, u32[]{:S(2)}) copy-start(f32[3072]{0:T(1024)} %param.22) | copy-start | bytes 36868
  12.0 12.6 %copy-start.4 = (f32[3072]{0:T(1024)S(1)}, f32[3072]{0:T(1024)}, u32[]{:S(2)}) copy-start(f32[3072]{0:T(1024)} %param.23) | copy-start | bytes 36868
  12.4 1.3 %collective-permute-start.3 = (bf16[16,1024]{1,0:T(8,128)(2,1)S(1)}, bf16[16,1024]{1,0:T(8,128)(2,1)S(1)}, u32[]{:S(2)}, u32[]{:S(2)}) collective-permute-start(bf16[16,1024]{1,0:T(8,128)(2,1)S(1)} %add_convert_fusion), channel_id=1, source_target_pairs={{0,4},{4,0},{8,12},{12,8},{16,20},{20,16},{24,28},{28,24},{1,5},{5... | collective-permute-start | bytes 98312 | tf_op jit(solution)/shard_map/ppermute | solution.py:271
  13.7 6.5 %collective-permute-start.6 = (bf16[32,1024]{1,0:T(8,128)(2,1)S(1)}, bf16[32,1024]{1,0:T(8,128)(2,1)S(1)}, u32[]{:S(2)}, u32[]{:S(2)}) collective-permute-start(bf16[32,1024]{1,0:T(8,128)(2,1)S(1)} %pad_maximum_fusion.refs_0_), channel_id=1, source_target_pairs={{0,24},{4,28},{8,16},{12,20},{16,8},{20,12},{24,0},{28,4},{1,25},{... | collective-permute-start | bytes 196616 | tf_op jit(solution)/shard_map/ppermute | solution.py:271
  16.1 5.4 %collective-permute-start.5 = (bf16[32,1024]{1,0:T(8,128)(2,1)S(1)}, bf16[32,1024]{1,0:T(8,128)(2,1)S(1)}, u32[]{:S(2)}, u32[]{:S(2)}) collective-permute-start(bf16[32,1024]{1,0:T(8,128)(2,1)S(1)} %pad_maximum_fusion.refs_0_), channel_id=1, source_target_pairs={{0,16},{4,20},{8,24},{12,28},{16,0},{20,4},{24,8},{28,12},{1,17},{... | collective-permute-start | bytes 196616 | tf_op jit(solution)/shard_map/ppermute | solution.py:271
  16.6 4.9 %collective-permute-start.4 = (bf16[32,1024]{1,0:T(8,128)(2,1)S(1)}, bf16[32,1024]{1,0:T(8,128)(2,1)S(1)}, u32[]{:S(2)}, u32[]{:S(2)}) collective-permute-start(bf16[32,1024]{1,0:T(8,128)(2,1)S(1)} %pad_maximum_fusion.refs_0_), channel_id=1, source_target_pairs={{0,8},{4,12},{8,0},{12,4},{16,24},{20,28},{24,16},{28,20},{1,9},{5... | collective-permute-start | bytes 196616 | tf_op jit(solution)/shard_map/ppermute | solution.py:271
  17.2 6.4 %collective-permute-start.9 = (f32[2,3072]{1,0:T(2,128)S(1)}, f32[2,3072]{1,0:T(2,128)S(1)}, u32[]{:S(2)}, u32[]{:S(2)}) collective-permute-start(f32[2,3072]{1,0:T(2,128)S(1)} %get-tuple-element.52.refs_0_), channel_id=1, source_target_pairs={{0,3},{1,2},{2,1},{3,0},{4,7},{5,6},{6,5},{7,4},{8,11},{9,10},{10,... | collective-permute-start | bytes 73736 | tf_op jit(solution)/shard_map/ppermute | solution.py:271
  19.8 4.9 %collective-permute-start.8 = (f32[2,3072]{1,0:T(2,128)S(1)}, f32[2,3072]{1,0:T(2,128)S(1)}, u32[]{:S(2)}, u32[]{:S(2)}) collective-permute-start(f32[2,3072]{1,0:T(2,128)S(1)} %get-tuple-element.52.refs_0_), channel_id=1, source_target_pairs={{0,2},{1,3},{2,0},{3,1},{4,6},{5,7},{6,4},{7,5},{8,10},{9,11},{10,... | collective-permute-start | bytes 73736 | tf_op jit(solution)/shard_map/ppermute | solution.py:271
  20.1 4.5 %collective-permute-start.7 = (f32[2,3072]{1,0:T(2,128)S(1)}, f32[2,3072]{1,0:T(2,128)S(1)}, u32[]{:S(2)}, u32[]{:S(2)}) collective-permute-start(f32[2,3072]{1,0:T(2,128)S(1)} %get-tuple-element.52.refs_0_), channel_id=1, source_target_pairs={{0,1},{1,0},{2,3},{3,2},{4,5},{5,4},{6,7},{7,6},{8,9},{9,8},{10,11... | collective-permute-start | bytes 73736 | tf_op jit(solution)/shard_map/ppermute | solution.py:271

commit v7 on v6

--- a/solution.py
+++ b/solution.py
@@ -23,6 +23,10 @@
     for c in copies:
         c.start()
     return copies
+
+
+def turns(n_col):
+    return [tuple(d for d in order if d < n_col) for order in ((2, 3, 1), (3, 1, 2))]
 
 
 def tile_of(n, most):
@@ -83,7 +87,9 @@
     inv = inv_ref[...]
     panel = panel_ref[...]
     if swapped:
-        panel = jnp.concatenate([panel_ref[pl.ds((me ^ d) * rows, rows), :] for d in range(n_col)], axis=0)
+        odd = lax.axis_index("row") % 2
+        steps = [0] + [jnp.where(odd == 1, b, a) for a, b in zip(*turns(n_col))]
+        panel = jnp.concatenate([panel_ref[pl.ds((me ^ d) * rows, rows), :] for d in steps], axis=0)
     slab = lax.dot_general(
         panel, inv, (((1,), (1,)), ((), ())), preferred_element_type=jnp.float32
     ).astype(jnp.bfloat16)
@@ -219,7 +225,7 @@
 def update(blocks, places, k, rhs, panel, trailing):
     depth, wide = k.shape
     rows = rhs.shape[0]
-    tile = tile_of(wide, 512)
+    tile = tile_of(wide, 1024)
     edges = list(range(0, wide, tile)) + [wide - tile // 2, wide]
     cuts = list(zip(edges, edges[1:]))
     return pl.pallas_call(
@@ -265,6 +271,12 @@
         name="finish",
     )(*parts, mean.reshape(1, wide), var.reshape(1, wide))
     return out_mean.reshape(wide), out_var.reshape(wide)
+
+
+def meet(x, a, b):
+    n_row, n_col = lax.axis_size("row"), lax.axis_size("col")
+    pairs = [(r * n_col + c, r * n_col + (c ^ (b if r % 2 else a))) for r in range(n_row) for c in range(n_col)]
+    return lax.ppermute(x, ("row", "col"), pairs)
 
 
 def swap(x, axis, d):
@@ -290,7 +302,7 @@
     more = (panel_points, lengthscales.reshape(1, -1), targets, pick_sets, base_a, base_b)
     ins, parts = partial(panel_block, diag_inverse, more, n_col, near)
     if near:
-        got = [swap(parts[d], "col", d) for d in (2, 3, 1) if d < n_col]
+        got = [meet(x, a, b) for x, a, b in zip(parts[1:], *turns(n_col))]
     k, sums = columns(ins)
     if near:
         got, k, sums = lax.optimization_barrier((got, k, sums))

time: 25.5 us -> 25.5 us (level)
    ppermute x0 -> x3, starting transfers between devices: none -> 5.68 us  [meet(): return lax.ppermute(x, ('row', 'col'), pairs)]
    ppermute x10 -> x7, starting transfers between devices: 13.6 us -> 7.95 us  [swap(): lax.ppermute(x, axis, [(i, i ^ d) for i in range(lax.axis_size(axis))])]
    ppermute x0 -> x3, waiting for transfers between devices: none -> 0.54 us  [meet(): return lax.ppermute(x, ('row', 'col'), pairs)]
    ppermute x10 -> x7, waiting for transfers between devices: 2.63 us -> 2.19 us  [swap(): lax.ppermute(x, axis, [(i, i ^ d) for i in range(lax.axis_size(axis))])]
  transfers between devices with their start and end apart: 10 -> 10, of which waited for: 3 -> 3; matrix products, arithmetic and copies ran while one was open for 0% -> 0% of each run, Pallas kernels for 23% -> 22%
where the time goes in v7:
time: 25.5 us; the launch traced here: 25.3 us
  starting transfers between devices  13.6 us (53%)
  Pallas kernels  8.14 us (32%)
  waiting for transfers between devices  2.73 us (11%)
  between operations  0.76 us (3%)
    ppermute x7, starting transfers between devices, swap(): lax.ppermute(x, axis, [(i, i ^ d) for i in range(lax.axis_size(axis))])  7.95 us
    ppermute x3, starting transfers between devices, meet(): return lax.ppermute(x, ('row', 'col'), pairs)  5.68 us
    pallas_call x1, Pallas kernels, columns(): pl.pallas_call(functools.partial(columns_kernel, tile), out_shape=[jax.Sh...  3.79 us
    ppermute x7, waiting for transfers between devices, swap(): lax.ppermute(x, axis, [(i, i ^ d) for i in range(lax.axis_size(axis))])  2.19 us
    pallas_call x1, Pallas kernels, partial(): pl.pallas_call(functools.partial(partial_kernel, n_col, swapped, len(more...  1.87 us
    pallas_call x1, Pallas kernels, update(): pl.pallas_call(functools.partial(update_kernel, places, cuts, len(blocks)...  1.86 us
    pallas_call x1, Pallas kernels, finish(): pl.pallas_call(finish_kernel, out_shape=[flat, flat], in_specs=[VMEM] * (...  0.62 us
    ppermute x3, waiting for transfers between devices, meet(): return lax.ppermute(x, ('row', 'col'), pairs)  0.54 us
  transfers between devices with their start and end apart: 10, of which 3 were waited for; matrix products, arithmetic and copies ran while one was open for 0% of the time, Pallas kernels for 22%

profile of v7, /device:TPU:0, one launch (start us, length us, event | category | flops | bytes accessed | tf_op | source)
XLA Modules:
  0.0 25.3 jit_solution(7556488754702136475)
XLA Ops:
  0.6 1.9 %partial.1 = (bf16[256,1024]{1,0:T(8,128)(2,1)S(1)}, f32[1,20]{1,0:T(1,128)S(1)}, bf16[1024]{0:T(1024)(128)(2,1)S(1)}, s32[12,20]{1,0:T(8,128)S(1)}, f32[20,3072...) custom-call(bf16[64,1024]{1,0:T(8,128)(2,1)} %refs_6_.3, ...), custom_call_target="tpu_custom_call" | custom-call | tf_op jit(solution)/shard_map/partial/pallas_call | solution.py:115
  2.5 0.0 copy-start
  2.5 0.0 copy-start.1
  2.5 0.0 copy-start.2
  2.5 4.1 %collective-permute-start = (bf16[16,1024]{1,0:T(8,128)(2,1)S(1)}, bf16[16,1024]{1,0:T(8,128)(2,1)S(1)}, u32[]{:S(2)}, u32[]{:S(2)}) collective-permute-start(bf16[16,1024]{1,0:T(8,128)(2,1)S(1)} %get-tuple-element.32), channel_id=1, source_target_pairs={{0,2},{1,3},{2,0},{3,1},{4,7},{5,6},{6,5},{7,4},{8,10},{9,11},{10,... | collective-permute-start | bytes 98312 | tf_op jit(solution)/shard_map/ppermute | solution.py:279
  6.6 1.3 %collective-permute-start.1 = (bf16[16,1024]{1,0:T(8,128)(2,1)S(1)}, bf16[16,1024]{1,0:T(8,128)(2,1)S(1)}, u32[]{:S(2)}, u32[]{:S(2)}) collective-permute-start(bf16[16,1024]{1,0:T(8,128)(2,1)S(1)} %get-tuple-element.33), channel_id=1, source_target_pairs={{0,3},{1,2},{2,1},{3,0},{4,5},{5,4},{6,7},{7,6},{8,11},{9,10},{10,... | collective-permute-start | bytes 98312 | tf_op jit(solution)/shard_map/ppermute | solution.py:279
  8.0 0.2 collective-permute-start.2
  8.2 3.8 %columns.1 = (bf16[1024,3072]{1,0:T(8,128)(2,1)S(1)}, f32[2,3072]{1,0:T(2,128)S(1)}) custom-call(bf16[256,1024]{1,0:T(8,128)(2,1)S(1)} %get-tuple-element.35.inv_ref, f32[1,20]{1,0:T(1,128)S(1)} %get-tuple-element.36.scale_ref, bf16[1024]{0:T(1024)(128)(2,1)S(1)} %get-tuple-element.37.target_ref, s32[12,20]{1,0:T(8,128)S(1)} %get-tuple-element.38.pick_ref, ...), custom_call_target="tpu_custom_call" | custom-call | flops 3221225472 | bytes 6291456 | tf_op jit(solution)/shard_map/columns/pallas_call | solution.py:180
  12.0 0.0 copy-start.3
  12.0 0.0 copy-start.4
  12.1 0.5 %collective-permute-done.1 = bf16[16,1024]{1,0:T(8,128)(2,1)S(1)} collective-permute-done((bf16[16,1024]{1,0:T(8,128)(2,1)S(1)}, bf16[16,1024]{1,0:T(8,128)(2,1)S(1)}, u32[]{:S(2)}, u32[]{:S(2)}) %collective-permute-start.1) | collective-permute-done | bytes 32800 | tf_op jit(solution)/shard_map/ppermute | solution.py:279
  12.6 0.1 collective-permute-start.3
  12.7 1.2 %collective-permute-done.3 = bf16[16,1024]{1,0:T(8,128)(2,1)S(1)} collective-permute-done((bf16[16,1024]{1,0:T(8,128)(2,1)S(1)}, bf16[16,1024]{1,0:T(8,128)(2,1)S(1)}, u32[]{:S(2)}, u32[]{:S(2)}) %collective-permute-start.3) | collective-permute-done | bytes 32800 | tf_op jit(solution)/shard_map/ppermute | solution.py:283
  13.9 2.4 %collective-permute-start.6 = (bf16[32,1024]{1,0:T(8,128)(2,1)S(1)}, bf16[32,1024]{1,0:T(8,128)(2,1)S(1)}, u32[]{:S(2)}, u32[]{:S(2)}) collective-permute-start(bf16[32,1024]{1,0:T(8,128)(2,1)S(1)} %pad_maximum_fusion.refs_0_), channel_id=1, source_target_pairs={{0,24},{4,28},{8,16},{12,20},{16,8},{20,12},{24,0},{28,4},{1,25},{... | collective-permute-start | bytes 196616 | tf_op jit(solution)/shard_map/ppermute | solution.py:283
  16.3 0.5 %collective-permute-start.5 = (bf16[32,1024]{1,0:T(8,128)(2,1)S(1)}, bf16[32,1024]{1,0:T(8,128)(2,1)S(1)}, u32[]{:S(2)}, u32[]{:S(2)}) collective-permute-start(bf16[32,1024]{1,0:T(8,128)(2,1)S(1)} %pad_maximum_fusion.refs_0_), channel_id=1, source_target_pairs={{0,16},{4,20},{8,24},{12,28},{16,0},{20,4},{24,8},{28,12},{1,17},{... | collective-permute-start | bytes 196616 | tf_op jit(solution)/shard_map/ppermute | solution.py:283
  16.9 0.5 %collective-permute-start.4 = (bf16[32,1024]{1,0:T(8,128)(2,1)S(1)}, bf16[32,1024]{1,0:T(8,128)(2,1)S(1)}, u32[]{:S(2)}, u32[]{:S(2)}) collective-permute-start(bf16[32,1024]{1,0:T(8,128)(2,1)S(1)} %pad_maximum_fusion.refs_0_), channel_id=1, source_target_pairs={{0,8},{4,12},{8,0},{12,4},{16,24},{20,28},{24,16},{28,20},{1,9},{5... | collective-permute-start | bytes 196616 | tf_op jit(solution)/shard_map/ppermute | solution.py:283
  17.4 2.4 %collective-permute-start.9 = (f32[2,3072]{1,0:T(2,128)S(1)}, f32[2,3072]{1,0:T(2,128)S(1)}, u32[]{:S(2)}, u32[]{:S(2)}) collective-permute-start(f32[2,3072]{1,0:T(2,128)S(1)} %get-tuple-element.52.refs_0_), channel_id=1, source_target_pairs={{0,3},{1,2},{2,1},{3,0},{4,7},{5,6},{6,5},{7,4},{8,11},{9,10},{10,... | collective-permute-start | bytes 73736 | tf_op jit(solution)/shard_map/ppermute | solution.py:283
  19.8 0.3 %collective-permute-start.8 = (f32[2,3072]{1,0:T(2,128)S(1)}, f32[2,3072]{1,0:T(2,128)S(1)}, u32[]{:S(2)}, u32[]{:S(2)}) collective-permute-start(f32[2,3072]{1,0:T(2,128)S(1)} %get-tuple-element.52.refs_0_), channel_id=1, source_target_pairs={{0,2},{1,3},{2,0},{3,1},{4,6},{5,7},{6,4},{7,5},{8,10},{9,11},{10,... | collective-permute-start | bytes 73736 | tf_op jit(solution)/shard_map/ppermute | solution.py:283
  20.1 0.0 collective-permute-done.6.refs_3_
  20.1 1.6 %collective-permute-start.7 = (f32[2,3072]{1,0:T(2,128)S(1)}, f32[2,3072]{1,0:T(2,128)S(1)}, u32[]{:S(2)}, u32[]{:S(2)}) collective-permute-start(f32[2,3072]{1,0:T(2,128)S(1)} %get-tuple-element.52.refs_0_), channel_id=1, source_target_pairs={{0,1},{1,0},{2,3},{3,2},{4,5},{5,4},{6,7},{7,6},{8,9},{9,8},{10,11... | collective-permute-start | bytes 73736 | tf_op jit(solution)/shard_map/ppermute | solution.py:283
  21.8 0.0 collective-permute-done.5.refs_2_
  21.8 1.9 %update.1 = (bf16[128,3072]{1,0:T(8,128)(2,1)}, f32[64,128]{1,0:T(8,128)}) custom-call(bf16[32,1024]{1,0:T(8,128)(2,1)S(1)} %pad_maximum_fusion.refs_0_, bf16[32,1024]{1,0:T(8,128)(2,1)S(1)} %collective-permute-done.4.refs_1_, bf16[32,1024]{1,0:T(8,128)(2,1)S(1)} %collective-permute-done.5.refs_2_, bf16[32,1024]{1,0:T(8,128)(2,1)S(1)} %collective-permute-done.6.refs_3_, ...), custom_call_target="tpu_custom_call" | custom-call | flops 805306368 | bytes 6291456 | tf_op jit(solution)/shard_map/update/pallas_call | solution.py:231
  23.7 1.0 %collective-permute-done.8.refs_2_ = f32[2,3072]{1,0:T(2,128)S(1)} collective-permute-done((f32[2,3072]{1,0:T(2,128)S(1)}, f32[2,3072]{1,0:T(2,128)S(1)}, u32[]{:S(2)}, u32[]{:S(2)}) %collective-permute-start.8) | collective-permute-done | bytes 24608 | tf_op jit(solution)/shard_map/ppermute | solution.py:283
  24.7 0.6 %finish.1 = (f32[1,3072]{1,0:T(1,128)}, f32[1,3072]{1,0:T(1,128)}) custom-call(f32[2,3072]{1,0:T(2,128)S(1)} %get-tuple-element.52.refs_0_, f32[2,3072]{1,0:T(2,128)S(1)} %collective-permute-done.7.refs_1_, f32[2,3072]{1,0:T(2,128)S(1)} %collective-permute-done.8.refs_2_, f32[2,3072]{1,0:T(2,128)S(1)} %collective-permute-done.9.refs_3_, ...), custom_call_target="tpu_custom_call" | custom-call | tf_op jit(solution)/shard_map/finish/pallas_call | solution.py:265
  (12 shorter events, 0.1 us)
Async XLA Ops:
  2.5 19.3 %copy-start = (bf16[128,3072]{1,0:T(8,128)(2,1)S(1)}, bf16[128,3072]{1,0:T(8,128)(2,1)}, u32[]{:S(2)}) copy-start(bf16[128,3072]{1,0:T(8,128)(2,1)} %refs_5_.3) | copy-start | bytes 2359300
  2.5 19.3 %copy-start.1 = (bf16[64,1024]{1,0:T(8,128)(2,1)S(1)}, bf16[64,1024]{1,0:T(8,128)(2,1)}, u32[]{:S(2)}) copy-start(bf16[64,1024]{1,0:T(8,128)(2,1)} %refs_6_.3) | copy-start | bytes 393220
  2.5 19.3 %copy-start.2 = (f32[64,128]{1,0:T(8,128)S(1)}, f32[64,128]{1,0:T(8,128)}, u32[]{:S(2)}) copy-start(f32[64,128]{1,0:T(8,128)} %refs_7_.3) | copy-start | bytes 98308
  2.5 9.5 %collective-permute-start = (bf16[16,1024]{1,0:T(8,128)(2,1)S(1)}, bf16[16,1024]{1,0:T(8,128)(2,1)S(1)}, u32[]{:S(2)}, u32[]{:S(2)}) collective-permute-start(bf16[16,1024]{1,0:T(8,128)(2,1)S(1)} %get-tuple-element.32), channel_id=1, source_target_pairs={{0,2},{1,3},{2,0},{3,1},{4,7},{5,6},{6,5},{7,4},{8,10},{9,11},{10,... | collective-permute-start | bytes 98312 | tf_op jit(solution)/shard_map/ppermute | solution.py:279
  6.6 5.9 %collective-permute-start.1 = (bf16[16,1024]{1,0:T(8,128)(2,1)S(1)}, bf16[16,1024]{1,0:T(8,128)(2,1)S(1)}, u32[]{:S(2)}, u32[]{:S(2)}) collective-permute-start(bf16[16,1024]{1,0:T(8,128)(2,1)S(1)} %get-tuple-element.33), channel_id=1, source_target_pairs={{0,3},{1,2},{2,1},{3,0},{4,5},{5,4},{6,7},{7,6},{8,11},{9,10},{10,... | collective-permute-start | bytes 98312 | tf_op jit(solution)/shard_map/ppermute | solution.py:279
  8.0 4.6 %collective-permute-start.2 = (bf16[16,1024]{1,0:T(8,128)(2,1)S(1)}, bf16[16,1024]{1,0:T(8,128)(2,1)S(1)}, u32[]{:S(2)}, u32[]{:S(2)}) collective-permute-start(bf16[16,1024]{1,0:T(8,128)(2,1)S(1)} %get-tuple-element.34), channel_id=1, source_target_pairs={{0,1},{1,0},{2,3},{3,2},{4,6},{5,7},{6,4},{7,5},{8,9},{9,8},{10,11... | collective-permute-start | bytes 98312 | tf_op jit(solution)/shard_map/ppermute | solution.py:279
  12.0 12.7 %copy-start.3 = (f32[3072]{0:T(1024)S(1)}, f32[3072]{0:T(1024)}, u32[]{:S(2)}) copy-start(f32[3072]{0:T(1024)} %param.22) | copy-start | bytes 36868
  12.0 12.6 %copy-start.4 = (f32[3072]{0:T(1024)S(1)}, f32[3072]{0:T(1024)}, u32[]{:S(2)}) copy-start(f32[3072]{0:T(1024)} %param.23) | copy-start | bytes 36868
  12.6 1.3 %collective-permute-start.3 = (bf16[16,1024]{1,0:T(8,128)(2,1)S(1)}, bf16[16,1024]{1,0:T(8,128)(2,1)S(1)}, u32[]{:S(2)}, u32[]{:S(2)}) collective-permute-start(bf16[16,1024]{1,0:T(8,128)(2,1)S(1)} %add_convert_fusion), channel_id=1, source_target_pairs={{0,4},{4,0},{8,12},{12,8},{16,20},{20,16},{24,28},{28,24},{1,5},{5... | collective-permute-start | bytes 98312 | tf_op jit(solution)/shard_map/ppermute | solution.py:283
  13.9 6.2 %collective-permute-start.6 = (bf16[32,1024]{1,0:T(8,128)(2,1)S(1)}, bf16[32,1024]{1,0:T(8,128)(2,1)S(1)}, u32[]{:S(2)}, u32[]{:S(2)}) collective-permute-start(bf16[32,1024]{1,0:T(8,128)(2,1)S(1)} %pad_maximum_fusion.refs_0_), channel_id=1, source_target_pairs={{0,24},{4,28},{8,16},{12,20},{16,8},{20,12},{24,0},{28,4},{1,25},{... | collective-permute-start | bytes 196616 | tf_op jit(solution)/shard_map/ppermute | solution.py:283
  16.3 5.4 %collective-permute-start.5 = (bf16[32,1024]{1,0:T(8,128)(2,1)S(1)}, bf16[32,1024]{1,0:T(8,128)(2,1)S(1)}, u32[]{:S(2)}, u32[]{:S(2)}) collective-permute-start(bf16[32,1024]{1,0:T(8,128)(2,1)S(1)} %pad_maximum_fusion.refs_0_), channel_id=1, source_target_pairs={{0,16},{4,20},{8,24},{12,28},{16,0},{20,4},{24,8},{28,12},{1,17},{... | collective-permute-start | bytes 196616 | tf_op jit(solution)/shard_map/ppermute | solution.py:283
  16.9 4.9 %collective-permute-start.4 = (bf16[32,1024]{1,0:T(8,128)(2,1)S(1)}, bf16[32,1024]{1,0:T(8,128)(2,1)S(1)}, u32[]{:S(2)}, u32[]{:S(2)}) collective-permute-start(bf16[32,1024]{1,0:T(8,128)(2,1)S(1)} %pad_maximum_fusion.refs_0_), channel_id=1, source_target_pairs={{0,8},{4,12},{8,0},{12,4},{16,24},{20,28},{24,16},{28,20},{1,9},{5... | collective-permute-start | bytes 196616 | tf_op jit(solution)/shard_map/ppermute | solution.py:283
  17.4 6.3 %collective-permute-start.9 = (f32[2,3072]{1,0:T(2,128)S(1)}, f32[2,3072]{1,0:T(2,128)S(1)}, u32[]{:S(2)}, u32[]{:S(2)}) collective-permute-start(f32[2,3072]{1,0:T(2,128)S(1)} %get-tuple-element.52.refs_0_), channel_id=1, source_target_pairs={{0,3},{1,2},{2,1},{3,0},{4,7},{5,6},{6,5},{7,4},{8,11},{9,10},{10,... | collective-permute-start | bytes 73736 | tf_op jit(solution)/shard_map/ppermute | solution.py:283
  19.8 4.9 %collective-permute-start.8 = (f32[2,3072]{1,0:T(2,128)S(1)}, f32[2,3072]{1,0:T(2,128)S(1)}, u32[]{:S(2)}, u32[]{:S(2)}) collective-permute-start(f32[2,3072]{1,0:T(2,128)S(1)} %get-tuple-element.52.refs_0_), channel_id=1, source_target_pairs={{0,2},{1,3},{2,0},{3,1},{4,6},{5,7},{6,4},{7,5},{8,10},{9,11},{10,... | collective-permute-start | bytes 73736 | tf_op jit(solution)/shard_map/ppermute | solution.py:283
  20.1 4.5 %collective-permute-start.7 = (f32[2,3072]{1,0:T(2,128)S(1)}, f32[2,3072]{1,0:T(2,128)S(1)}, u32[]{:S(2)}, u32[]{:S(2)}) collective-permute-start(f32[2,3072]{1,0:T(2,128)S(1)} %get-tuple-element.52.refs_0_), channel_id=1, source_target_pairs={{0,1},{1,0},{2,3},{3,2},{4,5},{5,4},{6,7},{7,6},{8,9},{9,8},{10,11... | collective-permute-start | bytes 73736 | tf_op jit(solution)/shard_map/ppermute | solution.py:283
